TPU v7x, 32 devices: a whole 2x2x4 slice. The times are simulated.
32 devices in a mesh: shard: 2 (over y), ctx: 4 (over x, core), tp: 4 (over z).
Axes of the slice: x: 2, y: 2, z: 4, core: 2. Of those that a mesh axis runs over, the one named last changes fastest.
Arguments:
- layer_input: bfloat16 [12, 1024, 768], P('shard', 'ctx'), may hold values from -6 to 6
- segment_ids: int32 [12, 1024], P('shard'), may hold values from 0 to 15, never falling along the last dimension, each value on 1 to 512 neighbouring positions
- query_proj: bfloat16 [768, 768], P('shard', 'tp'), may hold values from -0.21875 to 0.21875
- query_bias: bfloat16 [768], P('tp'), may hold values from -4 to 4
- key_proj: bfloat16 [768, 768], P('shard', 'tp'), may hold values from -0.21875 to 0.21875
- value_proj: bfloat16 [768, 768], P('shard', 'tp'), may hold values from -0.21875 to 0.21875
- value_bias: bfloat16 [768], P('tp'), may hold values from -3 to 3
- out_proj: bfloat16 [768, 768], P('tp', 'shard'), may hold values from -1.5 to 1.5
- out_bias: bfloat16 [768], replicated, may hold values from -3 to 3
- attn_gain: bfloat16 [768], replicated, may hold values from 0.099609375 to 1.8984375
- attn_shift: bfloat16 [768], replicated, may hold values from -3 to 3
- up_proj: bfloat16 [768, 3072], P('shard', 'tp'), may hold values from -0.21875 to 0.21875
- up_bias: bfloat16 [3072], P('tp'), may hold values from -3 to 3
- down_proj: bfloat16 [3072, 768], P('tp', 'shard'), may hold values from -0.109375 to 0.109375
- down_bias: bfloat16 [768], replicated, may hold values from -3 to 3
- ffn_gain: bfloat16 [768], replicated, may hold values from 0.099609375 to 1.8984375
- ffn_shift: bfloat16 [768], replicated, may hold values from -3 to 3
- out_cotangent: bfloat16 [12, 1024, 768], P('shard', 'ctx'), may hold values from -6 to 6
Outputs:
- layer_output: bfloat16 [12, 1024, 768], P('shard', 'ctx')
- input_grad: float32 [12, 1024, 768], P('shard', 'ctx')
- query_proj_grad: float32 [768, 768], P('shard', 'tp')
- query_bias_grad: float32 [768], P('tp')
- key_proj_grad: float32 [768, 768], P('shard', 'tp')
- value_proj_grad: float32 [768, 768], P('shard', 'tp')
- value_bias_grad: float32 [768], P('tp')
- out_proj_grad: float32 [768, 768], P('tp', 'shard')
- out_bias_grad: float32 [768], replicated
- attn_gain_grad: float32 [768], replicated
- attn_shift_grad: float32 [768], replicated
- up_proj_grad: float32 [768, 3072], P('shard', 'tp')
- up_bias_grad: float32 [3072], P('tp')
- down_proj_grad: float32 [3072, 768], P('tp', 'shard')
- down_bias_grad: float32 [768], replicated
- ffn_gain_grad: float32 [768], replicated
- ffn_shift_grad: float32 [768], replicated
Inputs may be any that keep to these rules, and one draw needn't show every extreme that they name: `segment_ids`: within a sequence the ids never fall; each of the 16 documents has 1 to 512 tokens, and one has exactly 512.
All inputs are finite; a program needn't handle non-finite values.
Results may differ from a plain program's by a relative error of at most 0.04.
Values may be sent and summed in bfloat16 or wider, within the bound.
No kernel may reach another device: no remote copies, remote signals or barrier semaphores. Data moves between devices by JAX's collectives and lax.ppermute only.
A program may use at most 192 MiB of HBM per device.

v0:
```python
from functools import partial
import math

import jax
import jax.numpy as jnp
from jax import lax
from jax.experimental import pallas as pl
from jax.experimental.pallas import tpu as pltpu
from jax.sharding import PartitionSpec as P

HEAD_DIM = 64


eps_norm = 1e-12
far_below = -1e30


def contract_rows(left, right):
    return lax.dot_general(
        left, right, (((0,), (0,)), ((), ())), preferred_element_type=jnp.float32
    )


def contract_last(left, right):
    return lax.dot_general(
        left, right, (((1,), (1,)), ((), ())), preferred_element_type=jnp.float32
    )


def norm_forward(resid, norm_gain, norm_shift):
    center = resid - jnp.mean(resid, axis=-1, keepdims=True)
    inv_std = lax.rsqrt(jnp.mean(center * center, axis=-1, keepdims=True) + eps_norm)
    normed = center * inv_std
    return (normed * norm_gain + norm_shift, normed, inv_std)


def norm_backward(grad_out, normed, inv_std, norm_gain):
    grad_normed = grad_out * norm_gain
    grad_in = inv_std * (
        grad_normed
        - jnp.mean(grad_normed, axis=-1, keepdims=True)
        - normed * jnp.mean(grad_normed * normed, axis=-1, keepdims=True)
    )
    return (grad_in, jnp.sum(grad_out * normed, axis=0), jnp.sum(grad_out, axis=0))


def split_heads(matrix):
    return matrix.reshape(matrix.shape[0], matrix.shape[1] // HEAD_DIM, HEAD_DIM)


def scores_of(queries, keys_all, query_docs, key_docs):
    scores = jnp.einsum(
        "qhd,khd->hqk",
        split_heads(queries),
        split_heads(keys_all),
        preferred_element_type=jnp.float32,
    )
    same_doc = (query_docs[:, None] == key_docs[None, :])[None]
    return jnp.where(same_doc, scores, jnp.float32(far_below))


def attend_forward(item):
    queries, keys_all, values_all, query_docs, key_docs = item
    scores = scores_of(queries, keys_all, query_docs, key_docs)
    top_score = jnp.max(scores, axis=-1, keepdims=True)
    expo = jnp.exp(scores - top_score)
    total = jnp.sum(expo, axis=-1, keepdims=True)
    probs = (expo / total).astype(jnp.bfloat16)
    mixed = jnp.einsum(
        "hqk,khd->qhd", probs, split_heads(values_all), preferred_element_type=jnp.float32
    )
    return (
        mixed.reshape(queries.shape).astype(jnp.bfloat16),
        (top_score + jnp.log(total))[:, :, 0],
    )


def score_grads(queries, keys_all, values_all, query_docs, key_docs, grad_mixed, log_total):
    scores = scores_of(queries, keys_all, query_docs, key_docs)
    probs = jnp.exp(scores - log_total[:, :, None])
    grad_probs = jnp.einsum(
        "qhd,khd->hqk",
        split_heads(grad_mixed),
        split_heads(values_all),
        preferred_element_type=jnp.float32,
    )
    inner = jnp.sum(grad_probs * probs, axis=-1)
    grad_scores = (probs * (grad_probs - inner[:, :, None])).astype(jnp.bfloat16)
    return (probs, grad_scores, inner)


def attend_backward(item):
    queries, keys_all, values_all, query_docs, key_docs, grad_mixed, log_total = item
    probs, grad_scores, inner = score_grads(
        queries, keys_all, values_all, query_docs, key_docs, grad_mixed, log_total
    )
    grad_heads = split_heads(grad_mixed)
    grad_queries = jnp.einsum(
        "hqk,khd->qhd", grad_scores, split_heads(keys_all), preferred_element_type=jnp.float32
    )
    grad_keys = jnp.einsum(
        "hqk,qhd->khd", grad_scores, split_heads(queries), preferred_element_type=jnp.float32
    )
    grad_values = jnp.einsum(
        "hqk,qhd->khd", probs.astype(jnp.bfloat16), grad_heads, preferred_element_type=jnp.float32
    )
    return (
        grad_queries.reshape(queries.shape).astype(jnp.bfloat16),
        grad_keys.reshape(keys_all.shape),
        grad_values.reshape(values_all.shape),
    )


def general_shards(
    layer_input,
    segment_ids,
    query_proj,
    query_bias,
    key_proj,
    value_proj,
    value_bias,
    out_proj,
    out_bias,
    attn_gain,
    attn_shift,
    up_proj,
    up_bias,
    down_proj,
    down_bias,
    ffn_gain,
    ffn_shift,
    out_cotangent,
):
    seq_here, ctx_rows, width = layer_input.shape
    scale = 1.0 / math.sqrt(HEAD_DIM)
    full_query, full_key, full_value, full_out, full_up, full_down = (
        lax.all_gather(query_proj, "shard", axis=0, tiled=True),
        lax.all_gather(key_proj, "shard", axis=0, tiled=True),
        lax.all_gather(value_proj, "shard", axis=0, tiled=True),
        lax.all_gather(out_proj, "shard", axis=1, tiled=True),
        lax.all_gather(up_proj, "shard", axis=0, tiled=True),
        lax.all_gather(down_proj, "shard", axis=1, tiled=True),
    )
    local_width = full_query.shape[1]
    joined_proj = jnp.concatenate([full_query, full_key, full_value], axis=1)
    rows_in = layer_input.reshape(seq_here * ctx_rows, width)
    projected = jnp.dot(rows_in, joined_proj, preferred_element_type=jnp.float32)
    shaped = (seq_here, ctx_rows, local_width)
    queries = (
        ((projected[:, :local_width] + query_bias) * scale).astype(jnp.bfloat16).reshape(shaped)
    )
    keys_mine = projected[:, local_width : 2 * local_width].astype(jnp.bfloat16).reshape(shaped)
    values_mine = (
        (projected[:, 2 * local_width :] + value_bias).astype(jnp.bfloat16).reshape(shaped)
    )
    keys_all, values_all = (
        lax.all_gather(keys_mine, "ctx", axis=1, tiled=True),
        lax.all_gather(values_mine, "ctx", axis=1, tiled=True),
    )
    query_docs = lax.dynamic_slice_in_dim(
        segment_ids, lax.axis_index("ctx") * ctx_rows, ctx_rows, 1
    )
    mixed, log_total = lax.map(
        attend_forward, (queries, keys_all, values_all, query_docs, segment_ids)
    )
    mixed_rows = mixed.reshape(-1, local_width)
    attended = (
        lax.psum(
            jnp.dot(mixed_rows, full_out, preferred_element_type=jnp.float32).astype(jnp.bfloat16),
            "tp",
        ).astype(jnp.float32)
        + out_bias
    )
    hidden, normed_one, inv_one = norm_forward(
        rows_in.astype(jnp.float32) + attended, attn_gain, attn_shift
    )
    hidden_low = hidden.astype(jnp.bfloat16)
    pre_act = jnp.dot(hidden_low, full_up, preferred_element_type=jnp.float32) + up_bias
    acts_low = jax.nn.gelu(pre_act, approximate=False).astype(jnp.bfloat16)
    ffn_out = (
        lax.psum(
            jnp.dot(acts_low, full_down, preferred_element_type=jnp.float32).astype(jnp.bfloat16),
            "tp",
        ).astype(jnp.float32)
        + down_bias
    )
    output_rows, normed_two, inv_two = norm_forward(hidden + ffn_out, ffn_gain, ffn_shift)
    layer_output = output_rows.astype(jnp.bfloat16).reshape(layer_input.shape)
    grad_out = out_cotangent.reshape(-1, width).astype(jnp.float32)
    grad_two, ffn_gain_grad, ffn_shift_grad = norm_backward(grad_out, normed_two, inv_two, ffn_gain)
    grad_ffn = grad_two.astype(jnp.bfloat16)
    down_bias_grad = jnp.sum(grad_ffn, axis=0, dtype=jnp.float32)
    down_part = contract_rows(acts_low, grad_ffn)
    grad_acts = contract_last(grad_ffn, full_down)
    _, gelu_back = jax.vjp(partial(jax.nn.gelu, approximate=False), pre_act)
    grad_pre = gelu_back(grad_acts)[0].astype(jnp.bfloat16)
    up_bias_grad = jnp.sum(grad_pre, axis=0, dtype=jnp.float32)
    up_part = contract_rows(hidden_low, grad_pre)
    grad_hidden = grad_two + lax.psum(
        contract_last(grad_pre, full_up).astype(jnp.bfloat16), "tp"
    ).astype(jnp.float32)
    grad_one, attn_gain_grad, attn_shift_grad = norm_backward(
        grad_hidden, normed_one, inv_one, attn_gain
    )
    grad_attn = grad_one.astype(jnp.bfloat16)
    out_bias_grad = jnp.sum(grad_attn, axis=0, dtype=jnp.float32)
    out_part = contract_rows(mixed_rows, grad_attn)
    grad_mixed = contract_last(grad_attn, full_out).astype(jnp.bfloat16).reshape(shaped)
    keys_back, values_back = (
        lax.all_gather(keys_mine, "ctx", axis=1, tiled=True),
        lax.all_gather(values_mine, "ctx", axis=1, tiled=True),
    )
    grad_queries, grad_keys_all, grad_values_all = lax.map(
        attend_backward,
        (queries, keys_back, values_back, query_docs, segment_ids, grad_mixed, log_total),
    )
    grad_keys, grad_values = (
        lax.psum_scatter(
            grad_keys_all.astype(jnp.bfloat16), "ctx", scatter_dimension=1, tiled=True
        ).astype(jnp.float32),
        lax.psum_scatter(
            grad_values_all.astype(jnp.bfloat16), "ctx", scatter_dimension=1, tiled=True
        ).astype(jnp.float32),
    )
    grad_keys = grad_keys.astype(jnp.bfloat16).reshape(-1, local_width)
    grad_values = grad_values.astype(jnp.bfloat16).reshape(-1, local_width)
    grad_scaled = grad_queries.reshape(-1, local_width) * jnp.bfloat16(scale)
    grad_joined = jnp.concatenate([grad_scaled, grad_keys, grad_values], axis=1)
    joined_part = contract_rows(rows_in, grad_joined)
    query_part = joined_part[:, :local_width]
    key_part = joined_part[:, local_width : 2 * local_width]
    value_part = joined_part[:, 2 * local_width :]
    query_bias_grad = jnp.sum(grad_scaled, axis=0, dtype=jnp.float32)
    value_bias_grad = jnp.sum(grad_values, axis=0, dtype=jnp.float32)
    back_terms = contract_last(grad_joined, joined_proj)
    input_grad = (
        grad_one + lax.psum(back_terms.astype(jnp.bfloat16), "tp").astype(jnp.float32)
    ).reshape(layer_input.shape)
    sliced = (
        lax.psum_scatter(
            query_part.astype(jnp.bfloat16), "shard", scatter_dimension=0, tiled=True
        ).astype(jnp.float32),
        lax.psum_scatter(
            key_part.astype(jnp.bfloat16), "shard", scatter_dimension=0, tiled=True
        ).astype(jnp.float32),
        lax.psum_scatter(
            value_part.astype(jnp.bfloat16), "shard", scatter_dimension=0, tiled=True
        ).astype(jnp.float32),
        lax.psum_scatter(
            out_part.astype(jnp.bfloat16), "shard", scatter_dimension=1, tiled=True
        ).astype(jnp.float32),
        lax.psum_scatter(
            up_part.astype(jnp.bfloat16), "shard", scatter_dimension=0, tiled=True
        ).astype(jnp.float32),
        lax.psum_scatter(
            down_part.astype(jnp.bfloat16), "shard", scatter_dimension=1, tiled=True
        ).astype(jnp.float32),
    )
    reduced = (
        lax.psum(sliced[0].astype(jnp.bfloat16), "ctx").astype(jnp.float32),
        lax.psum(sliced[1].astype(jnp.bfloat16), "ctx").astype(jnp.float32),
        lax.psum(sliced[2].astype(jnp.bfloat16), "ctx").astype(jnp.float32),
        lax.psum(sliced[3].astype(jnp.bfloat16), "ctx").astype(jnp.float32),
        lax.psum(sliced[4].astype(jnp.bfloat16), "ctx").astype(jnp.float32),
        lax.psum(sliced[5].astype(jnp.bfloat16), "ctx").astype(jnp.float32),
    )
    small = lax.psum(
        (
            query_bias_grad,
            value_bias_grad,
            out_bias_grad,
            attn_gain_grad,
            attn_shift_grad,
            up_bias_grad,
            down_bias_grad,
            ffn_gain_grad,
            ffn_shift_grad,
        ),
        ("shard", "ctx"),
    )
    return (
        layer_output,
        input_grad,
        reduced[0],
        small[0],
        reduced[1],
        reduced[2],
        small[1],
        reduced[3],
        small[2],
        small[3],
        small[4],
        reduced[4],
        small[5],
        reduced[5],
        small[6],
        small[7],
        small[8],
    )


PAIR = 2 * HEAD_DIM
QBLOCK = 128


def dot32(left, right):
    return jnp.dot(left, right, preferred_element_type=jnp.float32)


def stack_heads(rows):
    lane = lax.broadcasted_iota(jnp.int32, rows.shape, 1)
    nought = jnp.zeros_like(rows)
    return jnp.concatenate(
        [jnp.where(lane < HEAD_DIM, rows, nought), jnp.where(lane >= HEAD_DIM, rows, nought)], axis=0
    )


def unstack_heads(tall):
    count = tall.shape[0] // 2
    lane = lax.broadcasted_iota(jnp.int32, (count, tall.shape[1]), 1)
    return jnp.where(lane < HEAD_DIM, tall[:count], tall[count:])


def masked_scores(queries, keys, same):
    scores = contract_last(queries, keys)
    return jnp.where(jnp.concatenate([same, same], axis=0), scores, jnp.float32(far_below))


def attend_kernel(span, q_ref, k_ref, v_ref, kd_ref, qd_ref, *refs):
    o_ref, l_ref = refs[-2:]
    here = pl.ds(pl.multiple_of(pl.program_id(1) * QBLOCK, QBLOCK), span)
    same = qd_ref[:, :1] == kd_ref[:, here]
    logs = []
    for pair in range(q_ref.shape[1] // PAIR):
        cols = slice(pair * PAIR, (pair + 1) * PAIR)
        scores = masked_scores(stack_heads(q_ref[:, cols]), k_ref[here, cols], same)
        top = jnp.max(scores, axis=1, keepdims=True)
        expo = jnp.exp(scores - top)
        total = jnp.sum(expo, axis=1, keepdims=True)
        mixed = dot32(expo.astype(jnp.bfloat16), v_ref[here, cols]) * (1.0 / total)
        o_ref[:, cols] = unstack_heads(mixed).astype(jnp.bfloat16)
        log = top + jnp.log(total)
        logs += [log[:QBLOCK], log[QBLOCK:]]
    l_ref[0] = jnp.concatenate(logs, axis=1)


def attend_back_kernel(span, q_ref, k_ref, v_ref, kd_ref, qd_ref, do_ref, l_ref, *refs):
    dq_ref, dk_ref, dv_ref, dk_acc, dv_acc = refs[-5:]
    step = pl.program_id(1)

    @pl.when(step == 0)
    def _():
        dk_acc[...] = jnp.zeros_like(dk_acc)
        dv_acc[...] = jnp.zeros_like(dv_acc)

    here = pl.ds(pl.multiple_of(step * QBLOCK, QBLOCK), span)
    same = qd_ref[:, :1] == kd_ref[:, here]
    logs = l_ref[0]
    for pair in range(q_ref.shape[1] // PAIR):
        cols = slice(pair * PAIR, (pair + 1) * PAIR)
        keys = k_ref[here, cols]
        queries, grads = stack_heads(q_ref[:, cols]), stack_heads(do_ref[:, cols])
        log = jnp.concatenate([logs[:, 2 * pair + i : 2 * pair + i + 1] for i in (0, 1)], axis=0)
        probs = jnp.exp(masked_scores(queries, keys, same) - log)
        grad_probs = contract_last(grads, v_ref[here, cols])
        inner = jnp.sum(grad_probs * probs, axis=1, keepdims=True)
        grad_scores = (probs * (grad_probs - inner)).astype(jnp.bfloat16)
        grad_queries = unstack_heads(dot32(grad_scores, keys))
        dq_ref[:, cols] = (grad_queries * (1.0 / math.sqrt(HEAD_DIM))).astype(jnp.bfloat16)
        dk_acc[here, cols] += contract_rows(grad_scores, queries)
        dv_acc[here, cols] += contract_rows(probs.astype(jnp.bfloat16), grads)

    @pl.when(step == pl.num_programs(1) - 1)
    def _():
        dk_ref[...] = dk_acc[...].astype(jnp.bfloat16)
        dv_ref[...] = dv_acc[...].astype(jnp.bfloat16)


def attention_specs(window, cols, at):
    rows = pl.BlockSpec((QBLOCK, cols), lambda h, i: (i, at + h))
    keys = pl.BlockSpec((window, cols), lambda h, i: (0, at + h))
    key_docs = pl.BlockSpec((1, window), lambda h, i: (0, 0))
    query_docs = pl.BlockSpec((QBLOCK, QBLOCK), lambda h, i: (i, 0))
    logs = pl.BlockSpec((1, QBLOCK, cols // HEAD_DIM), lambda h, i: (at + h, i, 0))
    return rows, keys, key_docs, query_docs, logs


def attend(queries, keys, values, key_docs, query_docs, reach, half, prior=()):
    count, width = queries.shape
    window, cols = keys.shape[0], width // 2
    span = QBLOCK + 2 * reach
    rows, key_spec, kd_spec, qd_spec, logs = attention_specs(window, cols, half)
    return pl.pallas_call(
        partial(attend_kernel, span),
        grid=(1, count // QBLOCK),
        in_specs=[rows, key_spec, key_spec, kd_spec, qd_spec]
        + [pl.BlockSpec(memory_space=pl.ANY)] * len(prior),
        out_specs=[rows, logs],
        out_shape=[
            jax.ShapeDtypeStruct((count, width), jnp.bfloat16),
            jax.ShapeDtypeStruct((2, count, cols // HEAD_DIM), jnp.float32),
        ],
        input_output_aliases={5 + i: i for i in range(len(prior))},
        compiler_params=pltpu.CompilerParams(vmem_limit_bytes=16 << 20),
        cost_estimate=pl.CostEstimate(
            flops=16 * count * span * cols, bytes_accessed=4 << 20, transcendentals=0
        ),
        name="attend",
    )(queries, keys, values, key_docs, query_docs, *prior)


def attend_back(queries, keys, values, key_docs, query_docs, reach, grads, logs_in):
    count, width = queries.shape
    window, cols = keys.shape[0], width // 2
    span = QBLOCK + 2 * reach
    rows, key_spec, kd_spec, qd_spec, logs = attention_specs(window, cols, 0)
    return pl.pallas_call(
        partial(attend_back_kernel, span),
        grid=(2, count // QBLOCK),
        in_specs=[rows, key_spec, key_spec, kd_spec, qd_spec, rows, logs],
        out_specs=[rows, key_spec, key_spec],
        out_shape=[
            jax.ShapeDtypeStruct((count, width), jnp.bfloat16),
            jax.ShapeDtypeStruct((window, width), jnp.bfloat16),
            jax.ShapeDtypeStruct((window, width), jnp.bfloat16),
        ],
        scratch_shapes=[pltpu.VMEM((window, cols), jnp.float32)] * 2,
        compiler_params=pltpu.CompilerParams(vmem_limit_bytes=24 << 20),
        cost_estimate=pl.CostEstimate(
            flops=40 * count * span * width, bytes_accessed=12 << 20, transcendentals=0
        ),
        name="attend_back",
    )(queries, keys, values, key_docs, query_docs, grads, logs_in)


def half_cols(position, half):
    return pl.ds(pl.multiple_of(position * half, half), half)


def add_or_set(first, ref, index, terms):
    @pl.when(first)
    def _():
        ref[index] = terms

    @pl.when(jnp.logical_not(first))
    def _():
        ref[index] += terms


def ffn_kernel(first_block, place_ref, hb_ref, w_ref, bias_ref, *refs):
    half = w_ref.shape[3]
    count = hb_ref.shape[0] // 2
    near, far = half_cols(place_ref[1], half), half_cols(1 - place_ref[1], half)
    hb_near = refs[-1]
    hb_near[:, :half] = hb_ref[:, near]
    hb_near[:, half:] = hb_ref[:, far]

    def chunk(block, rows, acts_ref, slope_ref):
        up = w_ref[block, :, :half].reshape(2 * half, half)
        pre_act = dot32(hb_near[rows], up) + bias_ref[block]
        cdf = 0.5 * (1.0 + lax.erf(pre_act * math.sqrt(0.5)))
        bell = jnp.exp(-0.5 * pre_act * pre_act) * (1.0 / math.sqrt(2 * math.pi))
        acts = (pre_act * cdf).astype(jnp.bfloat16)
        cols = pl.ds(pl.multiple_of(block * half, half), half)
        acts_ref[rows, cols] = acts
        slope_ref[rows, cols] = (cdf + pre_act * bell).astype(jnp.bfloat16)
        return dot32(acts, w_ref[block, 0, half:]), dot32(acts, w_ref[block, 1, half:])

    blocks = w_ref.shape[0]
    if first_block:
        base_ref, _, _, acts_ref, slope_ref, own_ref, other_ref = refs[:-1]
        for part, to in enumerate((own_ref, other_ref)):
            rows = slice(part * count, (part + 1) * count)
            terms = chunk(blocks - 1, rows, acts_ref, slope_ref)
            for y, cols in enumerate((near, far)):
                base = base_ref[rows, y * half : (y + 1) * half]
                to[:, cols] = (base + terms[y]).astype(to.dtype)
    else:
        acts_ref, slope_ref, total = refs[:-1]
        total[...] = jnp.zeros_like(total)

        @pl.loop(0, 2 * (blocks - 1))
        def _(i):
            rows = pl.ds(pl.multiple_of((i & 1) * count, count), count)
            one, two = chunk(i >> 1, rows, acts_ref, slope_ref)
            total[rows, :half] += one
            total[rows, half:] += two


def ffn_back_kernel(
    place_ref,
    dz_ref,
    hb_ref,
    acts_ref,
    slope_ref,
    w_ref,
    own_ref,
    other_ref,
    up_keep,
    up_give,
    down_keep,
    down_give,
    sums_ref,
    total,
    grad_pre,
    dz_near,
    rows_t,
    up_both,
    down_both,
    sums,
):
    step = pl.program_id(0)
    half = w_ref.shape[3]
    quarter = half // 2
    count = own_ref.shape[0]
    near, far = half_cols(place_ref[1], half), half_cols(1 - place_ref[1], half)
    first, second = slice(0, half), slice(half, 2 * half)

    @pl.when(step == 0)
    def _():
        total[...] = jnp.zeros_like(total)
        for to, cols in ((first, near), (second, far)):
            dz_near[:, to] = dz_ref[:, cols]
            rows_t[to] = hb_ref[:, cols].T

    for k, hid in enumerate((first, second)):
        for y, to in enumerate((first, second)):
            up_both[to, hid] = w_ref[k, y, :half]
            down_both[hid, to] = w_ref[k, y, half:]
    sums[...] = jnp.zeros_like(sums)

    @pl.loop(0, 2)
    def _(part):
        rows = pl.ds(pl.multiple_of(part * count, count), count)
        grad_acts = contract_last(dz_near[rows], down_both[...])
        low = (slope_ref[rows].astype(jnp.float32) * grad_acts).astype(jnp.bfloat16)
        grad_pre[rows] = low
        sums[...] += row_sum(low.astype(jnp.float32))
        total[rows] += contract_last(low, up_both[...])

    tps = [(place_ref[2] + 4 - jnp.where(step == 0, k, 3 - k)) & 3 for k in (0, 1)]
    for tp, hid in zip(tps, (first, second)):
        sums_ref[tp] = sums[:, hid]
    acts_t = acts_ref[...].T
    for side, cols in enumerate((first, second)):
        up_grad = dot32(rows_t[cols], grad_pre[...]).astype(jnp.bfloat16)
        down_grad = dot32(acts_t, dz_near[:, cols]).astype(jnp.bfloat16)
        down_to = down_give if side else down_keep
        for across in (0, 1):

            @pl.when(place_ref[3] == across)
            def _():
                for k in (0, 1):
                    tp = tps[k]
                    hid = slice(k * half, (k + 1) * half)
                    for x in (0, 1):
                        part = slice((x ^ across) * quarter, (x ^ across) * quarter + quarter)
                        down_rows = slice(k * half + part.start, k * half + part.stop)
                        (up_give if x else up_keep)[side, tp] = up_grad[part, hid]
                        down_to[x, tp] = down_grad[down_rows]

    @pl.when(step == pl.num_programs(0) - 1)
    def _():
        own_ref[:, near] = total[:count, first].astype(jnp.bfloat16)
        own_ref[:, far] = total[:count, second].astype(jnp.bfloat16)
        other_ref[:, near] = total[count:, first].astype(jnp.bfloat16)
        other_ref[:, far] = total[count:, second].astype(jnp.bfloat16)


def once(shape):
    return pl.BlockSpec(
        shape, lambda *_: (0,) * len(shape), pipeline_mode=pl.Buffered(buffer_count=1)
    )


def whole(shape):
    return pl.BlockSpec(shape, lambda *_: (0,) * len(shape))


def ffn(place, rows, weights, bias, prior=()):
    both, width = rows.shape
    tps, shards, _, half = weights.shape
    count = both // 2
    vmem = pl.BlockSpec(memory_space=pltpu.VMEM)
    low = jax.ShapeDtypeStruct((count, width), jnp.bfloat16)
    hidden = jax.ShapeDtypeStruct((both, tps * half), jnp.bfloat16)
    last = [low, low] if prior else [jax.ShapeDtypeStruct((both, width), jnp.float32)]
    steps = 1 if prior else tps - 1
    return pl.pallas_call(
        partial(ffn_kernel, bool(prior)),
        in_specs=[pl.BlockSpec(memory_space=pltpu.SMEM)] + [vmem] * (3 + len(prior)),
        out_specs=[vmem] * (2 + len(last)),
        out_shape=[hidden, hidden] + last,
        scratch_shapes=[pltpu.VMEM((both, width), jnp.bfloat16)],
        input_output_aliases={5: 0, 6: 1} if prior else {},
        compiler_params=pltpu.CompilerParams(vmem_limit_bytes=16 << 20),
        cost_estimate=pl.CostEstimate(
            flops=12 * both * width * steps * half, bytes_accessed=3 * steps << 20, transcendentals=0
        ),
        name="ffn",
    )(place, rows, weights, bias, *prior)


def ffn_back(place, grads, rows, acts, slope, weights):
    both, width = rows.shape
    tps, shards, _, half = weights.shape
    count = both // 2
    block = pl.BlockSpec((both, 2 * half), lambda i, _: (0, i))
    parts = (2, tps, half // 2, half)
    low = jax.ShapeDtypeStruct((count, width), jnp.bfloat16)
    return pl.pallas_call(
        ffn_back_kernel,
        grid_spec=pltpu.PrefetchScalarGridSpec(
            num_scalar_prefetch=1,
            grid=(tps // 2,),
            in_specs=[
                once((both, width)),
                once((both, width)),
                block,
                block,
                pl.BlockSpec((2, shards, 2 * half, half), lambda i, _: (i, 0, 0, 0)),
            ],
            out_specs=[
                whole((count, width)),
                whole((count, width)),
                *[whole(parts)] * 4,
                whole((tps, 1, half)),
            ],
            scratch_shapes=[
                pltpu.VMEM((both, width), jnp.float32),
                pltpu.VMEM((both, 2 * half), jnp.bfloat16),
                pltpu.VMEM((both, width), jnp.bfloat16),
                pltpu.VMEM((width, both), jnp.bfloat16),
                pltpu.VMEM((width, 2 * half), jnp.bfloat16),
                pltpu.VMEM((2 * half, width), jnp.bfloat16),
                pltpu.VMEM((1, 2 * half), jnp.float32),
            ],
        ),
        out_shape=[
            low,
            low,
            *[jax.ShapeDtypeStruct(parts, jnp.bfloat16)] * 4,
            jax.ShapeDtypeStruct((tps, 1, half), jnp.float32),
        ],
        compiler_params=pltpu.CompilerParams(vmem_limit_bytes=30 << 20),
        cost_estimate=pl.CostEstimate(
            flops=12 * both * width * tps * half, bytes_accessed=20 << 20, transcendentals=0
        ),
        name="ffn_back",
    )(place, grads, rows, acts, slope, weights)


def project_kernel(
    place_ref, w_mine, w_other, x_mine, x_other, bias_ref, q_ref, k_ref, v_ref, x_ref, wt
):
    core, shard, tp, across, start = (place_ref[i] for i in range(5))
    depth = w_mine.shape[3]
    width = x_ref.shape[1]
    part = width // 8
    length = 4 * x_mine.shape[2]
    reach = length // 2
    for c, source in enumerate((w_mine, w_other)):
        for y in (0, 1):
            cols = half_cols(shard + y - 2 * shard * y, depth)
            for k in range(4):
                row = ((tp + 4 - k) & 3) * 2 + core + c - 2 * core * c
                rows = pl.ds(pl.multiple_of(row * part, part), part)
                for m in range(3):
                    wt[m, rows, cols] = source[y, k, m * part : (m + 1) * part]
    for i in range(x_ref.shape[0] // QBLOCK):
        row = start - reach + i * QBLOCK
        inside = jnp.logical_and(row >= 0, row < 2 * length)
        at = jnp.where(inside, row, 0) // QBLOCK
        seq, block, piece = at // 8, (at // 2) & 3, at & 1
        here = jnp.where((block >> 1) == across, 0, 1)
        rows = pl.ds(pl.multiple_of(piece * QBLOCK, QBLOCK), QBLOCK)
        mine, other = x_mine[here, seq, rows], x_other[here, seq, rows]
        found = jnp.where((block & 1) == core, mine, other)
        x_ref[i * QBLOCK : (i + 1) * QBLOCK] = jnp.where(inside, found, jnp.zeros_like(found))
    count = q_ref.shape[0]
    scaled = contract_last(x_ref[reach : reach + count], wt[0]) + bias_ref[0:1]
    q_ref[...] = (scaled * (1.0 / math.sqrt(HEAD_DIM))).astype(jnp.bfloat16)
    chunk = x_ref.shape[0] // 4

    @pl.loop(0, 4)
    def _(step):
        rows = pl.ds(pl.multiple_of(step * chunk, 32), chunk)
        k_ref[rows] = contract_last(x_ref[rows], wt[1]).astype(jnp.bfloat16)
        v_ref[rows] = (contract_last(x_ref[rows], wt[2]) + bias_ref[1:2]).astype(jnp.bfloat16)


def project(place, w_mine, w_other, x_mine, x_other, biases, count, window):
    width = x_mine.shape[-1]
    return pl.pallas_call(
        project_kernel,
        in_specs=[pl.BlockSpec(memory_space=pltpu.SMEM)]
        + [pl.BlockSpec(memory_space=pltpu.VMEM)] * 5,
        out_specs=[pl.BlockSpec(memory_space=pltpu.VMEM)] * 5,
        out_shape=[
            jax.ShapeDtypeStruct((count, width), jnp.bfloat16),
            jax.ShapeDtypeStruct((window, width), jnp.bfloat16),
            jax.ShapeDtypeStruct((window, width), jnp.bfloat16),
            jax.ShapeDtypeStruct((window, width), jnp.bfloat16),
            jax.ShapeDtypeStruct((3, width, width), jnp.bfloat16),
        ],
        compiler_params=pltpu.CompilerParams(vmem_limit_bytes=24 << 20),
        cost_estimate=pl.CostEstimate(
            flops=4 * window * width * width, bytes_accessed=16 << 20, transcendentals=0
        ),
        name="project",
    )(place, w_mine, w_other, x_mine, x_other, biases)


def norm_pieces(resid):
    center = resid - jnp.mean(resid, axis=-1, keepdims=True)
    inv_std = lax.rsqrt(jnp.mean(center * center, axis=-1, keepdims=True) + eps_norm)
    return center * inv_std, inv_std


def norm_pull(grad_out, normed, inv_std, gain):
    grad_normed = grad_out * gain
    return inv_std * (
        grad_normed
        - jnp.mean(grad_normed, axis=-1, keepdims=True)
        - normed * jnp.mean(grad_normed * normed, axis=-1, keepdims=True)
    )


def row_sum(rows):
    return jnp.sum(rows, axis=0, keepdims=True)


def attend_out_kernel(
    place_ref, o_ref, x_ref, w_mine, w_other, vec_ref, hb_ref, n_ref, i_ref, wo_ref
):
    core, shard, tp = (place_ref[i] for i in range(3))
    part, depth = w_mine.shape[2:]

    @pl.when(pl.program_id(0) == 0)
    def _():
        for c, source in enumerate((w_mine, w_other)):
            for y in (0, 1):
                cols = half_cols(shard + y - 2 * shard * y, depth)
                for k in range(4):
                    row = ((tp + 4 - k) & 3) * 2 + core + c - 2 * core * c
                    rows = pl.ds(pl.multiple_of(row * part, part), part)
                    wo_ref[rows, cols] = source[k, y]

    resid = x_ref[...].astype(jnp.float32) + dot32(o_ref[...], wo_ref[...]) + vec_ref[0:1]
    normed, inv_std = norm_pieces(resid)
    hb_ref[...] = (normed * vec_ref[1:2] + vec_ref[2:3]).astype(jnp.bfloat16)
    n_ref[...] = normed.astype(jnp.bfloat16)
    i_ref[...] = jnp.broadcast_to(inv_std, i_ref.shape)


def row_blocks(width):
    return pl.BlockSpec((QBLOCK, width), lambda i, *_: (i, 0))


def on_rows(kernel, count, in_specs, out_specs, out_shape, name, scalars=0):
    return pl.pallas_call(
        kernel,
        grid_spec=pltpu.PrefetchScalarGridSpec(
            num_scalar_prefetch=scalars,
            grid=(count // QBLOCK,),
            in_specs=in_specs,
            out_specs=out_specs,
        ),
        out_shape=out_shape,
        compiler_params=pltpu.CompilerParams(vmem_limit_bytes=12 << 20),
        cost_estimate=pl.CostEstimate(flops=1 << 28, bytes_accessed=6 << 20, transcendentals=0),
        name=name,
    )


def attend_out(place, mixed, window_rows, reach, w_mine, w_other, vectors):
    count, width = mixed.shape
    rows = row_blocks(width)
    low = jax.ShapeDtypeStruct((count, width), jnp.bfloat16)
    return on_rows(
        attend_out_kernel,
        count,
        [
            rows,
            pl.BlockSpec((QBLOCK, width), lambda i, *_: (i + reach // QBLOCK, 0)),
            whole(w_mine.shape),
            whole(w_other.shape),
            whole(vectors.shape),
        ],
        [rows, rows, row_blocks(QBLOCK), whole((width, width))],
        [
            low,
            low,
            jax.ShapeDtypeStruct((count, QBLOCK), jnp.float32),
            jax.ShapeDtypeStruct((width, width), jnp.bfloat16),
        ],
        "attend_out",
        1,
    )(place, mixed, window_rows, w_mine, w_other, vectors)


def norm_sums(sums_ref, rows):
    sums = jnp.concatenate([row_sum(row) for row in rows], axis=0)
    add_or_set(pl.program_id(0) == 0, sums_ref, slice(None), sums)


def ffn_norm_kernel(h_ref, own_ref, got_ref, g_ref, vec_ref, y_ref, dz_ref, sums_ref):
    resid = h_ref[...].astype(jnp.float32) + own_ref[...].astype(jnp.float32)
    resid += got_ref[...].astype(jnp.float32) + vec_ref[0:1]
    normed, inv_std = norm_pieces(resid)
    y_ref[...] = (normed * vec_ref[1:2] + vec_ref[2:3]).astype(jnp.bfloat16)
    grad_out = g_ref[...].astype(jnp.float32)
    low = norm_pull(grad_out, normed, inv_std, vec_ref[1:2]).astype(jnp.bfloat16)
    dz_ref[...] = low
    norm_sums(sums_ref, (low.astype(jnp.float32), grad_out * normed, grad_out))


def ffn_norm(hidden, own, got, cots, vectors):
    count, width = hidden.shape
    rows = row_blocks(width)
    low = jax.ShapeDtypeStruct((count, width), jnp.bfloat16)
    return on_rows(
        ffn_norm_kernel,
        count,
        [rows, rows, rows, rows, whole(vectors.shape)],
        [rows, rows, whole((3, width))],
        [low, low, jax.ShapeDtypeStruct((3, width), jnp.float32)],
        "ffn_norm",
    )(hidden, own, got, cots, vectors)


def attend_norm_kernel(
    dz_ref, own_ref, got_ref, n_ref, i_ref, vec_ref, wo_ref, out_ref, da_ref, do_ref, sums_ref
):
    grad_out = dz_ref[...].astype(jnp.float32) + own_ref[...].astype(jnp.float32)
    grad_out += got_ref[...].astype(jnp.float32)
    normed = n_ref[...].astype(jnp.float32)
    grad = norm_pull(grad_out, normed, i_ref[:, :1], vec_ref[1:2])
    low = grad.astype(jnp.bfloat16)
    out_ref[...] = grad
    da_ref[...] = low
    do_ref[...] = contract_last(low, wo_ref[...]).astype(jnp.bfloat16)
    norm_sums(sums_ref, (low.astype(jnp.float32), grad_out * normed, grad_out))


def attend_norm(grads, own, got, normed, inv_std, vectors, weights):
    count, width = grads.shape
    rows = row_blocks(width)
    low = jax.ShapeDtypeStruct((count, width), jnp.bfloat16)
    return on_rows(
        attend_norm_kernel,
        count,
        [rows, rows, rows, rows, row_blocks(QBLOCK), whole(vectors.shape), whole(weights.shape)],
        [rows, rows, rows, whole((3, width))],
        [
            jax.ShapeDtypeStruct((count, width), jnp.float32),
            low,
            low,
            jax.ShapeDtypeStruct((3, width), jnp.float32),
        ],
        "attend_norm",
    )(grads, own, got, normed, inv_std, vectors, weights)


def attn_grads_kernel(
    place_ref, dq_ref, dk_ref, dv_ref, o_ref, da_ref, w_ref, attn_ref, ffn_ref, up_ref, *parts
):
    core, shard, across = place_ref[0], place_ref[1], place_ref[3]
    grad_ref = parts[2]
    depth = w_ref.shape[1] // 2
    part = depth // 4
    count = dq_ref.shape[0]
    reach = (w_ref.shape[0] - count) // 2
    sides = (
        (dq_ref, w_ref.at[reach : reach + count]),
        (dk_ref, w_ref),
        (dv_ref, w_ref),
        (o_ref, da_ref),
    )
    for m, (left, right) in enumerate(sides):
        grad_ref[...] = contract_rows(left[...], right[...]).astype(jnp.bfloat16)
        group = across if m < 2 else 1 - across
        rows = slice((m % 2) * part, (m % 2 + 1) * part)
        for z in (0, 1):
            for c in (0, 1):
                at = pl.ds(pl.multiple_of((2 * z + c + core - 2 * c * core) * part, part), part)
                parts[c][shard, group, z, rows] = grad_ref[at, :depth]
                parts[c][1 - shard, group, z, rows] = grad_ref[at, depth:]
    query_sum = row_sum(dq_ref[...].astype(jnp.float32))
    value_sum = row_sum(dv_ref[...].astype(jnp.float32))
    shared = []
    for source in (attn_ref, ffn_ref):
        for r in range(3):
            shared += [source[r : r + 1, :depth], source[r : r + 1, depth:]]
    half = depth // 2
    for z in (0, 1):
        own = slice(z * half, (z + 1) * half)
        heads = jnp.concatenate([query_sum[:, own], value_sum[:, own]], axis=1)
        none = jnp.zeros_like(heads)
        rows = [heads] + shared
        for c in (0, 1):
            last = [none if c else up_ref[z], none, none]
            for x, group in ((across, rows[:8]), (1 - across, rows[8:] + last)):
                block = jnp.concatenate(group, axis=0).astype(jnp.bfloat16)
                for y in (0, 1):
                    parts[c][y, x, z, 2 * part :] = block


def attn_grads(
    place, grad_queries, grad_keys, grad_values, mixed, grad_attn, near, attn_sums, ffn_sums, up_sums
):
    count, width = mixed.shape
    window = near.shape[0]
    depth = width // 2
    high = depth // 2 + 8
    cols = pl.BlockSpec((count, depth), lambda i, _: (0, i))
    near_cols = pl.BlockSpec((window, depth), lambda i, _: (0, i))
    return pl.pallas_call(
        attn_grads_kernel,
        grid_spec=pltpu.PrefetchScalarGridSpec(
            num_scalar_prefetch=1,
            grid=(2,),
            in_specs=[
                cols,
                near_cols,
                near_cols,
                cols,
                whole((count, width)),
                whole((window, width)),
                whole((3, width)),
                whole((3, width)),
                pl.BlockSpec((2, 1, depth), lambda i, _: (i, 0, 0)),
            ],
            out_specs=[pl.BlockSpec((2, 2, 2, high, depth), lambda i, _: (0, 0, i, 0, 0))] * 2,
            scratch_shapes=[pltpu.VMEM((depth, width), jnp.bfloat16)],
        ),
        out_shape=[jax.ShapeDtypeStruct((2, 2, 4, high, depth), jnp.bfloat16)] * 2,
        compiler_params=pltpu.CompilerParams(vmem_limit_bytes=24 << 20),
        cost_estimate=pl.CostEstimate(
            flops=4 * (window + count) * width * width, bytes_accessed=16 << 20, transcendentals=0
        ),
        name="attn_grads",
    )(
        place,
        grad_queries,
        grad_keys,
        grad_values,
        mixed,
        grad_attn,
        near,
        attn_sums,
        ffn_sums,
        up_sums,
    )


def span_grads_kernel(
    place_ref,
    dq_ref,
    dk_ref,
    dv_ref,
    w_ref,
    base_ref,
    own_ref,
    first_ref,
    second_ref,
    give_ref,
    near,
):
    core = place_ref[0]
    count, reach = own_ref.shape[0], give_ref.shape[0]
    far = count + reach
    size = near.shape[0] // 4

    @pl.loop(0, 4)
    def _(step):
        rows = pl.ds(pl.multiple_of(step * size, 32), size)
        near[rows] = dot32(dk_ref[rows], w_ref[1]) + dot32(dv_ref[rows], w_ref[2])

    def rows_at(start, size):
        return near[pl.ds(pl.multiple_of(start, QBLOCK), size)].astype(jnp.bfloat16)

    give_ref[...] = rows_at((1 - core) * far, reach)
    first_ref[...] = rows_at(jnp.where(core == 0, reach - count, far), count)
    second_ref[...] = rows_at(jnp.where(core == 0, 0, far + count), reach - count)
    own_ref[...] = base_ref[...] + dot32(dq_ref[...], w_ref[0]) + near[reach:far]


def span_grads(place, grad_queries, grad_keys, grad_values, weights, base):
    count, width = base.shape
    reach = (grad_keys.shape[0] - count) // 2
    vmem = pl.BlockSpec(memory_space=pltpu.VMEM)
    return pl.pallas_call(
        span_grads_kernel,
        in_specs=[pl.BlockSpec(memory_space=pltpu.SMEM)] + [vmem] * 5,
        out_specs=[vmem] * 4,
        out_shape=[
            jax.ShapeDtypeStruct((count, width), jnp.float32),
            jax.ShapeDtypeStruct((count, width), jnp.bfloat16),
            jax.ShapeDtypeStruct((reach - count, width), jnp.bfloat16),
            jax.ShapeDtypeStruct((reach, width), jnp.bfloat16),
        ],
        scratch_shapes=[pltpu.VMEM(grad_keys.shape, jnp.float32)],
        compiler_params=pltpu.CompilerParams(vmem_limit_bytes=16 << 20),
        cost_estimate=pl.CostEstimate(
            flops=4 * (count + 2 * reach) * width * width,
            bytes_accessed=12 << 20,
            transcendentals=0,
        ),
        name="span_grads",
    )(place, grad_queries, grad_keys, grad_values, weights, base)


def assemble_kernel(place_ref, one, two, three, four, halves, out_ref):
    core, tp, across = place_ref[0], place_ref[2], place_ref[3]
    block = out_ref.shape[1]
    part = block // 2
    mine = pl.ds(pl.multiple_of(core * part, part), part)
    other = pl.ds(pl.multiple_of((1 - core) * part, part), part)
    for k, source in enumerate((one, two, three, four)):
        z = (tp + 4 - k) & 3
        group, side = 3 * (z >> 1), z & 1
        out_ref[group + jnp.where(side == 1, 1, 2 * across)] = source[:block].astype(out_ref.dtype)
        foreign = group + 2 - 2 * across

        @pl.when(((side + across + core) & 1) == 1)
        def _():
            out_ref[foreign, mine] = source[block:].astype(out_ref.dtype)
            out_ref[foreign, other] = halves[k].astype(out_ref.dtype)


def assemble_late_kernel(place_ref, one, two, three, four, middle, foreign, out_ref):
    core, tp, across = place_ref[0], place_ref[2], place_ref[3]
    block = out_ref.shape[1]
    part = block // 2
    for k, source in enumerate((one, two, three, four)):
        z = (tp + 4 - k) & 3
        group, side = 3 * (z >> 1), z & 1
        at = group + jnp.where(side == 1, 1, 2 * across)
        odd = (across + side) & 1

        @pl.when(jnp.logical_and(odd == 0, core == 0))
        def _():
            out_ref[at] = source[:block]

        @pl.when(jnp.logical_and(odd == 0, core == 1))
        def _():
            out_ref[at, :part] = middle[k]
            out_ref[at, part:] = source[:part]

        @pl.when(jnp.logical_and(odd == 1, core == 0))
        def _():
            out_ref[at, :part] = source[block:]
            out_ref[at, part:] = middle[k]

        @pl.when(jnp.logical_and(odd == 1, core == 1))
        def _():
            out_ref[at] = source[part:]

        @pl.when(((side + across + core) & 1) == 1)
        def _():
            out_ref[group + 2 - 2 * across] = foreign[k // 2]


def assemble(kernel, place, pieces, others, seqs, dtype):
    rows, width = pieces[0].shape
    vmem = pl.BlockSpec(memory_space=pltpu.VMEM)
    return pl.pallas_call(
        kernel,
        in_specs=[pl.BlockSpec(memory_space=pltpu.SMEM)] + [vmem] * (4 + len(others)),
        out_specs=vmem,
        out_shape=jax.ShapeDtypeStruct((seqs, rows * 2 // 3, width), dtype),
        compiler_params=pltpu.CompilerParams(vmem_limit_bytes=10 << 20),
        cost_estimate=pl.CostEstimate(flops=1 << 20, bytes_accessed=8 << 20, transcendentals=0),
        name="assemble",
    )(place, *pieces, *others)


def finish_ffn_kernel(place_ref, mine, across_got, core_got, both_got, up_ref, down_ref):
    core, across = place_ref[0], place_ref[3]
    depth = mine.shape[1]
    part = depth // 2
    for c, x, source in (
        (core, across, mine),
        (core, 1 - across, across_got),
        (1 - core, across, core_got),
        (1 - core, 1 - across, both_got),
    ):
        rows = pl.ds(pl.multiple_of(x * part, part), part)
        up_ref[rows, half_cols(c, depth)] = source[:part].astype(jnp.float32)
        rows = pl.ds(pl.multiple_of(c * depth + x * part, part), part)
        down_ref[rows] = source[part:].astype(jnp.float32)


def finish_attn_kernel(
    place_ref, mine, across_got, core_got, both_got, q_ref, k_ref, v_ref, o_ref, sums_ref
):
    core, across = place_ref[0], place_ref[3]
    part = q_ref.shape[0] // 2
    for c, x, source in (
        (core, across, mine),
        (core, 1 - across, across_got),
        (1 - core, across, core_got),
        (1 - core, 1 - across, both_got),
    ):
        rows = pl.ds(pl.multiple_of(c * part, part), part)
        one = source[:part].astype(jnp.float32)
        two = source[part : 2 * part].astype(jnp.float32)
        sums_ref[c, x] = source[2 * part :].astype(jnp.float32)

        @pl.when(x == 0)
        def _():
            q_ref[rows], k_ref[rows] = one, two

        @pl.when(x == 1)
        def _():
            v_ref[rows], o_ref[rows] = one, two


def finish(kernel, place, pieces, shapes, name):
    vmem = pl.BlockSpec(memory_space=pltpu.VMEM)
    return pl.pallas_call(
        kernel,
        in_specs=[pl.BlockSpec(memory_space=pltpu.SMEM)] + [vmem] * 4,
        out_specs=[vmem] * len(shapes),
        out_shape=[jax.ShapeDtypeStruct(shape, jnp.float32) for shape in shapes],
        compiler_params=pltpu.CompilerParams(vmem_limit_bytes=8 << 20),
        cost_estimate=pl.CostEstimate(flops=1 << 20, bytes_accessed=4 << 20, transcendentals=0),
        name=name,
    )(place, *pieces)


def ctx_swap(array, bit):
    return lax.ppermute(array, "ctx", [(i, i ^ bit) for i in range(4)])


def core_swap(array):
    return ctx_swap(array, 1)


def tie(*arrays):
    return lax.optimization_barrier(arrays)


def across_swap(array):
    return ctx_swap(array, 2)


def in_order(flag, mine, other):
    return jnp.where(flag == 0, mine, other), jnp.where(flag == 0, other, mine)


def at(across, core, tp):
    return (2 * across + core) * 4 + tp


def across_pairs():
    pairs = []
    for tp in range(4):
        for across in (0, 1):
            core = across ^ (tp & 1)
            pairs.append((at(1 - across, core, tp), at(across, core, tp)))
    return pairs


def tp_shifts(array, cuts=(slice(None), slice(None), slice(None))):
    return [
        lax.ppermute(array[cut], "tp", [(i, (i + shift) % 4) for i in range(4)])
        for shift, cut in zip((1, 2, 3), cuts)
        if cut is not None
    ]


def by_tp(array, shifted):
    one, two, three = shifted
    line = jnp.stack([three, two, one, array, three, two, one])
    return lax.dynamic_slice_in_dim(line, 3 - lax.axis_index("tp"), 4, 0)


def shard_swap(array):
    return lax.ppermute(array, "shard", [(0, 1), (1, 0)])


def low_sum(left, right):
    return (left.astype(jnp.float32) + right.astype(jnp.float32)).astype(jnp.bfloat16)


def scatter_tp_start(parts):
    tp = lax.axis_index("tp")
    moved = [lax.dynamic_index_in_dim(parts, tp, 0, keepdims=False)]
    for shift in (1, 2, 3):
        sent = lax.dynamic_index_in_dim(parts, (tp + shift) & 3, 0, keepdims=False)
        moved.append(lax.ppermute(sent, "tp", [(i, (i + shift) % 4) for i in range(4)]))
    return moved


def scatter_tp_end(moved):
    return sum(part.astype(jnp.float32) for part in moved).astype(jnp.bfloat16)


def chain_pairs(turn):
    pairs = []
    for group in (0, 2):
        path = [(0, group), (0, group + 1), (1, group + 1), (1, group)]
        for (across, tp), (next_across, next_tp) in zip(path[:-1], path[1:]):
            pairs.append((at(across, 1, tp), at(next_across, 1 ^ turn, next_tp)))
            pairs.append((at(next_across, 0, next_tp), at(across, turn, tp)))
    return pairs


def block_pairs(core):
    pairs = []
    for tp in range(4):
        for across in (0, 1):
            source = 1 ^ across ^ (tp & 1)
            pairs.append((at(across, source, tp), at(1 - across, core, tp)))
    return pairs


def span_shards(
    layer_input,
    segment_ids,
    query_proj,
    query_bias,
    key_proj,
    value_proj,
    value_bias,
    out_proj,
    out_bias,
    attn_gain,
    attn_shift,
    up_proj,
    up_bias,
    down_proj,
    down_bias,
    ffn_gain,
    ffn_shift,
    out_cotangent,
):
    seqs, block, width = layer_input.shape
    length = segment_ids.shape[1]
    reach = length // 2
    count = seqs * block // 4
    window = count + 2 * reach
    bf16, f32 = jnp.bfloat16, jnp.float32
    ctx, tp = lax.axis_index("ctx"), lax.axis_index("tp")
    shard = lax.axis_index("shard")
    core, across, side = ctx & 1, ctx >> 1, tp & 1
    place = 2 * across + (side ^ across)
    odd = across ^ side

    heads = query_proj.shape[1]
    half = heads // 2
    depth = query_proj.shape[0]
    cut = up_proj.shape[1] // 2
    own_in = lax.dynamic_slice_in_dim(
        jnp.stack([query_proj.T, key_proj.T, value_proj.T]), core * half, half, 1
    ).reshape(3 * half, depth)
    own_biases = jnp.stack(
        [
            jnp.concatenate([query_bias, value_bias]),
            lax.dynamic_slice_in_dim(up_bias, core * cut, cut, 0),
        ]
    )
    own_in = jnp.concatenate([own_in, own_biases, jnp.zeros((14, depth), bf16)], axis=0)
    out_half = out_proj.shape[0] // 2
    own_rest = jnp.concatenate(
        [
            lax.dynamic_slice_in_dim(up_proj, core * cut, cut, 1),
            lax.dynamic_slice_in_dim(down_proj, core * cut, cut, 0),
            lax.dynamic_slice_in_dim(out_proj, core * out_half, out_half, 0),
        ],
        axis=0,
    )
    first_seq = 3 * (tp >> 1)
    mine = lax.dynamic_slice_in_dim(layer_input, first_seq + across, 2, 0)
    theirs = across_swap(lax.dynamic_slice_in_dim(layer_input, first_seq + 1 - across, 2, 0))
    in_shifted = tp_shifts(own_in)
    far_rest = shard_swap(own_rest)
    *in_shifted, theirs, far_rest = tie(*in_shifted, theirs, far_rest)
    in_near = jnp.stack([own_in] + in_shifted)
    (rest_one,) = tp_shifts(tie(own_rest, in_near)[0], (slice(None), None, None))
    own_pair = jnp.stack([own_rest[: 2 * cut], far_rest[: 2 * cut]])
    near_cot = lax.dynamic_index_in_dim(
        out_cotangent, first_seq + odd + across, 0, keepdims=False
    )
    far_cot = lax.ppermute(
        lax.dynamic_index_in_dim(
            tie(out_cotangent, theirs)[0], first_seq + 2 - 2 * across, 0, keepdims=False
        ),
        ("ctx", "tp"),
        across_pairs(),
    )
    in_far, rest_one, own_pair, far_cot = tie(shard_swap(in_near), rest_one, own_pair, far_cot)
    in_mine = jnp.stack([in_near, in_far])
    (rest_three,) = tp_shifts(tie(own_rest, in_near)[0], (None, None, slice(None)))
    in_other, rest_three = tie(core_swap(in_mine), rest_three)
    own_late = tie(own_rest, rest_three)[0]
    (some_two,) = tp_shifts(own_late, (None, slice(cut, None), None))
    (up_two,) = tp_shifts(own_late, (None, slice(cut), None))
    far_three = shard_swap(rest_three)
    bias_rows = in_mine[0, :, 3 * half]
    in_biases = by_tp(bias_rows[0], [bias_rows[1], bias_rows[2], bias_rows[3]]).astype(f32)
    in_biases = jnp.stack([in_biases[:, :heads].reshape(-1), in_biases[:, heads:].reshape(-1)])
    up_bias_here = in_mine[0, :, 3 * half + 1].reshape(4, 1, cut).astype(f32)

    pair = jnp.stack([mine, theirs])
    pair_other = core_swap(pair)
    start = 2 * count * place + count * core - length * across
    ids = lax.dynamic_slice_in_dim(segment_ids, first_seq + across, 2, 0)
    ids = (ids + jnp.array([[0], [1 << 16]], jnp.int32)).reshape(-1)
    no_doc = jnp.full((reach,), -1, jnp.int32)
    window_docs = lax.dynamic_slice_in_dim(
        jnp.concatenate([no_doc, ids, no_doc]), start, window, 0
    )
    key_docs = window_docs[None]
    query_docs = jnp.broadcast_to(window_docs[reach : reach + count, None], (count, QBLOCK))

    place = jnp.stack([core, shard, tp, across, start])
    far_one = shard_swap(rest_one)
    queries, keys, values, in_window, weights_t = project(
        place, in_mine, in_other, pair, pair_other, in_biases, count, window
    )
    attention = queries, keys, values, key_docs, query_docs, reach
    mixed, logs = attend(*attention, 0)
    mixed, far_one, far_three, some_two = tie(mixed, far_one, far_three, some_two)
    far_some_two = shard_swap(some_two)
    mixed, logs = attend(*attention, 1, (mixed, logs))
    mixed, far_some_two, up_two = tie(mixed, far_some_two, up_two)
    far_up_two = shard_swap(up_two)
    out_mine = jnp.stack(
        [
            jnp.stack([one[-out_half:], two[-out_half:]])
            for one, two in (
                (own_rest, far_rest),
                (rest_one, far_one),
                (some_two, far_some_two),
                (rest_three, far_three),
            )
        ]
    )
    attn_vectors = jnp.stack([out_bias, attn_gain, attn_shift]).astype(f32)
    hidden_low, normed_one, inv_one, full_out = attend_out(
        place, mixed, in_window, reach, out_mine, core_swap(out_mine), attn_vectors
    )
    hidden_other = core_swap(hidden_low)
    hidden_both = jnp.concatenate([hidden_low, hidden_other], axis=0)
    ffn_weights = jnp.stack(
        [
            own_pair,
            jnp.stack([rest_one[: 2 * cut], far_one[: 2 * cut]]),
            jnp.stack([rest_three[: 2 * cut], far_three[: 2 * cut]]),
            own_pair,
        ]
    )
    ffn_bias = jnp.stack([up_bias_here[k] for k in (0, 1, 3, 2)])
    acts, slope, ffn_sum = ffn(place, hidden_both, ffn_weights, ffn_bias)
    ffn_sum, far_up_two = tie(ffn_sum, far_up_two)
    rest = ffn_weights.at[3].set(
        jnp.stack(
            [
                jnp.concatenate([up_two, some_two[:cut]], axis=0),
                jnp.concatenate([far_up_two, far_some_two[:cut]], axis=0),
            ]
        )
    )
    acts, slope, ffn_own, ffn_other = ffn(
        place, hidden_both, rest, ffn_bias, (ffn_sum, acts, slope)
    )

    half_block = block // 2

    def deliver_start(rows):
        far_rows = jnp.where(odd == 0, rows[-block:], rows[:block])
        return (
            core_swap(jnp.where(odd == 0, rows[block:], rows[:half_block])),
            lax.ppermute(far_rows[:half_block], ("ctx", "tp"), block_pairs(0)),
            lax.ppermute(far_rows[half_block:], ("ctx", "tp"), block_pairs(1)),
        )

    def deliver_pack(rows, middle, low, high):
        where_kept = [
            rows[:block],
            jnp.concatenate([middle, rows[:half_block]], axis=0),
            jnp.concatenate([rows[block:], middle], axis=0),
            rows[half_block:],
        ]
        kept = jnp.where(
            odd == 0,
            jnp.where(core == 0, where_kept[0], where_kept[1]),
            jnp.where(core == 0, where_kept[2], where_kept[3]),
        )
        return jnp.concatenate([kept, low + high], axis=0)

    cot_pair = tie(jnp.stack([near_cot, far_cot]), queries)[0]
    cot_swapped = core_swap(cot_pair)
    low_cot, high_cot = in_order(core, near_cot, cot_swapped[0])
    far_cot = jnp.where(core == odd, far_cot, cot_swapped[1])
    chip_cot = jnp.where(
        odd == 0,
        jnp.concatenate([low_cot, high_cot, far_cot], axis=0),
        jnp.concatenate([far_cot, low_cot, high_cot], axis=0),
    )
    cot_rows = lax.dynamic_slice_in_dim(chip_cot, core * count, count, 0)


    ffn_vectors = jnp.stack([down_bias, ffn_gain, ffn_shift]).astype(f32)
    output_rows, grad_ffn, ffn_sums = ffn_norm(
        hidden_low, ffn_own, core_swap(ffn_other), cot_rows, ffn_vectors
    )
    grad_other = core_swap(grad_ffn)
    grad_ffn_both = jnp.concatenate([grad_ffn, grad_other], axis=0)
    out_pieces = [output_rows] + tp_shifts(output_rows)
    back_own, back_other, up_keep, up_give, down_keep, down_give, up_sums = ffn_back(
        place, grad_ffn_both, hidden_both, acts, slope, rest
    )
    back_own, out_pieces[1] = tie(back_own, out_pieces[1])
    grad_one, grad_attn, grad_mixed, attn_sums = attend_norm(
        grad_ffn, back_own, core_swap(back_other), normed_one, inv_one, attn_vectors, full_out
    )
    up_got = across_swap(up_give)
    down_got = shard_swap(down_give)
    grad_scaled, grad_keys, grad_values = attend_back(*attention, grad_mixed, logs)
    grad_keys, up_got, down_got, out_pieces[2] = tie(grad_keys, up_got, down_got, out_pieces[2])
    up_parts = [low_sum(up_keep[i], up_got[i]) for i in (0, 1)]
    down_parts = [low_sum(down_keep[i], down_got[i]) for i in (0, 1)]
    up_got, down_got = shard_swap(up_parts[1]), across_swap(down_parts[1])
    own_sum, first, second, give = span_grads(
        place, grad_scaled, grad_keys, grad_values, weights_t, grad_one
    )
    got = core_swap(give)
    shared = reach - count
    to_own = lax.dynamic_slice_in_dim(got, (1 - core) * shared, count, 0)
    to_next = lax.dynamic_slice_in_dim(got, core * count, shared, 0)
    no_rows = jnp.zeros((count - shared, width), bf16)
    first = low_sum(
        first,
        jnp.where(
            core == 0,
            jnp.concatenate([no_rows, to_next], axis=0),
            jnp.concatenate([to_next, no_rows], axis=0),
        ),
    )
    first_now, up_got, down_got, out_pieces[3] = tie(first, up_got, down_got, out_pieces[3])
    ffn_parts = jnp.concatenate(
        [low_sum(up_parts[0], up_got), low_sum(down_parts[0], down_got)], axis=1
    )
    ffn_near = scatter_tp_start(ffn_parts)
    first_got = lax.ppermute(first, ("ctx", "tp"), chain_pairs(1))
    second_got = lax.ppermute(second, ("ctx", "tp"), chain_pairs(0))
    grad_keys, first_now = tie(grad_keys, first)
    attn_parts = attn_grads(
        place,
        grad_scaled,
        grad_keys,
        grad_values,
        mixed,
        grad_attn,
        in_window,
        attn_sums,
        ffn_sums,
        up_sums,
    )
    first_got, second_got, attn_keep, attn_give, ffn_near[1], ffn_near[3] = tie(
        first_got, second_got, *attn_parts, ffn_near[1], ffn_near[3]
    )
    attn_core = core_swap(attn_give)
    own_sum += to_own.astype(f32) + first_got.astype(f32)
    own_sum += jnp.where(
        core == 0,
        jnp.concatenate([no_rows, second_got], axis=0),
        jnp.concatenate([second_got, no_rows], axis=0),
    ).astype(f32)
    own_low = own_sum.astype(bf16)
    in_moves = deliver_start(own_low)
    *in_moves, attn_core, ffn_near[2] = tie(*in_moves, attn_core, ffn_near[2])
    in_packed = deliver_pack(own_low, *in_moves)
    in_pieces = [in_packed] + tp_shifts(in_packed)
    attn_parts = [low_sum(attn_keep[i], attn_core[i]) for i in (0, 1)]
    attn_got = shard_swap(attn_parts[1])
    parity = (tp + 1 + across + core) & 1
    out_sent = [
        jnp.where(
            core == 0,
            jnp.where(parity == 0, even[:block], odd_one[:block]),
            jnp.where(parity == 0, even[-block:], odd_one[-block:]),
        )
        for even, odd_one in (out_pieces[:2], out_pieces[2:])
    ]
    out_foreign = lax.ppermute(jnp.stack(out_sent), "ctx", [(i, 3 - i) for i in range(4)])
    out_middle = core_swap(
        jnp.stack(
            [
                jnp.where(((across + tp + k) & 1) == 0, piece[block:], piece[:half_block])
                for k, piece in enumerate(out_pieces)
            ]
        )
    )
    attn_got, in_pieces[1], in_pieces[3] = tie(attn_got, in_pieces[1], in_pieces[3])
    attn_mid = [low_sum(attn_parts[0][i], attn_got[i]) for i in (0, 1)]
    attn_got = across_swap(attn_mid[1])
    ffn_low = scatter_tp_end(ffn_near)
    ffn_got = across_swap(ffn_low)
    attn_got, out_foreign, out_middle = tie(attn_got, out_foreign, out_middle)
    attn_near = scatter_tp_start(low_sum(attn_mid[0], attn_got))
    layer_output = assemble(
        assemble_late_kernel, place, out_pieces, (out_middle, out_foreign), seqs, bf16
    )
    layer_output, in_pieces[2], attn_near[3], ffn_got = tie(
        layer_output, in_pieces[2], attn_near[3], ffn_got
    )
    in_halves = core_swap(jnp.stack([piece[block:] for piece in in_pieces]))
    input_grad = assemble(assemble_kernel, place, in_pieces, (in_halves,), seqs, f32)
    up_grad, down_grad = finish(
        finish_ffn_kernel,
        place,
        (ffn_low, ffn_got, core_swap(ffn_low), core_swap(ffn_got)),
        ((cut, 2 * cut), (2 * cut, cut)),
        "finish_ffn",
    )
    attn_low = scatter_tp_end(attn_near)
    attn_got, input_grad = tie(across_swap(attn_low), input_grad)
    *weight_grads, sums = finish(
        finish_attn_kernel,
        place,
        (attn_low, attn_got, core_swap(attn_low), core_swap(attn_got)),
        ((heads, depth),) * 4 + ((2, 2, 8, depth),),
        "finish_attn",
    )
    up_bias_grad = sums[:, 1, 5].reshape(-1)
    sums = sums[0].reshape(16, depth)
    row_sums = sums[1:13].reshape(6, width)
    return (
        layer_output,
        input_grad,
        weight_grads[0].T,
        sums[0, :heads],
        weight_grads[1].T,
        weight_grads[2].T,
        sums[0, heads:],
        weight_grads[3],
        row_sums[0],
        row_sums[1],
        row_sums[2],
        up_grad,
        up_bias_grad,
        down_grad,
        row_sums[3],
        row_sums[4],
        row_sums[5],
    )


def pick_plan(mesh):
    shape = dict(mesh.shape)

    def plan(layer_input, segment_ids, *others):
        seqs, block, _ = layer_input.shape
        fits = (
            (shape["shard"], shape["ctx"], shape["tp"]) == (2, 4, 4)
            and seqs == 6
            and segment_ids.shape[1] == 4 * block
            and block == 2 * QBLOCK
        )
        chosen = span_shards if fits else general_shards
        return chosen(layer_input, segment_ids, *others)

    return plan


def solution(mesh):
    return jax.shard_map(
        pick_plan(mesh),
        mesh=mesh,
        in_specs=(
            P("shard", "ctx", None),
            P("shard", None),
            P("shard", "tp"),
            P("tp"),
            P("shard", "tp"),
            P("shard", "tp"),
            P("tp"),
            P("tp", "shard"),
            P(),
            P(),
            P(),
            P("shard", "tp"),
            P("tp"),
            P("tp", "shard"),
            P(),
            P(),
            P(),
            P("shard", "ctx", None),
        ),
        out_specs=(
            P("shard", "ctx", None),
            P("shard", "ctx", None),
            P("shard", "tp"),
            P("tp"),
            P("shard", "tp"),
            P("shard", "tp"),
            P("tp"),
            P("tp", "shard"),
            P(),
            P(),
            P(),
            P("shard", "tp"),
            P("tp"),
            P("tp", "shard"),
            P(),
            P(),
            P(),
        ),
        check_vma=False,
    )
```

profile of v0, /device:TPU:1, one launch (start us, length us, event | category | flops | bytes accessed | tf_op | source)
XLA Modules:
  0.0 333.9 jit_solution(10387591024884396391)
XLA Ops:
  19.4 5.3 %collective-permute-done.1 = bf16[304,384]{1,0:T(8,128)(2,1)} collective-permute-done((bf16[304,384]{1,0:T(8,128)(2,1)}, bf16[304,384]{1,0:T(8,128)(2,1)}, u32[]{:S(2)}, u32[]{:S(2)}) %collective-permute-start.1) | collective-permute-done | bytes 233504 | tf_op jit(solution)/shard_map/ppermute | solution.py:1168
  24.8 3.7 %collective-permute-done.4 = bf16[864,384]{1,0:T(8,128)(2,1)} collective-permute-done((bf16[864,384]{1,0:T(8,128)(2,1)}, bf16[864,384]{1,0:T(8,128)(2,1)}, u32[]{:S(2)}, u32[]{:S(2)}) %collective-permute-start.4) | collective-permute-done | bytes 663584 | tf_op jit(solution)/shard_map/ppermute | solution.py:1181
  28.9 2.6 fusion.41
  37.8 3.1 collective-permute-start.7
  45.9 2.8 collective-permute-done.6
  48.7 2.9 collective-permute-done.5
  53.1 3.7 %collective-permute-start.8 = (bf16[2,4,304,384]{3,2,1,0:T(8,128)(2,1)S(1)}, bf16[2,4,304,384]{3,2,1,0:T(8,128)(2,1)}, u32[]{:S(2)}, u32[]{:S(2)}) collective-permute-start(bf16[2,4,304,384]{3,2,1,0:T(8,128)(2,1)S(1)} %pad_maximum_fusion.1.w_mine), channel_id=1, source_target_pairs={{0,4},{4,0},{8,12},{12,8},{1,5},{5,1},{9,13},{13,9},{2,6},{6,2},{1... | collective-permute-start | bytes 5603336 | tf_op jit(solution)/shard_map/ppermute | solution.py:1134
  71.3 7.4 %project.1 = (bf16[384,768]{1,0:T(8,128)(2,1)S(1)}, bf16[1408,768]{1,0:T(8,128)(2,1)S(1)}, bf16[1408,768]{1,0:T(8,128)(2,1)S(1)}, bf16[1408,768]{1,0:T(8,128)(2,1)S(1)}, bf16[3,768,768]{2,1,0:T(8,128)(2,1)S(1)}) custom-call(s32[5]{0:T(128)S(1)} %stack.253.place_ref, bf16[2,4,304,384]{3,2,1,0:T(8,128)(2,1)S(1)} %pad_maximum_fusion.1.w_mine, ...), custom_call_target="tpu_custom_call" | custom-call | flops 3321888768 | bytes 16777216 | tf_op jit(solution)/shard_map/project/pallas_call | solution.py:694
  81.0 6.5 %attend.2 = (bf16[384,768]{1,0:T(8,128)(2,1)S(1)}, f32[2,384,6]{2,1,0:T(8,128)S(1)}) custom-call(bf16[384,768]{1,0:T(8,128)(2,1)S(1)} %get-tuple-element.145.q_ref, bf16[1408,768]{1,0:T(8,128)(2,1)S(1)} %get-tuple-element.146.k_ref, bf16[1408,768]{1,0:T(8,128)(2,1)S(1)} %get-tuple-element.147.v_ref, s32[1,1408]{1,0:T(1,128)S(1)} %broadcast_in_dim.18.kd_ref, ...), custom_call_target="tpu_custom_call" | custom-call | flops 2717908992 | bytes 4194304 | tf_op jit(solution)/shard_map/attend/pallas_call | solution.py:393
  87.6 6.9 %collective-permute-done.13 = bf16[480,384]{1,0:T(8,128)(2,1)S(1)} collective-permute-done((bf16[480,384]{1,0:T(8,128)(2,1)S(1)}, bf16[480,384]{1,0:T(8,128)(2,1)S(1)}, u32[]{:S(2)}, u32[]{:S(2)}) %collective-permute-start.13) | collective-permute-done | bytes 368672 | tf_op jit(solution)/shard_map/ppermute | solution.py:1168
  95.8 6.6 %attend.3 = (bf16[384,768]{1,0:T(8,128)(2,1)S(1)}, f32[2,384,6]{2,1,0:T(8,128)S(1)}) custom-call(bf16[384,768]{1,0:T(8,128)(2,1)S(1)} %get-tuple-element.145.q_ref, bf16[1408,768]{1,0:T(8,128)(2,1)S(1)} %get-tuple-element.146.k_ref, bf16[1408,768]{1,0:T(8,128)(2,1)S(1)} %get-tuple-element.147.v_ref, ...), custom_call_target="tpu_custom_call", output_to_operand_aliasing={{0}: (5, {}), {1}: (6, {})} | custom-call | flops 2717908992 | bytes 4194304 | tf_op jit(solution)/shard_map/attend/pallas_call | solution.py:393
  112.4 7.0 %ffn.2 = (bf16[768,1536]{1,0:T(8,128)(2,1)S(1)}, bf16[768,1536]{1,0:T(8,128)(2,1)S(1)}, f32[768,768]{1,0:T(8,128)S(1)}) custom-call(s32[5]{0:T(128)S(1)} %stack.253.place_ref, bf16[768,768]{1,0:T(8,128)(2,1)S(1)} %constant_dynamic-update-slice_fusion.hb_ref, bf16[4,2,768,384]{3,2,1,0:T(8,128)(2,1)S(1)} %pad_maximum_fusion.w_ref, ...), custom_call_target="tpu_custom_call" | custom-call | flops 8153726976 | bytes 9437184 | tf_op jit(solution)/shard_map/ffn/pallas_call | solution.py:589
  119.8 2.5 ffn.3
  129.4 13.0 %ffn_back.1 = (bf16[384,768]{1,0:T(8,128)(2,1)S(1)}, bf16[384,768]{1,0:T(8,128)(2,1)S(1)}, bf16[2,4,192,384]{3,2,1,0:T(8,128)(2,1)S(1)}, bf16[2,4,192,384]{3,2,1...) custom-call(s32[5]{0:T(128)S(1)} %stack.253.place_ref, ...), custom_call_target="tpu_custom_call" | custom-call | flops 10871635968 | bytes 20971520 | tf_op jit(solution)/shard_map/ffn_back/pallas_call | solution.py:611
  148.9 23.4 %attend_back.1 = (bf16[384,768]{1,0:T(8,128)(2,1)S(1)}, bf16[1408,768]{1,0:T(8,128)(2,1)S(1)}, bf16[1408,768]{1,0:T(8,128)(2,1)S(1)}) custom-call(bf16[384,768]{1,0:T(8,128)(2,1)S(1)} %get-tuple-element.145.q_ref, bf16[1408,768]{1,0:T(8,128)(2,1)S(1)} %get-tuple-element.146.k_ref, bf16[1408,768]{1,0:T(8,128)(2,1)S(1)} %get-tuple-element.147.v_ref, ...), custom_call_target="tpu_custom_call" | custom-call | flops 13589544960 | bytes 12582912 | tf_op jit(solution)/shard_map/attend_back/pallas_call | solution.py:417
  172.4 6.3 %span_grads.1 = (f32[384,768]{1,0:T(8,128)S(1)}, bf16[384,768]{1,0:T(8,128)(2,1)S(1)}, bf16[128,768]{1,0:T(8,128)(2,1)S(1)}, bf16[512,768]{1,0:T(8,128)(2,1)}) custom-call(s32[5]{0:T(128)S(1)} %stack.253.place_ref, bf16[384,768]{1,0:T(8,128)(2,1)S(1)} %get-tuple-element.190.dq_ref, bf16[1408,768]{1,0:T(8,128)(2,1)S(1)} %get-tuple-element.203.dk_ref, ...), custom_call_target="tpu_custom_call" | custom-call | flops 3321888768 | bytes 12582912 | tf_op jit(solution)/shard_map/span_grads/pallas_call | solution.py:993
  185.0 2.6 collective-permute-start.32
  189.8 4.0 %collective-permute-start.31 = (bf16[384,768]{1,0:T(8,128)(2,1)S(1)}, bf16[384,768]{1,0:T(8,128)(2,1)S(1)}, u32[]{:S(2)}, u32[]{:S(2)}) collective-permute-start(bf16[384,768]{1,0:T(8,128)(2,1)S(1)} %add_convert_fusion.7), channel_id=1, source_target_pairs={{4,1},{1,4},{5,9},{9,5},{13,8},{8,13},{6,3},{3,6},{7,11},{11,7},{1... | collective-permute-start | bytes 1769480 | tf_op jit(solution)/shard_map/ppermute | solution.py:1449
  193.8 2.9 collective-permute-done.30.four
  204.2 2.7 collective-permute-start.34
  208.6 8.3 %attn_grads.1 = (bf16[2,2,4,200,384]{4,3,2,1,0:T(8,128)(2,1)S(1)}, bf16[2,2,4,200,384]{4,3,2,1,0:T(8,128)(2,1)}) custom-call(s32[5]{0:T(128)S(1)} %stack.253.place_ref, bf16[384,768]{1,0:T(8,128)(2,1)S(1)} %copy-done.25, bf16[1408,768]{1,0:T(8,128)(2,1)S(1)} %copy-done.21, bf16[1408,768]{1,0:T(8,128)(2,1)S(1)} %copy-done.23, ...), custom_call_target="tpu_custom_call" | custom-call | flops 4227858432 | bytes 16777216 | tf_op jit(solution)/shard_map/attn_grads/pallas_call | solution.py:918
  229.6 8.6 %collective-permute-done.39 = bf16[384,384]{1,0:T(8,128)(2,1)S(1)} collective-permute-done((bf16[384,384]{1,0:T(8,128)(2,1)S(1)}, bf16[384,384]{1,0:T(8,128)(2,1)S(1)}, u32[]{:S(2)}, u32[]{:S(2)}) %collective-permute-start.39) | collective-permute-done | bytes 294944 | tf_op jit(solution)/shard_map/ppermute | solution.py:1193
  243.2 3.3 collective-permute-start.42
  249.9 9.3 %collective-permute-done.41.two = bf16[384,768]{1,0:T(8,128)(2,1)S(1)} collective-permute-done((bf16[384,768]{1,0:T(8,128)(2,1)S(1)}, bf16[384,768]{1,0:T(8,128)(2,1)S(1)}, u32[]{:S(2)}, u32[]{:S(2)}) %collective-permute-start.41) | collective-permute-done | bytes 589856 | tf_op jit(solution)/shard_map/ppermute | solution.py:1168
  259.2 10.8 %collective-permute-done.42.four = bf16[384,768]{1,0:T(8,128)(2,1)S(1)} collective-permute-done((bf16[384,768]{1,0:T(8,128)(2,1)S(1)}, bf16[384,768]{1,0:T(8,128)(2,1)S(1)}, u32[]{:S(2)}, u32[]{:S(2)}) %collective-permute-start.42) | collective-permute-done | bytes 589856 | tf_op jit(solution)/shard_map/ppermute | solution.py:1168
  277.2 9.0 %collective-permute-done.43 = bf16[4,200,384]{2,1,0:T(8,128)(2,1)} collective-permute-done((bf16[4,200,384]{2,1,0:T(8,128)(2,1)}, bf16[4,200,384]{2,1,0:T(8,128)(2,1)}, u32[]{:S(2)}, u32[]{:S(2)}) %collective-permute-start.43) | collective-permute-done | bytes 614432 | tf_op jit(solution)/shard_map/ppermute | solution.py:1134
  287.7 2.4 collective-permute-start.47
  290.2 3.1 assemble.2
  293.3 6.9 %collective-permute-done.46.three = bf16[384,768]{1,0:T(8,128)(2,1)S(1)} collective-permute-done((bf16[384,768]{1,0:T(8,128)(2,1)S(1)}, bf16[384,768]{1,0:T(8,128)(2,1)S(1)}, u32[]{:S(2)}, u32[]{:S(2)}) %collective-permute-start.46) | collective-permute-done | bytes 589856 | tf_op jit(solution)/shard_map/ppermute | solution.py:1168
  300.2 4.0 %collective-permute-done.47 = bf16[200,384]{1,0:T(8,128)(2,1)S(1)} collective-permute-done((bf16[200,384]{1,0:T(8,128)(2,1)S(1)}, bf16[200,384]{1,0:T(8,128)(2,1)S(1)}, u32[]{:S(2)}, u32[]{:S(2)}) %collective-permute-start.47) | collective-permute-done | bytes 153632 | tf_op jit(solution)/shard_map/ppermute | solution.py:1193
  307.3 11.0 %collective-permute-done.50 = bf16[200,384]{1,0:T(8,128)(2,1)S(1)} collective-permute-done((bf16[200,384]{1,0:T(8,128)(2,1)S(1)}, bf16[200,384]{1,0:T(8,128)(2,1)S(1)}, u32[]{:S(2)}, u32[]{:S(2)}) %collective-permute-start.50) | collective-permute-done | bytes 153632 | tf_op jit(solution)/shard_map/ppermute | solution.py:1193
  321.2 3.1 assemble.3
  (349 shorter events, 135.8 us)
Async XLA Ops:
  4.1 15.3 %collective-permute-start = (bf16[304,384]{1,0:T(8,128)(2,1)}, bf16[304,384]{1,0:T(8,128)(2,1)}, u32[]{:S(2)}, u32[]{:S(2)}) collective-permute-start(bf16[304,384]{1,0:T(8,128)(2,1)} %maximum_maximum_fusion), channel_id=1, source_target_pairs={{0,1},{1,2},{2,3},{3,0},{4,5},{5,6},{6,7},{7,4},{8,9},{9,10},{10,1... | collective-permute-start | bytes 700424 | tf_op jit(solution)/shard_map/ppermute | solution.py:1168
  6.2 18.5 %collective-permute-start.1 = (bf16[304,384]{1,0:T(8,128)(2,1)}, bf16[304,384]{1,0:T(8,128)(2,1)}, u32[]{:S(2)}, u32[]{:S(2)}) collective-permute-start(bf16[304,384]{1,0:T(8,128)(2,1)} %maximum_maximum_fusion), channel_id=1, source_target_pairs={{0,2},{1,3},{2,0},{3,1},{4,6},{5,7},{6,4},{7,5},{8,10},{9,11},{10,... | collective-permute-start | bytes 700424 | tf_op jit(solution)/shard_map/ppermute | solution.py:1168
  8.5 16.2 %collective-permute-start.2 = (bf16[304,384]{1,0:T(8,128)(2,1)}, bf16[304,384]{1,0:T(8,128)(2,1)}, u32[]{:S(2)}, u32[]{:S(2)}) collective-permute-start(bf16[304,384]{1,0:T(8,128)(2,1)} %maximum_maximum_fusion), channel_id=1, source_target_pairs={{0,3},{1,0},{2,1},{3,2},{4,7},{5,4},{6,5},{7,6},{8,11},{9,8},{10,9... | collective-permute-start | bytes 700424 | tf_op jit(solution)/shard_map/ppermute | solution.py:1168
  11.2 17.7 %collective-permute-start.3 = (bf16[2,256,768]{2,1,0:T(8,128)(2,1)S(1)}, bf16[2,256,768]{2,1,0:T(8,128)(2,1)S(1)}, u32[]{:S(2)}, u32[]{:S(2)}) collective-permute-start(bf16[2,256,768]{2,1,0:T(8,128)(2,1)S(1)} %get-tuple-element.246), channel_id=1, source_target_pairs={{0,8},{4,12},{8,0},{12,4},{1,9},{5,13},{9,1},{13,5},{2,10},{6,14},... | collective-permute-start | bytes 2359304 | tf_op jit(solution)/shard_map/ppermute | solution.py:1134
  31.4 20.2 %collective-permute-start.5 = (bf16[4,304,384]{2,1,0:T(8,128)(2,1)}, bf16[4,304,384]{2,1,0:T(8,128)(2,1)}, u32[]{:S(2)}, u32[]{:S(2)}) collective-permute-start(bf16[4,304,384]{2,1,0:T(8,128)(2,1)} %get-tuple-element.257), channel_id=1, source_target_pairs={{0,16},{16,0},{1,17},{17,1},{2,18},{18,2},{3,19},{19,3},{4,20},{20... | collective-permute-start | bytes 2801672 | tf_op jit(solution)/shard_map/ppermute | solution.py:1181
  32.7 16.0 %collective-permute-start.6 = (bf16[864,384]{1,0:T(8,128)(2,1)}, bf16[864,384]{1,0:T(8,128)(2,1)}, u32[]{:S(2)}, u32[]{:S(2)}) collective-permute-start(bf16[864,384]{1,0:T(8,128)(2,1)} %pad_maximum_fusion.10), channel_id=1, source_target_pairs={{0,1},{1,2},{2,3},{3,0},{4,5},{5,6},{6,7},{7,4},{8,9},{9,10},{10,1... | collective-permute-start | bytes 1990664 | tf_op jit(solution)/shard_map/ppermute | solution.py:1168
  33.9 30.6 %collective-permute-start.9 = (bf16[864,384]{1,0:T(8,128)(2,1)}, bf16[864,384]{1,0:T(8,128)(2,1)}, u32[]{:S(2)}, u32[]{:S(2)}) collective-permute-start(bf16[864,384]{1,0:T(8,128)(2,1)} %pad_maximum_fusion.10), channel_id=1, source_target_pairs={{0,3},{1,0},{2,1},{3,2},{4,7},{5,4},{6,5},{7,6},{8,11},{9,8},{10,9... | collective-permute-start | bytes 1990664 | tf_op jit(solution)/shard_map/ppermute | solution.py:1168
  41.1 30.2 %collective-permute-start.10 = (bf16[2,2,256,768]{3,2,1,0:T(8,128)(2,1)S(1)}, bf16[2,2,256,768]{3,2,1,0:T(8,128)(2,1)}, u32[]{:S(2)}, u32[]{:S(2)}) collective-permute-start(bf16[2,2,256,768]{3,2,1,0:T(8,128)(2,1)S(1)} %pad_maximum_fusion.2.x_mine), channel_id=1, source_target_pairs={{0,4},{4,0},{8,12},{12,8},{1,5},{5,1},{9,13},{13,9},{2,6},{6,2},{1... | collective-permute-start | bytes 4718600 | tf_op jit(solution)/shard_map/ppermute | solution.py:1134
  59.6 27.9 %collective-permute-start.11 = (bf16[864,384]{1,0:T(8,128)(2,1)}, bf16[864,384]{1,0:T(8,128)(2,1)S(1)}, u32[]{:S(2)}, u32[]{:S(2)}) collective-permute-start(bf16[864,384]{1,0:T(8,128)(2,1)} %collective-permute-done.6), channel_id=1, source_target_pairs={{0,16},{16,0},{1,17},{17,1},{2,18},{18,2},{3,19},{19,3},{4,20},{20... | collective-permute-start | bytes 1990664 | tf_op jit(solution)/shard_map/ppermute | solution.py:1181
  64.6 29.8 %collective-permute-start.12 = (bf16[864,384]{1,0:T(8,128)(2,1)}, bf16[864,384]{1,0:T(8,128)(2,1)S(1)}, u32[]{:S(2)}, u32[]{:S(2)}) collective-permute-start(bf16[864,384]{1,0:T(8,128)(2,1)} %collective-permute-done.9), channel_id=1, source_target_pairs={{0,16},{16,0},{1,17},{17,1},{2,18},{18,2},{3,19},{19,3},{4,20},{20... | collective-permute-start | bytes 1990664 | tf_op jit(solution)/shard_map/ppermute | solution.py:1181
  68.9 25.5 %collective-permute-start.13 = (bf16[480,384]{1,0:T(8,128)(2,1)S(1)}, bf16[480,384]{1,0:T(8,128)(2,1)S(1)}, u32[]{:S(2)}, u32[]{:S(2)}) collective-permute-start(bf16[480,384]{1,0:T(8,128)(2,1)S(1)} %slice.326), channel_id=1, source_target_pairs={{0,2},{1,3},{2,0},{3,1},{4,6},{5,7},{6,4},{7,5},{8,10},{9,11},{10,... | collective-permute-start | bytes 1105928 | tf_op jit(solution)/shard_map/ppermute | solution.py:1168
  69.0 33.4 %collective-permute-start.15 = (bf16[384,384]{1,0:T(8,128)(2,1)S(1)}, bf16[384,384]{1,0:T(8,128)(2,1)S(1)}, u32[]{:S(2)}, u32[]{:S(2)}) collective-permute-start(bf16[384,384]{1,0:T(8,128)(2,1)S(1)} %slice.327), channel_id=1, source_target_pairs={{0,2},{1,3},{2,0},{3,1},{4,6},{5,7},{6,4},{7,5},{8,10},{9,11},{10,... | collective-permute-start | bytes 884744 | tf_op jit(solution)/shard_map/ppermute | solution.py:1168
  78.8 44.5 %collective-permute-start.20 = (bf16[2,256,768]{2,1,0:T(8,128)(2,1)S(1)}, bf16[2,256,768]{2,1,0:T(8,128)(2,1)S(1)}, u32[]{:S(2)}, u32[]{:S(2)}) collective-permute-start(bf16[2,256,768]{2,1,0:T(8,128)(2,1)S(1)} %pad_maximum_fusion.6), channel_id=1, source_target_pairs={{0,4},{4,0},{8,12},{12,8},{1,5},{5,1},{9,13},{13,9},{2,6},{6,2},{1... | collective-permute-start | bytes 2359304 | tf_op jit(solution)/shard_map/ppermute | solution.py:1134
  127.3 16.3 %collective-permute-start.22 = (bf16[384,768]{1,0:T(8,128)(2,1)S(1)}, bf16[384,768]{1,0:T(8,128)(2,1)S(1)}, u32[]{:S(2)}, u32[]{:S(2)}) collective-permute-start(bf16[384,768]{1,0:T(8,128)(2,1)S(1)} %get-tuple-element.173.one), channel_id=1, source_target_pairs={{0,1},{1,2},{2,3},{3,0},{4,5},{5,6},{6,7},{7,4},{8,9},{9,10},{10,1... | collective-permute-start | bytes 1769480 | tf_op jit(solution)/shard_map/ppermute | solution.py:1168
  142.6 29.7 %collective-permute-start.26 = (bf16[384,768]{1,0:T(8,128)(2,1)S(1)}, bf16[384,768]{1,0:T(8,128)(2,1)S(1)}, u32[]{:S(2)}, u32[]{:S(2)}) collective-permute-start(bf16[384,768]{1,0:T(8,128)(2,1)S(1)} %get-tuple-element.173.one), channel_id=1, source_target_pairs={{0,2},{1,3},{2,0},{3,1},{4,6},{5,7},{6,4},{7,5},{8,10},{9,11},{10,... | collective-permute-start | bytes 1769480 | tf_op jit(solution)/shard_map/ppermute | solution.py:1168
  143.6 28.7 %collective-permute-start.24 = (bf16[2,4,192,384]{3,2,1,0:T(8,128)(2,1)S(1)}, bf16[2,4,192,384]{3,2,1,0:T(8,128)(2,1)S(1)}, u32[]{:S(2)}, u32[]{:S(2)}) collective-permute-start(bf16[2,4,192,384]{3,2,1,0:T(8,128)(2,1)S(1)} %get-tuple-element.187), channel_id=1, source_target_pairs={{0,8},{4,12},{8,0},{12,4},{1,9},{5,13},{9,1},{13,5},{2,10},{6,14},... | collective-permute-start | bytes 3538952 | tf_op jit(solution)/shard_map/ppermute | solution.py:1134
  144.8 27.5 %collective-permute-start.25 = (bf16[2,4,192,384]{3,2,1,0:T(8,128)(2,1)S(1)}, bf16[2,4,192,384]{3,2,1,0:T(8,128)(2,1)S(1)}, u32[]{:S(2)}, u32[]{:S(2)}) collective-permute-start(bf16[2,4,192,384]{3,2,1,0:T(8,128)(2,1)S(1)} %get-tuple-element.188), channel_id=1, source_target_pairs={{0,16},{16,0},{1,17},{17,1},{2,18},{18,2},{3,19},{19,3},{4,20},{20... | collective-permute-start | bytes 3538952 | tf_op jit(solution)/shard_map/ppermute | solution.py:1181
  181.4 15.3 %collective-permute-start.30 = (bf16[384,768]{1,0:T(8,128)(2,1)S(1)}, bf16[384,768]{1,0:T(8,128)(2,1)S(1)}, u32[]{:S(2)}, u32[]{:S(2)}) collective-permute-start(bf16[384,768]{1,0:T(8,128)(2,1)S(1)} %get-tuple-element.173.one), channel_id=1, source_target_pairs={{0,3},{1,0},{2,1},{3,2},{4,7},{5,4},{6,5},{7,6},{8,11},{9,8},{10,9... | collective-permute-start | bytes 1769480 | tf_op jit(solution)/shard_map/ppermute | solution.py:1168
  182.6 15.1 %collective-permute-start.28 = (bf16[4,192,384]{2,1,0:T(8,128)(2,1)}, bf16[4,192,384]{2,1,0:T(8,128)(2,1)}, u32[]{:S(2)}, u32[]{:S(2)}) collective-permute-start(bf16[4,192,384]{2,1,0:T(8,128)(2,1)} %fusion.9), channel_id=1, source_target_pairs={{0,16},{16,0},{1,17},{17,1},{2,18},{18,2},{3,19},{19,3},{4,20},{20... | collective-permute-start | bytes 1769480 | tf_op jit(solution)/shard_map/ppermute | solution.py:1181
  185.0 33.3 %collective-permute-start.32 = (bf16[128,768]{1,0:T(8,128)(2,1)}, bf16[128,768]{1,0:T(8,128)(2,1)S(1)}, u32[]{:S(2)}, u32[]{:S(2)}) collective-permute-start(bf16[128,768]{1,0:T(8,128)(2,1)} %copy-done.17), channel_id=1, source_target_pairs={{4,5},{1,0},{5,13},{9,1},{13,12},{8,9},{6,7},{3,2},{7,15},{11,3},{... | collective-permute-start | bytes 589832 | tf_op jit(solution)/shard_map/ppermute | solution.py:1450
  189.8 28.6 %collective-permute-start.31 = (bf16[384,768]{1,0:T(8,128)(2,1)S(1)}, bf16[384,768]{1,0:T(8,128)(2,1)S(1)}, u32[]{:S(2)}, u32[]{:S(2)}) collective-permute-start(bf16[384,768]{1,0:T(8,128)(2,1)S(1)} %add_convert_fusion.7), channel_id=1, source_target_pairs={{4,1},{1,4},{5,9},{9,5},{13,8},{8,13},{6,3},{3,6},{7,11},{11,7},{1... | collective-permute-start | bytes 1769480 | tf_op jit(solution)/shard_map/ppermute | solution.py:1449
  219.4 19.5 %collective-permute-start.38 = (bf16[2,2,4,200,384]{4,3,2,1,0:T(8,128)(2,1)}, bf16[2,2,4,200,384]{4,3,2,1,0:T(8,128)(2,1)}, u32[]{:S(2)}, u32[]{:S(2)}) collective-permute-start(bf16[2,2,4,200,384]{4,3,2,1,0:T(8,128)(2,1)} %get-tuple-element.216), channel_id=1, source_target_pairs={{0,4},{4,0},{8,12},{12,8},{1,5},{5,1},{9,13},{13,9},{2,6},{6,2},{1... | collective-permute-start | bytes 7372808 | tf_op jit(solution)/shard_map/ppermute | solution.py:1134
  222.4 15.9 %collective-permute-start.39 = (bf16[384,384]{1,0:T(8,128)(2,1)S(1)}, bf16[384,384]{1,0:T(8,128)(2,1)S(1)}, u32[]{:S(2)}, u32[]{:S(2)}) collective-permute-start(bf16[384,384]{1,0:T(8,128)(2,1)S(1)} %copy-done.51), channel_id=1, source_target_pairs={{0,2},{1,3},{2,0},{3,1},{4,6},{5,7},{6,4},{7,5},{8,10},{9,11},{10,... | collective-permute-start | bytes 884744 | tf_op jit(solution)/shard_map/ppermute | solution.py:1193
  241.2 29.6 %collective-permute-start.40 = (bf16[2,4,200,384]{3,2,1,0:T(8,128)(2,1)S(1)}, bf16[2,4,200,384]{3,2,1,0:T(8,128)(2,1)S(1)}, u32[]{:S(2)}, u32[]{:S(2)}) collective-permute-start(bf16[2,4,200,384]{3,2,1,0:T(8,128)(2,1)S(1)} %get-tuple-element.243), channel_id=1, source_target_pairs={{0,16},{16,0},{1,17},{17,1},{2,18},{18,2},{3,19},{19,3},{4,20},{20... | collective-permute-start | bytes 3686408 | tf_op jit(solution)/shard_map/ppermute | solution.py:1181
  243.1 16.1 %collective-permute-start.41 = (bf16[384,768]{1,0:T(8,128)(2,1)S(1)}, bf16[384,768]{1,0:T(8,128)(2,1)S(1)}, u32[]{:S(2)}, u32[]{:S(2)}) collective-permute-start(bf16[384,768]{1,0:T(8,128)(2,1)S(1)} %pad_maximum_fusion.12.one), channel_id=1, source_target_pairs={{0,1},{1,2},{2,3},{3,0},{4,5},{5,6},{6,7},{7,4},{8,9},{9,10},{10,1... | collective-permute-start | bytes 1769480 | tf_op jit(solution)/shard_map/ppermute | solution.py:1168
  243.2 26.8 %collective-permute-start.42 = (bf16[384,768]{1,0:T(8,128)(2,1)S(1)}, bf16[384,768]{1,0:T(8,128)(2,1)S(1)}, u32[]{:S(2)}, u32[]{:S(2)}) collective-permute-start(bf16[384,768]{1,0:T(8,128)(2,1)S(1)} %pad_maximum_fusion.12.one), channel_id=1, source_target_pairs={{0,3},{1,0},{2,1},{3,2},{4,7},{5,4},{6,5},{7,6},{8,11},{9,8},{10,9... | collective-permute-start | bytes 1769480 | tf_op jit(solution)/shard_map/ppermute | solution.py:1168
  247.5 29.7 %collective-permute-start.44 = (bf16[2,256,768]{2,1,0:T(8,128)(2,1)}, bf16[2,256,768]{2,1,0:T(8,128)(2,1)}, u32[]{:S(2)}, u32[]{:S(2)}) collective-permute-start(bf16[2,256,768]{2,1,0:T(8,128)(2,1)} %pad_maximum_fusion.7), channel_id=1, source_target_pairs={{0,12},{4,8},{8,4},{12,0},{1,13},{5,9},{9,5},{13,1},{2,14},{6,10},... | collective-permute-start | bytes 2359304 | tf_op jit(solution)/shard_map/ppermute | solution.py:1490
  249.9 27.3 %collective-permute-start.45 = (bf16[4,128,768]{2,1,0:T(8,128)(2,1)}, bf16[4,128,768]{2,1,0:T(8,128)(2,1)}, u32[]{:S(2)}, u32[]{:S(2)}) collective-permute-start(bf16[4,128,768]{2,1,0:T(8,128)(2,1)} %pad_maximum_fusion.8), channel_id=1, source_target_pairs={{0,4},{4,0},{8,12},{12,8},{1,5},{5,1},{9,13},{13,9},{2,6},{6,2},{1... | collective-permute-start | bytes 2359304 | tf_op jit(solution)/shard_map/ppermute | solution.py:1134
  272.1 28.1 %collective-permute-start.46 = (bf16[384,768]{1,0:T(8,128)(2,1)S(1)}, bf16[384,768]{1,0:T(8,128)(2,1)S(1)}, u32[]{:S(2)}, u32[]{:S(2)}) collective-permute-start(bf16[384,768]{1,0:T(8,128)(2,1)S(1)} %pad_maximum_fusion.12.one), channel_id=1, source_target_pairs={{0,2},{1,3},{2,0},{3,1},{4,6},{5,7},{6,4},{7,5},{8,10},{9,11},{10,... | collective-permute-start | bytes 1769480 | tf_op jit(solution)/shard_map/ppermute | solution.py:1168
  275.6 17.7 %collective-permute-start.48 = (bf16[384,384]{1,0:T(8,128)(2,1)S(1)}, bf16[384,384]{1,0:T(8,128)(2,1)S(1)}, u32[]{:S(2)}, u32[]{:S(2)}) collective-permute-start(bf16[384,384]{1,0:T(8,128)(2,1)S(1)} %fusion.20.mine), channel_id=1, source_target_pairs={{0,8},{4,12},{8,0},{12,4},{1,9},{5,13},{9,1},{13,5},{2,10},{6,14},... | collective-permute-start | bytes 884744 | tf_op jit(solution)/shard_map/ppermute | solution.py:1134
  287.7 16.5 %collective-permute-start.47 = (bf16[200,384]{1,0:T(8,128)(2,1)S(1)}, bf16[200,384]{1,0:T(8,128)(2,1)S(1)}, u32[]{:S(2)}, u32[]{:S(2)}) collective-permute-start(bf16[200,384]{1,0:T(8,128)(2,1)S(1)} %get-tuple-element.260), channel_id=1, source_target_pairs={{0,3},{1,0},{2,1},{3,2},{4,7},{5,4},{6,5},{7,6},{8,11},{9,8},{10,9... | collective-permute-start | bytes 460808 | tf_op jit(solution)/shard_map/ppermute | solution.py:1193
  304.4 16.8 %collective-permute-start.52 = (bf16[4,128,768]{2,1,0:T(8,128)(2,1)S(1)}, bf16[4,128,768]{2,1,0:T(8,128)(2,1)S(1)}, u32[]{:S(2)}, u32[]{:S(2)}) collective-permute-start(bf16[4,128,768]{2,1,0:T(8,128)(2,1)S(1)} %pad_maximum_fusion.9), channel_id=1, source_target_pairs={{0,4},{4,0},{8,12},{12,8},{1,5},{5,1},{9,13},{13,9},{2,6},{6,2},{1... | collective-permute-start | bytes 2359304 | tf_op jit(solution)/shard_map/ppermute | solution.py:1134
  (88 other events, 700.9 us)
where the time goes:
time: 339 us; the launch traced here: 334 us
  Pallas kernels  97 us (29%)
  waiting for transfers between devices  94.6 us (28%)
  starting transfers between devices  74.4 us (22%)
  other arithmetic  35.1 us (10%)
  local copies, waits for them, and re-layouts  30.4 us (9%)
    ppermute x13, waiting for transfers between devices, tp_shifts(): lax.ppermute(array[cut], 'tp', [(i, (i + shift) % 4) for i in range(4)])  46.7 us
    ppermute x6, waiting for transfers between devices, scatter_tp_start(): lax.ppermute(sent, 'tp', [(i, (i + shift) % 4) for i in range(4)])  23.7 us
    pallas_call x1, Pallas kernels, attend_back(): pl.pallas_call(partial(attend_back_kernel, span), grid=(2, count // QBLOC...  23.4 us
    ppermute x23, starting transfers between devices, ctx_swap(): return lax.ppermute(array, 'ctx', [(i, i ^ bit) for i in range(4)])  23.3 us
    ppermute x13, starting transfers between devices, tp_shifts(): lax.ppermute(array[cut], 'tp', [(i, (i + shift) % 4) for i in range(4)])  16.9 us
    ppermute x23, waiting for transfers between devices, ctx_swap(): return lax.ppermute(array, 'ctx', [(i, i ^ bit) for i in range(4)])  14.2 us
    pallas_call x2, Pallas kernels, attend(): pl.pallas_call(partial(attend_kernel, span), grid=(1, count // QBLOCK), i...  13.1 us
    pallas_call x1, Pallas kernels, ffn_back(): pl.pallas_call(ffn_back_kernel, grid_spec=pltpu.PrefetchScalarGridSpec(nu...  13 us
  transfers between devices with their start and end apart: 57, of which 22 were waited for; matrix products, arithmetic and copies ran while one was open for 13% of the time, Pallas kernels for 26%

commit v1 on v0

--- a/solution.py
+++ b/solution.py
@@ -447,13 +447,15 @@
         ref[index] += terms
 
 
-def ffn_kernel(first_block, place_ref, hb_ref, w_ref, bias_ref, *refs):
+def ffn_kernel(first_block, place_ref, h_ref, other_h_ref, w_ref, bias_ref, *refs):
     half = w_ref.shape[3]
-    count = hb_ref.shape[0] // 2
+    count = h_ref.shape[0]
     near, far = half_cols(place_ref[1], half), half_cols(1 - place_ref[1], half)
     hb_near = refs[-1]
-    hb_near[:, :half] = hb_ref[:, near]
-    hb_near[:, half:] = hb_ref[:, far]
+    for part, source in enumerate((h_ref, other_h_ref)):
+        rows = slice(part * count, (part + 1) * count)
+        hb_near[rows, :half] = source[:, near]
+        hb_near[rows, half:] = source[:, far]
 
     def chunk(block, rows, acts_ref, slope_ref):
         up = w_ref[block, :, :half].reshape(2 * half, half)
@@ -490,7 +492,9 @@
 def ffn_back_kernel(
     place_ref,
     dz_ref,
-    hb_ref,
+    other_dz_ref,
+    h_ref,
+    other_h_ref,
     acts_ref,
     slope_ref,
     w_ref,
@@ -520,8 +524,10 @@
     def _():
         total[...] = jnp.zeros_like(total)
         for to, cols in ((first, near), (second, far)):
-            dz_near[:, to] = dz_ref[:, cols]
-            rows_t[to] = hb_ref[:, cols].T
+            dz_near[:count, to] = dz_ref[:, cols]
+            dz_near[count:, to] = other_dz_ref[:, cols]
+            rows_t[to, :count] = h_ref[:, cols].T
+            rows_t[to, count:] = other_h_ref[:, cols].T
 
     for k, hid in enumerate((first, second)):
         for y, to in enumerate((first, second)):
@@ -577,10 +583,10 @@
     return pl.BlockSpec(shape, lambda *_: (0,) * len(shape))
 
 
-def ffn(place, rows, weights, bias, prior=()):
-    both, width = rows.shape
+def ffn(place, rows, other_rows, weights, bias, prior=()):
+    count, width = rows.shape
+    both = 2 * count
     tps, shards, _, half = weights.shape
-    count = both // 2
     vmem = pl.BlockSpec(memory_space=pltpu.VMEM)
     low = jax.ShapeDtypeStruct((count, width), jnp.bfloat16)
     hidden = jax.ShapeDtypeStruct((both, tps * half), jnp.bfloat16)
@@ -588,23 +594,23 @@
     steps = 1 if prior else tps - 1
     return pl.pallas_call(
         partial(ffn_kernel, bool(prior)),
-        in_specs=[pl.BlockSpec(memory_space=pltpu.SMEM)] + [vmem] * (3 + len(prior)),
+        in_specs=[pl.BlockSpec(memory_space=pltpu.SMEM)] + [vmem] * (4 + len(prior)),
         out_specs=[vmem] * (2 + len(last)),
         out_shape=[hidden, hidden] + last,
         scratch_shapes=[pltpu.VMEM((both, width), jnp.bfloat16)],
-        input_output_aliases={5: 0, 6: 1} if prior else {},
+        input_output_aliases={6: 0, 7: 1} if prior else {},
         compiler_params=pltpu.CompilerParams(vmem_limit_bytes=16 << 20),
         cost_estimate=pl.CostEstimate(
             flops=12 * both * width * steps * half, bytes_accessed=3 * steps << 20, transcendentals=0
         ),
         name="ffn",
-    )(place, rows, weights, bias, *prior)
-
-
-def ffn_back(place, grads, rows, acts, slope, weights):
-    both, width = rows.shape
+    )(place, rows, other_rows, weights, bias, *prior)
+
+
+def ffn_back(place, grads, other_grads, rows, other_rows, acts, slope, weights):
+    count, width = rows.shape
+    both = 2 * count
     tps, shards, _, half = weights.shape
-    count = both // 2
     block = pl.BlockSpec((both, 2 * half), lambda i, _: (0, i))
     parts = (2, tps, half // 2, half)
     low = jax.ShapeDtypeStruct((count, width), jnp.bfloat16)
@@ -614,8 +620,7 @@
             num_scalar_prefetch=1,
             grid=(tps // 2,),
             in_specs=[
-                once((both, width)),
-                once((both, width)),
+                *[once((count, width))] * 4,
                 block,
                 block,
                 pl.BlockSpec((2, shards, 2 * half, half), lambda i, _: (i, 0, 0, 0)),
@@ -647,7 +652,7 @@
             flops=12 * both * width * tps * half, bytes_accessed=20 << 20, transcendentals=0
         ),
         name="ffn_back",
-    )(place, grads, rows, acts, slope, weights)
+    )(place, grads, other_grads, rows, other_rows, acts, slope, weights)
 
 
 def project_kernel(
@@ -804,29 +809,44 @@
     add_or_set(pl.program_id(0) == 0, sums_ref, slice(None), sums)
 
 
-def ffn_norm_kernel(h_ref, own_ref, got_ref, g_ref, vec_ref, y_ref, dz_ref, sums_ref):
+def cot_source(i, place_ref):
+    core, tp, across = place_ref[0], place_ref[2], place_ref[3]
+    odd = (across + tp) & 1
+    block = 3 * core + i - 2 * odd
+    block = jnp.where(block < 0, block + 6, block)
+    far = block >> 1 == 2
+    held = jnp.where(far, core == odd, core == (block >> 1))
+    return jnp.where(far, 1, 0), block & 1, jnp.where(held, 1, 0)
+
+
+def ffn_norm_kernel(
+    place_ref, h_ref, own_ref, got_ref, g_ref, g_other_ref, vec_ref, y_ref, dz_ref, sums_ref
+):
     resid = h_ref[...].astype(jnp.float32) + own_ref[...].astype(jnp.float32)
     resid += got_ref[...].astype(jnp.float32) + vec_ref[0:1]
     normed, inv_std = norm_pieces(resid)
     y_ref[...] = (normed * vec_ref[1:2] + vec_ref[2:3]).astype(jnp.bfloat16)
-    grad_out = g_ref[...].astype(jnp.float32)
+    held = cot_source(pl.program_id(0), place_ref)[2]
+    grad_out = jnp.where(held == 1, g_ref[0], g_other_ref[0]).astype(jnp.float32)
     low = norm_pull(grad_out, normed, inv_std, vec_ref[1:2]).astype(jnp.bfloat16)
     dz_ref[...] = low
     norm_sums(sums_ref, (low.astype(jnp.float32), grad_out * normed, grad_out))
 
 
-def ffn_norm(hidden, own, got, cots, vectors):
+def ffn_norm(place, hidden, own, got, cots, other_cots, vectors):
     count, width = hidden.shape
     rows = row_blocks(width)
+    cot = pl.BlockSpec((1, QBLOCK, width), lambda i, at: (*cot_source(i, at)[:2], 0))
     low = jax.ShapeDtypeStruct((count, width), jnp.bfloat16)
     return on_rows(
         ffn_norm_kernel,
         count,
-        [rows, rows, rows, rows, whole(vectors.shape)],
+        [rows, rows, rows, cot, cot, whole(vectors.shape)],
         [rows, rows, whole((3, width))],
         [low, low, jax.ShapeDtypeStruct((3, width), jnp.float32)],
         "ffn_norm",
-    )(hidden, own, got, cots, vectors)
+        1,
+    )(place, hidden, own, got, cots, other_cots, vectors)
 
 
 def attend_norm_kernel(
@@ -1093,8 +1113,9 @@
 
 
 def finish_attn_kernel(
-    place_ref, mine, across_got, core_got, both_got, q_ref, k_ref, v_ref, o_ref, sums_ref
+    place_ref, mine, across_got, core_got, both_got, q_ref, k_ref, v_ref, o_ref, *refs
 ):
+    *vectors, sums_ref = refs
     core, across = place_ref[0], place_ref[3]
     part = q_ref.shape[0] // 2
     for c, x, source in (
@@ -1116,14 +1137,25 @@
         def _():
             v_ref[rows], o_ref[rows] = one, two
 
-
-def finish(kernel, place, pieces, shapes, name):
+    def flat(*rows):
+        return jnp.concatenate(rows, axis=1).reshape(-1)
+
+    sums = sums_ref[core].reshape(16, 4 * part)
+    for r, to in enumerate(vectors[:6]):
+        to[...] = flat(sums[2 * r + 1 : 2 * r + 2], sums[2 * r + 2 : 2 * r + 3])
+    vectors[6][...] = flat(sums_ref[0, 1, 5:6], sums_ref[1, 1, 5:6])
+    vectors[7][...] = sums[0:1, : 2 * part].reshape(-1)
+    vectors[8][...] = sums[0:1, 2 * part :].reshape(-1)
+
+
+def finish(kernel, place, pieces, shapes, name, scratch=()):
     vmem = pl.BlockSpec(memory_space=pltpu.VMEM)
     return pl.pallas_call(
         kernel,
         in_specs=[pl.BlockSpec(memory_space=pltpu.SMEM)] + [vmem] * 4,
         out_specs=[vmem] * len(shapes),
         out_shape=[jax.ShapeDtypeStruct(shape, jnp.float32) for shape in shapes],
+        scratch_shapes=scratch,
         compiler_params=pltpu.CompilerParams(vmem_limit_bytes=8 << 20),
         cost_estimate=pl.CostEstimate(flops=1 << 20, bytes_accessed=4 << 20, transcendentals=0),
         name=name,
@@ -1344,7 +1376,7 @@
         place, mixed, in_window, reach, out_mine, core_swap(out_mine), attn_vectors
     )
     hidden_other = core_swap(hidden_low)
-    hidden_both = jnp.concatenate([hidden_low, hidden_other], axis=0)
+    hidden_both = hidden_low, hidden_other
     ffn_weights = jnp.stack(
         [
             own_pair,
@@ -1354,7 +1386,7 @@
         ]
     )
     ffn_bias = jnp.stack([up_bias_here[k] for k in (0, 1, 3, 2)])
-    acts, slope, ffn_sum = ffn(place, hidden_both, ffn_weights, ffn_bias)
+    acts, slope, ffn_sum = ffn(place, *hidden_both, ffn_weights, ffn_bias)
     ffn_sum, far_up_two = tie(ffn_sum, far_up_two)
     rest = ffn_weights.at[3].set(
         jnp.stack(
@@ -1365,7 +1397,7 @@
         )
     )
     acts, slope, ffn_own, ffn_other = ffn(
-        place, hidden_both, rest, ffn_bias, (ffn_sum, acts, slope)
+        place, *hidden_both, rest, ffn_bias, (ffn_sum, acts, slope)
     )
 
     half_block = block // 2
@@ -1394,25 +1426,15 @@
 
     cot_pair = tie(jnp.stack([near_cot, far_cot]), queries)[0]
     cot_swapped = core_swap(cot_pair)
-    low_cot, high_cot = in_order(core, near_cot, cot_swapped[0])
-    far_cot = jnp.where(core == odd, far_cot, cot_swapped[1])
-    chip_cot = jnp.where(
-        odd == 0,
-        jnp.concatenate([low_cot, high_cot, far_cot], axis=0),
-        jnp.concatenate([far_cot, low_cot, high_cot], axis=0),
-    )
-    cot_rows = lax.dynamic_slice_in_dim(chip_cot, core * count, count, 0)
-
 
     ffn_vectors = jnp.stack([down_bias, ffn_gain, ffn_shift]).astype(f32)
     output_rows, grad_ffn, ffn_sums = ffn_norm(
-        hidden_low, ffn_own, core_swap(ffn_other), cot_rows, ffn_vectors
+        place, hidden_low, ffn_own, core_swap(ffn_other), cot_pair, cot_swapped, ffn_vectors
     )
     grad_other = core_swap(grad_ffn)
-    grad_ffn_both = jnp.concatenate([grad_ffn, grad_other], axis=0)
     out_pieces = [output_rows] + tp_shifts(output_rows)
     back_own, back_other, up_keep, up_give, down_keep, down_give, up_sums = ffn_back(
-        place, grad_ffn_both, hidden_both, acts, slope, rest
+        place, grad_ffn, grad_other, *hidden_both, acts, slope, rest
     )
     back_own, out_pieces[1] = tie(back_own, out_pieces[1])
     grad_one, grad_attn, grad_mixed, attn_sums = attend_norm(
@@ -1520,24 +1542,24 @@
     )
     attn_low = scatter_tp_end(attn_near)
     attn_got, input_grad = tie(across_swap(attn_low), input_grad)
-    *weight_grads, sums = finish(
+    finished = finish(
         finish_attn_kernel,
         place,
         (attn_low, attn_got, core_swap(attn_low), core_swap(attn_got)),
-        ((heads, depth),) * 4 + ((2, 2, 8, depth),),
+        ((heads, depth),) * 4 + ((width,),) * 6 + ((2 * cut,), (heads,), (heads,)),
         "finish_attn",
-    )
-    up_bias_grad = sums[:, 1, 5].reshape(-1)
-    sums = sums[0].reshape(16, depth)
-    row_sums = sums[1:13].reshape(6, width)
+        [pltpu.VMEM((2, 2, 8, depth), f32)],
+    )
+    weight_grads, row_sums = finished[:4], finished[4:10]
+    up_bias_grad, query_bias_grad, value_bias_grad = finished[10:]
     return (
         layer_output,
         input_grad,
         weight_grads[0].T,
-        sums[0, :heads],
+        query_bias_grad,
         weight_grads[1].T,
         weight_grads[2].T,
-        sums[0, heads:],
+        value_bias_grad,
         weight_grads[3],
         row_sums[0],
         row_sums[1],

time: 339 us -> 336 us (level)
    ppermute x13, waiting for transfers between devices: 46.7 us -> 42.1 us  [tp_shifts(): lax.ppermute(array[cut], 'tp', [(i, (i + shift) % 4) for i in range(4)])]
    another operation x3, local copies, waits for them, and re-layouts: 0.02 us -> 3.78 us  [span_shards(): attn_vectors = jnp.stack([out_bias, attn_gain, attn_shift]).astype(f32)]
    squeeze x6 -> x0, local copies, waits for them, and re-layouts: 3.6 us -> none  [the longest x1 0.6 us: span_shards(): row_sums[0]]
    unnamed x126 -> x119, local copies, waits for them, and re-layouts: 8.8 us -> 9.87 us
  transfers between devices with their start and end apart: 57 -> 57, of which waited for: 22 -> 25; matrix products, arithmetic and copies ran while one was open for 13% -> 15% of each run, Pallas kernels for 26% -> 26%
where the time goes in v1:
time: 336 us; the launch traced here: 331 us
  Pallas kernels  97.1 us (29%)
  waiting for transfers between devices  92.5 us (28%)
  starting transfers between devices  73.2 us (22%)
  other arithmetic  35.9 us (11%)
  local copies, waits for them, and re-layouts  29.6 us (9%)
    ppermute x13, waiting for transfers between devices, tp_shifts(): lax.ppermute(array[cut], 'tp', [(i, (i + shift) % 4) for i in range(4)])  42.1 us
    ppermute x6, waiting for transfers between devices, scatter_tp_start(): lax.ppermute(sent, 'tp', [(i, (i + shift) % 4) for i in range(4)])  24.3 us
    pallas_call x1, Pallas kernels, attend_back(): pl.pallas_call(partial(attend_back_kernel, span), grid=(2, count // QBLOC...  23.4 us
    ppermute x23, starting transfers between devices, ctx_swap(): return lax.ppermute(array, 'ctx', [(i, i ^ bit) for i in range(4)])  22.5 us
    ppermute x13, starting transfers between devices, tp_shifts(): lax.ppermute(array[cut], 'tp', [(i, (i + shift) % 4) for i in range(4)])  16.7 us
    ppermute x23, waiting for transfers between devices, ctx_swap(): return lax.ppermute(array, 'ctx', [(i, i ^ bit) for i in range(4)])  14.9 us
    pallas_call x1, Pallas kernels, ffn_back(): pl.pallas_call(ffn_back_kernel, grid_spec=pltpu.PrefetchScalarGridSpec(nu...  13.2 us
    pallas_call x2, Pallas kernels, attend(): pl.pallas_call(partial(attend_kernel, span), grid=(1, count // QBLOCK), i...  13.1 us
  transfers between devices with their start and end apart: 57, of which 25 were waited for; matrix products, arithmetic and copies ran while one was open for 15% of the time, Pallas kernels for 26%

profile of v1, /device:TPU:1, one launch (start us, length us, event | category | flops | bytes accessed | tf_op | source)
XLA Modules:
  0.0 330.7 jit_solution(237443668978087092)
XLA Ops:
  9.1 2.7 dynamic-slice_bitcast_fusion
  25.2 3.8 %collective-permute-done.4 = bf16[864,384]{1,0:T(8,128)(2,1)} collective-permute-done((bf16[864,384]{1,0:T(8,128)(2,1)}, bf16[864,384]{1,0:T(8,128)(2,1)}, u32[]{:S(2)}, u32[]{:S(2)}) %collective-permute-start.4) | collective-permute-done | bytes 663584 | tf_op jit(solution)/shard_map/ppermute | solution.py:1213
  33.6 2.9 collective-permute-start.9
  37.2 3.1 collective-permute-start.7
  45.4 3.7 %collective-permute-done.6 = bf16[864,384]{1,0:T(8,128)(2,1)} collective-permute-done((bf16[864,384]{1,0:T(8,128)(2,1)}, bf16[864,384]{1,0:T(8,128)(2,1)}, u32[]{:S(2)}, u32[]{:S(2)}) %collective-permute-start.6) | collective-permute-done | bytes 663584 | tf_op jit(solution)/shard_map/ppermute | solution.py:1200
  49.1 2.9 collective-permute-done.5
  53.5 3.9 %collective-permute-start.8 = (bf16[2,4,304,384]{3,2,1,0:T(8,128)(2,1)S(1)}, bf16[2,4,304,384]{3,2,1,0:T(8,128)(2,1)}, u32[]{:S(2)}, u32[]{:S(2)}) collective-permute-start(bf16[2,4,304,384]{3,2,1,0:T(8,128)(2,1)S(1)} %pad_maximum_fusion.1.w_mine), channel_id=1, source_target_pairs={{0,4},{4,0},{8,12},{12,8},{1,5},{5,1},{9,13},{13,9},{2,6},{6,2},{1... | collective-permute-start | bytes 5603336 | tf_op jit(solution)/shard_map/ppermute | solution.py:1166
  72.9 7.0 %project.1 = (bf16[384,768]{1,0:T(8,128)(2,1)S(1)}, bf16[1408,768]{1,0:T(8,128)(2,1)S(1)}, bf16[1408,768]{1,0:T(8,128)(2,1)S(1)}, bf16[1408,768]{1,0:T(8,128)(2,1)S(1)}, bf16[3,768,768]{2,1,0:T(8,128)(2,1)S(1)}) custom-call(s32[5]{0:T(128)S(1)} %stack.253.place_ref, bf16[2,4,304,384]{3,2,1,0:T(8,128)(2,1)S(1)} %pad_maximum_fusion.1.w_mine, ...), custom_call_target="tpu_custom_call" | custom-call | flops 3321888768 | bytes 16777216 | tf_op jit(solution)/shard_map/project/pallas_call | solution.py:699
  81.7 6.5 %attend.2 = (bf16[384,768]{1,0:T(8,128)(2,1)S(1)}, f32[2,384,6]{2,1,0:T(8,128)S(1)}) custom-call(bf16[384,768]{1,0:T(8,128)(2,1)S(1)} %get-tuple-element.153.q_ref, bf16[1408,768]{1,0:T(8,128)(2,1)S(1)} %get-tuple-element.154.k_ref, bf16[1408,768]{1,0:T(8,128)(2,1)S(1)} %get-tuple-element.155.v_ref, s32[1,1408]{1,0:T(1,128)S(1)} %broadcast_in_dim.18.kd_ref, ...), custom_call_target="tpu_custom_call" | custom-call | flops 2717908992 | bytes 4194304 | tf_op jit(solution)/shard_map/attend/pallas_call | solution.py:393
  88.2 7.5 %collective-permute-done.13 = bf16[480,384]{1,0:T(8,128)(2,1)S(1)} collective-permute-done((bf16[480,384]{1,0:T(8,128)(2,1)S(1)}, bf16[480,384]{1,0:T(8,128)(2,1)S(1)}, u32[]{:S(2)}, u32[]{:S(2)}) %collective-permute-start.13) | collective-permute-done | bytes 368672 | tf_op jit(solution)/shard_map/ppermute | solution.py:1200
  96.8 6.6 %attend.3 = (bf16[384,768]{1,0:T(8,128)(2,1)S(1)}, f32[2,384,6]{2,1,0:T(8,128)S(1)}) custom-call(bf16[384,768]{1,0:T(8,128)(2,1)S(1)} %get-tuple-element.153.q_ref, bf16[1408,768]{1,0:T(8,128)(2,1)S(1)} %get-tuple-element.154.k_ref, bf16[1408,768]{1,0:T(8,128)(2,1)S(1)} %get-tuple-element.155.v_ref, ...), custom_call_target="tpu_custom_call", output_to_operand_aliasing={{0}: (5, {}), {1}: (6, {})} | custom-call | flops 2717908992 | bytes 4194304 | tf_op jit(solution)/shard_map/attend/pallas_call | solution.py:393
  114.2 7.0 %ffn.2 = (bf16[768,1536]{1,0:T(8,128)(2,1)S(1)}, bf16[768,1536]{1,0:T(8,128)(2,1)S(1)}, f32[768,768]{1,0:T(8,128)S(1)}) custom-call(s32[5]{0:T(128)S(1)} %stack.253.place_ref, bf16[384,768]{1,0:T(8,128)(2,1)S(1)} %get-tuple-element.169.h_ref, bf16[384,768]{1,0:T(8,128)(2,1)S(1)} %collective-permute-done.17.other_h_ref, ...), custom_call_target="tpu_custom_call" | custom-call | flops 8153726976 | bytes 9437184 | tf_op jit(solution)/shard_map/ffn/pallas_call | solution.py:595
  121.7 2.5 ffn.3
  131.0 13.2 %ffn_back.1 = (bf16[384,768]{1,0:T(8,128)(2,1)S(1)}, bf16[384,768]{1,0:T(8,128)(2,1)S(1)}, bf16[2,4,192,384]{3,2,1,0:T(8,128)(2,1)S(1)}, bf16[2,4,192,384]{3,2,1...) custom-call(s32[5]{0:T(128)S(1)} %stack.253.place_ref, ...), custom_call_target="tpu_custom_call" | custom-call | flops 10871635968 | bytes 20971520 | tf_op jit(solution)/shard_map/ffn_back/pallas_call | solution.py:617
  151.1 23.4 %attend_back.1 = (bf16[384,768]{1,0:T(8,128)(2,1)S(1)}, bf16[1408,768]{1,0:T(8,128)(2,1)S(1)}, bf16[1408,768]{1,0:T(8,128)(2,1)S(1)}) custom-call(bf16[384,768]{1,0:T(8,128)(2,1)S(1)} %get-tuple-element.153.q_ref, bf16[1408,768]{1,0:T(8,128)(2,1)S(1)} %get-tuple-element.154.k_ref, bf16[1408,768]{1,0:T(8,128)(2,1)S(1)} %get-tuple-element.155.v_ref, ...), custom_call_target="tpu_custom_call" | custom-call | flops 13589544960 | bytes 12582912 | tf_op jit(solution)/shard_map/attend_back/pallas_call | solution.py:417
  174.6 6.3 %span_grads.1 = (f32[384,768]{1,0:T(8,128)S(1)}, bf16[384,768]{1,0:T(8,128)(2,1)S(1)}, bf16[128,768]{1,0:T(8,128)(2,1)S(1)}, bf16[512,768]{1,0:T(8,128)(2,1)}) custom-call(s32[5]{0:T(128)S(1)} %stack.253.place_ref, bf16[384,768]{1,0:T(8,128)(2,1)S(1)} %get-tuple-element.198.dq_ref, bf16[1408,768]{1,0:T(8,128)(2,1)S(1)} %get-tuple-element.211.dk_ref, ...), custom_call_target="tpu_custom_call" | custom-call | flops 3321888768 | bytes 12582912 | tf_op jit(solution)/shard_map/span_grads/pallas_call | solution.py:1013
  186.4 3.1 collective-permute-start.32
  191.7 3.7 %collective-permute-start.31 = (bf16[384,768]{1,0:T(8,128)(2,1)S(1)}, bf16[384,768]{1,0:T(8,128)(2,1)S(1)}, u32[]{:S(2)}, u32[]{:S(2)}) collective-permute-start(bf16[384,768]{1,0:T(8,128)(2,1)S(1)} %add_convert_fusion.7), channel_id=1, source_target_pairs={{4,1},{1,4},{5,9},{9,5},{13,8},{8,13},{6,3},{3,6},{7,11},{11,7},{1... | collective-permute-start | bytes 1769480 | tf_op jit(solution)/shard_map/ppermute | solution.py:1471
  195.4 2.8 collective-permute-done.30.four
  209.3 8.3 %attn_grads.1 = (bf16[2,2,4,200,384]{4,3,2,1,0:T(8,128)(2,1)S(1)}, bf16[2,2,4,200,384]{4,3,2,1,0:T(8,128)(2,1)}) custom-call(s32[5]{0:T(128)S(1)} %stack.253.place_ref, bf16[384,768]{1,0:T(8,128)(2,1)S(1)} %copy-done.25, bf16[1408,768]{1,0:T(8,128)(2,1)S(1)} %copy-done.21, bf16[1408,768]{1,0:T(8,128)(2,1)S(1)} %copy-done.23, ...), custom_call_target="tpu_custom_call" | custom-call | flops 4227858432 | bytes 16777216 | tf_op jit(solution)/shard_map/attn_grads/pallas_call | solution.py:938
  225.6 3.5 %collective-permute-start.36 = (bf16[128,768]{1,0:T(8,128)(2,1)S(1)}, bf16[128,768]{1,0:T(8,128)(2,1)S(1)}, u32[]{:S(2)}, u32[]{:S(2)}) collective-permute-start(bf16[128,768]{1,0:T(8,128)(2,1)S(1)} %get-tuple-element.279), channel_id=1, source_target_pairs={{4,8},{8,0},{1,9},{13,1},{6,10},{10,2},{3,11},{15,3},{20,24},{24,1... | collective-permute-start | bytes 589832 | tf_op jit(solution)/shard_map/ppermute | solution.py:1409
  231.2 8.4 %collective-permute-done.39 = bf16[384,384]{1,0:T(8,128)(2,1)S(1)} collective-permute-done((bf16[384,384]{1,0:T(8,128)(2,1)S(1)}, bf16[384,384]{1,0:T(8,128)(2,1)S(1)}, u32[]{:S(2)}, u32[]{:S(2)}) %collective-permute-start.39) | collective-permute-done | bytes 294944 | tf_op jit(solution)/shard_map/ppermute | solution.py:1225
  243.8 3.3 collective-permute-start.42
  251.8 7.6 %collective-permute-done.41.two = bf16[384,768]{1,0:T(8,128)(2,1)S(1)} collective-permute-done((bf16[384,768]{1,0:T(8,128)(2,1)S(1)}, bf16[384,768]{1,0:T(8,128)(2,1)S(1)}, u32[]{:S(2)}, u32[]{:S(2)}) %collective-permute-start.41) | collective-permute-done | bytes 589856 | tf_op jit(solution)/shard_map/ppermute | solution.py:1200
  259.4 10.8 %collective-permute-done.42.four = bf16[384,768]{1,0:T(8,128)(2,1)S(1)} collective-permute-done((bf16[384,768]{1,0:T(8,128)(2,1)S(1)}, bf16[384,768]{1,0:T(8,128)(2,1)S(1)}, u32[]{:S(2)}, u32[]{:S(2)}) %collective-permute-start.42) | collective-permute-done | bytes 589856 | tf_op jit(solution)/shard_map/ppermute | solution.py:1200
  277.4 8.6 %collective-permute-done.43 = bf16[4,200,384]{2,1,0:T(8,128)(2,1)} collective-permute-done((bf16[4,200,384]{2,1,0:T(8,128)(2,1)}, bf16[4,200,384]{2,1,0:T(8,128)(2,1)}, u32[]{:S(2)}, u32[]{:S(2)}) %collective-permute-start.43) | collective-permute-done | bytes 614432 | tf_op jit(solution)/shard_map/ppermute | solution.py:1166
  289.9 3.1 assemble.2
  293.0 8.4 %collective-permute-done.46.three = bf16[384,768]{1,0:T(8,128)(2,1)S(1)} collective-permute-done((bf16[384,768]{1,0:T(8,128)(2,1)S(1)}, bf16[384,768]{1,0:T(8,128)(2,1)S(1)}, u32[]{:S(2)}, u32[]{:S(2)}) %collective-permute-start.46) | collective-permute-done | bytes 589856 | tf_op jit(solution)/shard_map/ppermute | solution.py:1200
  301.4 3.4 %collective-permute-done.47 = bf16[200,384]{1,0:T(8,128)(2,1)S(1)} collective-permute-done((bf16[200,384]{1,0:T(8,128)(2,1)S(1)}, bf16[200,384]{1,0:T(8,128)(2,1)S(1)}, u32[]{:S(2)}, u32[]{:S(2)}) %collective-permute-start.47) | collective-permute-done | bytes 153632 | tf_op jit(solution)/shard_map/ppermute | solution.py:1225
  308.7 4.7 %collective-permute-done.49 = bf16[200,384]{1,0:T(8,128)(2,1)S(1)} collective-permute-done((bf16[200,384]{1,0:T(8,128)(2,1)S(1)}, bf16[200,384]{1,0:T(8,128)(2,1)S(1)}, u32[]{:S(2)}, u32[]{:S(2)}) %collective-permute-start.49) | collective-permute-done | bytes 153632 | tf_op jit(solution)/shard_map/ppermute | solution.py:1225
  313.4 6.5 %collective-permute-done.50 = bf16[200,384]{1,0:T(8,128)(2,1)S(1)} collective-permute-done((bf16[200,384]{1,0:T(8,128)(2,1)S(1)}, bf16[200,384]{1,0:T(8,128)(2,1)S(1)}, u32[]{:S(2)}, u32[]{:S(2)}) %collective-permute-start.50) | collective-permute-done | bytes 153632 | tf_op jit(solution)/shard_map/ppermute | solution.py:1225
  321.7 3.1 assemble.3
  (326 shorter events, 136.2 us)
Async XLA Ops:
  3.5 21.6 %collective-permute-start = (bf16[304,384]{1,0:T(8,128)(2,1)S(1)}, bf16[304,384]{1,0:T(8,128)(2,1)}, u32[]{:S(2)}, u32[]{:S(2)}) collective-permute-start(bf16[304,384]{1,0:T(8,128)(2,1)S(1)} %maximum_maximum_fusion), channel_id=1, source_target_pairs={{0,1},{1,2},{2,3},{3,0},{4,5},{5,6},{6,7},{7,4},{8,9},{9,10},{10,1... | collective-permute-start | bytes 700424 | tf_op jit(solution)/shard_map/ppermute | solution.py:1200
  5.7 19.4 %collective-permute-start.1 = (bf16[304,384]{1,0:T(8,128)(2,1)S(1)}, bf16[304,384]{1,0:T(8,128)(2,1)}, u32[]{:S(2)}, u32[]{:S(2)}) collective-permute-start(bf16[304,384]{1,0:T(8,128)(2,1)S(1)} %maximum_maximum_fusion), channel_id=1, source_target_pairs={{0,2},{1,3},{2,0},{3,1},{4,6},{5,7},{6,4},{7,5},{8,10},{9,11},{10,... | collective-permute-start | bytes 700424 | tf_op jit(solution)/shard_map/ppermute | solution.py:1200
  8.0 17.1 %collective-permute-start.2 = (bf16[304,384]{1,0:T(8,128)(2,1)S(1)}, bf16[304,384]{1,0:T(8,128)(2,1)}, u32[]{:S(2)}, u32[]{:S(2)}) collective-permute-start(bf16[304,384]{1,0:T(8,128)(2,1)S(1)} %maximum_maximum_fusion), channel_id=1, source_target_pairs={{0,3},{1,0},{2,1},{3,2},{4,7},{5,4},{6,5},{7,6},{8,11},{9,8},{10,9... | collective-permute-start | bytes 700424 | tf_op jit(solution)/shard_map/ppermute | solution.py:1200
  11.8 17.8 %collective-permute-start.3 = (bf16[2,256,768]{2,1,0:T(8,128)(2,1)}, bf16[2,256,768]{2,1,0:T(8,128)(2,1)}, u32[]{:S(2)}, u32[]{:S(2)}) collective-permute-start(bf16[2,256,768]{2,1,0:T(8,128)(2,1)} %get-tuple-element.262), channel_id=1, source_target_pairs={{0,8},{4,12},{8,0},{12,4},{1,9},{5,13},{9,1},{13,5},{2,10},{6,14},... | collective-permute-start | bytes 2359304 | tf_op jit(solution)/shard_map/ppermute | solution.py:1166
  14.1 14.9 %collective-permute-start.4 = (bf16[864,384]{1,0:T(8,128)(2,1)}, bf16[864,384]{1,0:T(8,128)(2,1)}, u32[]{:S(2)}, u32[]{:S(2)}) collective-permute-start(bf16[864,384]{1,0:T(8,128)(2,1)} %pad_maximum_fusion.9), channel_id=1, source_target_pairs={{0,16},{16,0},{1,17},{17,1},{2,18},{18,2},{3,19},{19,3},{4,20},{20... | collective-permute-start | bytes 1990664 | tf_op jit(solution)/shard_map/ppermute | solution.py:1213
  32.0 20.1 %collective-permute-start.5 = (bf16[4,304,384]{2,1,0:T(8,128)(2,1)}, bf16[4,304,384]{2,1,0:T(8,128)(2,1)}, u32[]{:S(2)}, u32[]{:S(2)}) collective-permute-start(bf16[4,304,384]{2,1,0:T(8,128)(2,1)} %get-tuple-element.271), channel_id=1, source_target_pairs={{0,16},{16,0},{1,17},{17,1},{2,18},{18,2},{3,19},{19,3},{4,20},{20... | collective-permute-start | bytes 2801672 | tf_op jit(solution)/shard_map/ppermute | solution.py:1213
  33.2 15.9 %collective-permute-start.6 = (bf16[864,384]{1,0:T(8,128)(2,1)}, bf16[864,384]{1,0:T(8,128)(2,1)}, u32[]{:S(2)}, u32[]{:S(2)}) collective-permute-start(bf16[864,384]{1,0:T(8,128)(2,1)} %pad_maximum_fusion.9), channel_id=1, source_target_pairs={{0,1},{1,2},{2,3},{3,0},{4,5},{5,6},{6,7},{7,4},{8,9},{9,10},{10,1... | collective-permute-start | bytes 1990664 | tf_op jit(solution)/shard_map/ppermute | solution.py:1200
  33.6 31.9 %collective-permute-start.9 = (bf16[864,384]{1,0:T(8,128)(2,1)}, bf16[864,384]{1,0:T(8,128)(2,1)}, u32[]{:S(2)}, u32[]{:S(2)}) collective-permute-start(bf16[864,384]{1,0:T(8,128)(2,1)} %pad_maximum_fusion.9), channel_id=1, source_target_pairs={{0,3},{1,0},{2,1},{3,2},{4,7},{5,4},{6,5},{7,6},{8,11},{9,8},{10,9... | collective-permute-start | bytes 1990664 | tf_op jit(solution)/shard_map/ppermute | solution.py:1200
  61.5 26.7 %collective-permute-start.11 = (bf16[864,384]{1,0:T(8,128)(2,1)}, bf16[864,384]{1,0:T(8,128)(2,1)S(1)}, u32[]{:S(2)}, u32[]{:S(2)}) collective-permute-start(bf16[864,384]{1,0:T(8,128)(2,1)} %collective-permute-done.6), channel_id=1, source_target_pairs={{0,16},{16,0},{1,17},{17,1},{2,18},{18,2},{3,19},{19,3},{4,20},{20... | collective-permute-start | bytes 1990664 | tf_op jit(solution)/shard_map/ppermute | solution.py:1213
  65.5 30.2 %collective-permute-start.12 = (bf16[864,384]{1,0:T(8,128)(2,1)}, bf16[864,384]{1,0:T(8,128)(2,1)S(1)}, u32[]{:S(2)}, u32[]{:S(2)}) collective-permute-start(bf16[864,384]{1,0:T(8,128)(2,1)} %collective-permute-done.9), channel_id=1, source_target_pairs={{0,16},{16,0},{1,17},{17,1},{2,18},{18,2},{3,19},{19,3},{4,20},{20... | collective-permute-start | bytes 1990664 | tf_op jit(solution)/shard_map/ppermute | solution.py:1213
  70.4 25.3 %collective-permute-start.13 = (bf16[480,384]{1,0:T(8,128)(2,1)S(1)}, bf16[480,384]{1,0:T(8,128)(2,1)S(1)}, u32[]{:S(2)}, u32[]{:S(2)}) collective-permute-start(bf16[480,384]{1,0:T(8,128)(2,1)S(1)} %slice.277), channel_id=1, source_target_pairs={{0,2},{1,3},{2,0},{3,1},{4,6},{5,7},{6,4},{7,5},{8,10},{9,11},{10,... | collective-permute-start | bytes 1105928 | tf_op jit(solution)/shard_map/ppermute | solution.py:1200
  70.5 32.9 %collective-permute-start.15 = (bf16[384,384]{1,0:T(8,128)(2,1)S(1)}, bf16[384,384]{1,0:T(8,128)(2,1)S(1)}, u32[]{:S(2)}, u32[]{:S(2)}) collective-permute-start(bf16[384,384]{1,0:T(8,128)(2,1)S(1)} %slice.278), channel_id=1, source_target_pairs={{0,2},{1,3},{2,0},{3,1},{4,6},{5,7},{6,4},{7,5},{8,10},{9,11},{10,... | collective-permute-start | bytes 884744 | tf_op jit(solution)/shard_map/ppermute | solution.py:1200
  79.9 45.6 %collective-permute-start.20 = (bf16[2,256,768]{2,1,0:T(8,128)(2,1)S(1)}, bf16[2,256,768]{2,1,0:T(8,128)(2,1)S(1)}, u32[]{:S(2)}, u32[]{:S(2)}) collective-permute-start(bf16[2,256,768]{2,1,0:T(8,128)(2,1)S(1)} %pad_maximum_fusion.5.g_ref), channel_id=1, source_target_pairs={{0,4},{4,0},{8,12},{12,8},{1,5},{5,1},{9,13},{13,9},{2,6},{6,2},{1... | collective-permute-start | bytes 2359304 | tf_op jit(solution)/shard_map/ppermute | solution.py:1166
  129.4 16.6 %collective-permute-start.22 = (bf16[384,768]{1,0:T(8,128)(2,1)S(1)}, bf16[384,768]{1,0:T(8,128)(2,1)S(1)}, u32[]{:S(2)}, u32[]{:S(2)}) collective-permute-start(bf16[384,768]{1,0:T(8,128)(2,1)S(1)} %get-tuple-element.181.one), channel_id=1, source_target_pairs={{0,1},{1,2},{2,3},{3,0},{4,5},{5,6},{6,7},{7,4},{8,9},{9,10},{10,1... | collective-permute-start | bytes 1769480 | tf_op jit(solution)/shard_map/ppermute | solution.py:1200
  144.7 29.8 %collective-permute-start.26 = (bf16[384,768]{1,0:T(8,128)(2,1)S(1)}, bf16[384,768]{1,0:T(8,128)(2,1)S(1)}, u32[]{:S(2)}, u32[]{:S(2)}) collective-permute-start(bf16[384,768]{1,0:T(8,128)(2,1)S(1)} %get-tuple-element.181.one), channel_id=1, source_target_pairs={{0,2},{1,3},{2,0},{3,1},{4,6},{5,7},{6,4},{7,5},{8,10},{9,11},{10,... | collective-permute-start | bytes 1769480 | tf_op jit(solution)/shard_map/ppermute | solution.py:1200
  146.0 28.5 %collective-permute-start.24 = (bf16[2,4,192,384]{3,2,1,0:T(8,128)(2,1)S(1)}, bf16[2,4,192,384]{3,2,1,0:T(8,128)(2,1)S(1)}, u32[]{:S(2)}, u32[]{:S(2)}) collective-permute-start(bf16[2,4,192,384]{3,2,1,0:T(8,128)(2,1)S(1)} %get-tuple-element.195), channel_id=1, source_target_pairs={{0,8},{4,12},{8,0},{12,4},{1,9},{5,13},{9,1},{13,5},{2,10},{6,14},... | collective-permute-start | bytes 3538952 | tf_op jit(solution)/shard_map/ppermute | solution.py:1166
  147.2 27.3 %collective-permute-start.25 = (bf16[2,4,192,384]{3,2,1,0:T(8,128)(2,1)S(1)}, bf16[2,4,192,384]{3,2,1,0:T(8,128)(2,1)S(1)}, u32[]{:S(2)}, u32[]{:S(2)}) collective-permute-start(bf16[2,4,192,384]{3,2,1,0:T(8,128)(2,1)S(1)} %get-tuple-element.196), channel_id=1, source_target_pairs={{0,16},{16,0},{1,17},{17,1},{2,18},{18,2},{3,19},{19,3},{4,20},{20... | collective-permute-start | bytes 3538952 | tf_op jit(solution)/shard_map/ppermute | solution.py:1213
  183.2 15.1 %collective-permute-start.30 = (bf16[384,768]{1,0:T(8,128)(2,1)S(1)}, bf16[384,768]{1,0:T(8,128)(2,1)S(1)}, u32[]{:S(2)}, u32[]{:S(2)}) collective-permute-start(bf16[384,768]{1,0:T(8,128)(2,1)S(1)} %get-tuple-element.181.one), channel_id=1, source_target_pairs={{0,3},{1,0},{2,1},{3,2},{4,7},{5,4},{6,5},{7,6},{8,11},{9,8},{10,9... | collective-permute-start | bytes 1769480 | tf_op jit(solution)/shard_map/ppermute | solution.py:1200
  184.2 15.1 %collective-permute-start.29 = (bf16[4,192,384]{2,1,0:T(8,128)(2,1)}, bf16[4,192,384]{2,1,0:T(8,128)(2,1)}, u32[]{:S(2)}, u32[]{:S(2)}) collective-permute-start(bf16[4,192,384]{2,1,0:T(8,128)(2,1)} %fusion.10), channel_id=1, source_target_pairs={{0,8},{4,12},{8,0},{12,4},{1,9},{5,13},{9,1},{13,5},{2,10},{6,14},... | collective-permute-start | bytes 1769480 | tf_op jit(solution)/shard_map/ppermute | solution.py:1166
  186.4 32.8 %collective-permute-start.32 = (bf16[128,768]{1,0:T(8,128)(2,1)}, bf16[128,768]{1,0:T(8,128)(2,1)S(1)}, u32[]{:S(2)}, u32[]{:S(2)}) collective-permute-start(bf16[128,768]{1,0:T(8,128)(2,1)} %copy-done.17), channel_id=1, source_target_pairs={{4,5},{1,0},{5,13},{9,1},{13,12},{8,9},{6,7},{3,2},{7,15},{11,3},{... | collective-permute-start | bytes 589832 | tf_op jit(solution)/shard_map/ppermute | solution.py:1472
  191.7 28.8 %collective-permute-start.31 = (bf16[384,768]{1,0:T(8,128)(2,1)S(1)}, bf16[384,768]{1,0:T(8,128)(2,1)S(1)}, u32[]{:S(2)}, u32[]{:S(2)}) collective-permute-start(bf16[384,768]{1,0:T(8,128)(2,1)S(1)} %add_convert_fusion.7), channel_id=1, source_target_pairs={{4,1},{1,4},{5,9},{9,5},{13,8},{8,13},{6,3},{3,6},{7,11},{11,7},{1... | collective-permute-start | bytes 1769480 | tf_op jit(solution)/shard_map/ppermute | solution.py:1471
  221.4 18.9 %collective-permute-start.38 = (bf16[2,2,4,200,384]{4,3,2,1,0:T(8,128)(2,1)}, bf16[2,2,4,200,384]{4,3,2,1,0:T(8,128)(2,1)}, u32[]{:S(2)}, u32[]{:S(2)}) collective-permute-start(bf16[2,2,4,200,384]{4,3,2,1,0:T(8,128)(2,1)} %get-tuple-element.224), channel_id=1, source_target_pairs={{0,4},{4,0},{8,12},{12,8},{1,5},{5,1},{9,13},{13,9},{2,6},{6,2},{1... | collective-permute-start | bytes 7372808 | tf_op jit(solution)/shard_map/ppermute | solution.py:1166
  223.4 16.1 %collective-permute-start.39 = (bf16[384,384]{1,0:T(8,128)(2,1)S(1)}, bf16[384,384]{1,0:T(8,128)(2,1)S(1)}, u32[]{:S(2)}, u32[]{:S(2)}) collective-permute-start(bf16[384,384]{1,0:T(8,128)(2,1)S(1)} %copy-done.47), channel_id=1, source_target_pairs={{0,2},{1,3},{2,0},{3,1},{4,6},{5,7},{6,4},{7,5},{8,10},{9,11},{10,... | collective-permute-start | bytes 884744 | tf_op jit(solution)/shard_map/ppermute | solution.py:1225
  242.5 28.5 %collective-permute-start.40 = (bf16[2,4,200,384]{3,2,1,0:T(8,128)(2,1)S(1)}, bf16[2,4,200,384]{3,2,1,0:T(8,128)(2,1)S(1)}, u32[]{:S(2)}, u32[]{:S(2)}) collective-permute-start(bf16[2,4,200,384]{3,2,1,0:T(8,128)(2,1)S(1)} %get-tuple-element.259), channel_id=1, source_target_pairs={{0,16},{16,0},{1,17},{17,1},{2,18},{18,2},{3,19},{19,3},{4,20},{20... | collective-permute-start | bytes 3686408 | tf_op jit(solution)/shard_map/ppermute | solution.py:1213
  243.7 15.7 %collective-permute-start.41 = (bf16[384,768]{1,0:T(8,128)(2,1)S(1)}, bf16[384,768]{1,0:T(8,128)(2,1)S(1)}, u32[]{:S(2)}, u32[]{:S(2)}) collective-permute-start(bf16[384,768]{1,0:T(8,128)(2,1)S(1)} %pad_maximum_fusion.11.one), channel_id=1, source_target_pairs={{0,1},{1,2},{2,3},{3,0},{4,5},{5,6},{6,7},{7,4},{8,9},{9,10},{10,1... | collective-permute-start | bytes 1769480 | tf_op jit(solution)/shard_map/ppermute | solution.py:1200
  243.8 26.4 %collective-permute-start.42 = (bf16[384,768]{1,0:T(8,128)(2,1)S(1)}, bf16[384,768]{1,0:T(8,128)(2,1)S(1)}, u32[]{:S(2)}, u32[]{:S(2)}) collective-permute-start(bf16[384,768]{1,0:T(8,128)(2,1)S(1)} %pad_maximum_fusion.11.one), channel_id=1, source_target_pairs={{0,3},{1,0},{2,1},{3,2},{4,7},{5,4},{6,5},{7,6},{8,11},{9,8},{10,9... | collective-permute-start | bytes 1769480 | tf_op jit(solution)/shard_map/ppermute | solution.py:1200
  248.0 29.3 %collective-permute-start.45 = (bf16[4,128,768]{2,1,0:T(8,128)(2,1)}, bf16[4,128,768]{2,1,0:T(8,128)(2,1)}, u32[]{:S(2)}, u32[]{:S(2)}) collective-permute-start(bf16[4,128,768]{2,1,0:T(8,128)(2,1)} %pad_maximum_fusion.7), channel_id=1, source_target_pairs={{0,4},{4,0},{8,12},{12,8},{1,5},{5,1},{9,13},{13,9},{2,6},{6,2},{1... | collective-permute-start | bytes 2359304 | tf_op jit(solution)/shard_map/ppermute | solution.py:1166
  250.7 26.6 %collective-permute-start.44 = (bf16[2,256,768]{2,1,0:T(8,128)(2,1)}, bf16[2,256,768]{2,1,0:T(8,128)(2,1)}, u32[]{:S(2)}, u32[]{:S(2)}) collective-permute-start(bf16[2,256,768]{2,1,0:T(8,128)(2,1)} %pad_maximum_fusion.6), channel_id=1, source_target_pairs={{0,12},{4,8},{8,4},{12,0},{1,13},{5,9},{9,5},{13,1},{2,14},{6,10},... | collective-permute-start | bytes 2359304 | tf_op jit(solution)/shard_map/ppermute | solution.py:1512
  273.6 27.9 %collective-permute-start.46 = (bf16[384,768]{1,0:T(8,128)(2,1)S(1)}, bf16[384,768]{1,0:T(8,128)(2,1)S(1)}, u32[]{:S(2)}, u32[]{:S(2)}) collective-permute-start(bf16[384,768]{1,0:T(8,128)(2,1)S(1)} %pad_maximum_fusion.11.one), channel_id=1, source_target_pairs={{0,2},{1,3},{2,0},{3,1},{4,6},{5,7},{6,4},{7,5},{8,10},{9,11},{10,... | collective-permute-start | bytes 1769480 | tf_op jit(solution)/shard_map/ppermute | solution.py:1200
  277.0 16.0 %collective-permute-start.48 = (bf16[384,384]{1,0:T(8,128)(2,1)S(1)}, bf16[384,384]{1,0:T(8,128)(2,1)S(1)}, u32[]{:S(2)}, u32[]{:S(2)}) collective-permute-start(bf16[384,384]{1,0:T(8,128)(2,1)S(1)} %fusion.15.mine), channel_id=1, source_target_pairs={{0,8},{4,12},{8,0},{12,4},{1,9},{5,13},{9,1},{13,5},{2,10},{6,14},... | collective-permute-start | bytes 884744 | tf_op jit(solution)/shard_map/ppermute | solution.py:1166
  287.5 17.3 %collective-permute-start.47 = (bf16[200,384]{1,0:T(8,128)(2,1)S(1)}, bf16[200,384]{1,0:T(8,128)(2,1)S(1)}, u32[]{:S(2)}, u32[]{:S(2)}) collective-permute-start(bf16[200,384]{1,0:T(8,128)(2,1)S(1)} %get-tuple-element.274), channel_id=1, source_target_pairs={{0,3},{1,0},{2,1},{3,2},{4,7},{5,4},{6,5},{7,6},{8,11},{9,8},{10,9... | collective-permute-start | bytes 460808 | tf_op jit(solution)/shard_map/ppermute | solution.py:1225
  304.9 16.8 %collective-permute-start.52 = (bf16[4,128,768]{2,1,0:T(8,128)(2,1)S(1)}, bf16[4,128,768]{2,1,0:T(8,128)(2,1)S(1)}, u32[]{:S(2)}, u32[]{:S(2)}) collective-permute-start(bf16[4,128,768]{2,1,0:T(8,128)(2,1)S(1)} %pad_maximum_fusion.8), channel_id=1, source_target_pairs={{0,4},{4,0},{8,12},{12,8},{1,5},{5,1},{9,13},{13,9},{2,6},{6,2},{1... | collective-permute-start | bytes 2359304 | tf_op jit(solution)/shard_map/ppermute | solution.py:1166
  (85 other events, 691.0 us)

commit v2 on v1

--- a/solution.py
+++ b/solution.py
@@ -344,8 +344,10 @@
     l_ref[0] = jnp.concatenate(logs, axis=1)
 
 
-def attend_back_kernel(span, q_ref, k_ref, v_ref, kd_ref, qd_ref, do_ref, l_ref, *refs):
-    dq_ref, dk_ref, dv_ref, dk_acc, dv_acc = refs[-5:]
+def attend_back_kernel(
+    span, short, plan_ref, q_ref, k_ref, v_ref, kd_ref, qd_ref, do_ref, l_ref, *refs
+):
+    dq_ref, dk_ref, dv_ref, dk_acc, dv_acc = refs
     step = pl.program_id(1)
 
     @pl.when(step == 0)
@@ -353,14 +355,11 @@
         dk_acc[...] = jnp.zeros_like(dk_acc)
         dv_acc[...] = jnp.zeros_like(dv_acc)
 
-    here = pl.ds(pl.multiple_of(step * QBLOCK, QBLOCK), span)
-    same = qd_ref[:, :1] == kd_ref[:, here]
     logs = l_ref[0]
-    for pair in range(q_ref.shape[1] // PAIR):
-        cols = slice(pair * PAIR, (pair + 1) * PAIR)
+
+    def one_pair(here, same, cols, log):
         keys = k_ref[here, cols]
         queries, grads = stack_heads(q_ref[:, cols]), stack_heads(do_ref[:, cols])
-        log = jnp.concatenate([logs[:, 2 * pair + i : 2 * pair + i + 1] for i in (0, 1)], axis=0)
         probs = jnp.exp(masked_scores(queries, keys, same) - log)
         grad_probs = contract_last(grads, v_ref[here, cols])
         inner = jnp.sum(grad_probs * probs, axis=1, keepdims=True)
@@ -370,6 +369,34 @@
         dk_acc[here, cols] += contract_rows(grad_scores, queries)
         dv_acc[here, cols] += contract_rows(probs.astype(jnp.bfloat16), grads)
 
+    pairs = q_ref.shape[1] // PAIR
+    fits = plan_ref[1, step] == 1
+
+    @pl.when(fits)
+    def _():
+        here = pl.ds(pl.multiple_of(plan_ref[0, step], QBLOCK), short)
+        same = qd_ref[:, :1] == kd_ref[:, here]
+        for pair in range(pairs):
+            log = [logs[:, 2 * pair + i : 2 * pair + i + 1] for i in (0, 1)]
+            one_pair(
+                here, same, slice(pair * PAIR, (pair + 1) * PAIR), jnp.concatenate(log, axis=0)
+            )
+
+    @pl.when(jnp.logical_not(fits))
+    def _():
+        here = pl.ds(pl.multiple_of(step * QBLOCK, QBLOCK), span)
+        same = qd_ref[:, :1] == kd_ref[:, here]
+        lane = lax.broadcasted_iota(jnp.int32, logs.shape, 1)
+
+        @pl.loop(0, pairs)
+        def _(pair):
+            log = [
+                jnp.sum(jnp.where(lane == 2 * pair + i, logs, 0.0), axis=1, keepdims=True)
+                for i in (0, 1)
+            ]
+            cols = pl.ds(pl.multiple_of(pair * PAIR, PAIR), PAIR)
+            one_pair(here, same, cols, jnp.concatenate(log, axis=0))
+
     @pl.when(step == pl.num_programs(1) - 1)
     def _():
         dk_ref[...] = dk_acc[...].astype(jnp.bfloat16)
@@ -377,11 +404,11 @@
 
 
 def attention_specs(window, cols, at):
-    rows = pl.BlockSpec((QBLOCK, cols), lambda h, i: (i, at + h))
-    keys = pl.BlockSpec((window, cols), lambda h, i: (0, at + h))
-    key_docs = pl.BlockSpec((1, window), lambda h, i: (0, 0))
-    query_docs = pl.BlockSpec((QBLOCK, QBLOCK), lambda h, i: (i, 0))
-    logs = pl.BlockSpec((1, QBLOCK, cols // HEAD_DIM), lambda h, i: (at + h, i, 0))
+    rows = pl.BlockSpec((QBLOCK, cols), lambda h, i, *_: (i, at + h))
+    keys = pl.BlockSpec((window, cols), lambda h, i, *_: (0, at + h))
+    key_docs = pl.BlockSpec((1, window), lambda h, i, *_: (0, 0))
+    query_docs = pl.BlockSpec((QBLOCK, QBLOCK), lambda h, i, *_: (i, 0))
+    logs = pl.BlockSpec((1, QBLOCK, cols // HEAD_DIM), lambda h, i, *_: (at + h, i, 0))
     return rows, keys, key_docs, query_docs, logs
 
 
@@ -409,28 +436,45 @@
     )(queries, keys, values, key_docs, query_docs, *prior)
 
 
-def attend_back(queries, keys, values, key_docs, query_docs, reach, grads, logs_in):
+def attend_back(plan, queries, keys, values, key_docs, query_docs, reach, grads, logs_in):
     count, width = queries.shape
     window, cols = keys.shape[0], width // 2
     span = QBLOCK + 2 * reach
     rows, key_spec, kd_spec, qd_spec, logs = attention_specs(window, cols, 0)
     return pl.pallas_call(
-        partial(attend_back_kernel, span),
-        grid=(2, count // QBLOCK),
-        in_specs=[rows, key_spec, key_spec, kd_spec, qd_spec, rows, logs],
-        out_specs=[rows, key_spec, key_spec],
+        partial(attend_back_kernel, span, short_span(reach)),
+        grid_spec=pltpu.PrefetchScalarGridSpec(
+            num_scalar_prefetch=1,
+            grid=(2, count // QBLOCK),
+            in_specs=[rows, key_spec, key_spec, kd_spec, qd_spec, rows, logs],
+            out_specs=[rows, key_spec, key_spec],
+            scratch_shapes=[pltpu.VMEM((window, cols), jnp.float32)] * 2,
+        ),
         out_shape=[
             jax.ShapeDtypeStruct((count, width), jnp.bfloat16),
             jax.ShapeDtypeStruct((window, width), jnp.bfloat16),
             jax.ShapeDtypeStruct((window, width), jnp.bfloat16),
         ],
-        scratch_shapes=[pltpu.VMEM((window, cols), jnp.float32)] * 2,
         compiler_params=pltpu.CompilerParams(vmem_limit_bytes=24 << 20),
         cost_estimate=pl.CostEstimate(
             flops=40 * count * span * width, bytes_accessed=12 << 20, transcendentals=0
         ),
         name="attend_back",
-    )(queries, keys, values, key_docs, query_docs, grads, logs_in)
+    )(plan, queries, keys, values, key_docs, query_docs, grads, logs_in)
+
+
+def short_span(reach):
+    return (QBLOCK + 2 * reach) * 2 // 3 // QBLOCK * QBLOCK
+
+
+def key_plan(docs, reach, count):
+    window, short = docs.shape[0], short_span(reach)
+    rows = docs[reach : reach + count].reshape(-1, QBLOCK)
+    at = jnp.arange(window, dtype=jnp.int32)
+    low = jnp.min(jnp.where(docs == rows[:, :1], at, window), axis=1)
+    high = jnp.max(jnp.where(docs == rows[:, -1:], at + 1, 0), axis=1)
+    start = jnp.minimum(low // QBLOCK * QBLOCK, window - short)
+    return jnp.stack([start, (high - start <= short).astype(jnp.int32)])
 
 
 def half_cols(position, half):
@@ -1358,7 +1402,9 @@
     mixed, far_one, far_three, some_two = tie(mixed, far_one, far_three, some_two)
     far_some_two = shard_swap(some_two)
     mixed, logs = attend(*attention, 1, (mixed, logs))
-    mixed, far_some_two, up_two = tie(mixed, far_some_two, up_two)
+    mixed, far_some_two, up_two, plan = tie(
+        mixed, far_some_two, up_two, key_plan(window_docs, reach, count)
+    )
     far_up_two = shard_swap(up_two)
     out_mine = jnp.stack(
         [
@@ -1442,14 +1488,14 @@
     )
     up_got = across_swap(up_give)
     down_got = shard_swap(down_give)
-    grad_scaled, grad_keys, grad_values = attend_back(*attention, grad_mixed, logs)
-    grad_keys, up_got, down_got, out_pieces[2] = tie(grad_keys, up_got, down_got, out_pieces[2])
+    grad_scaled, grad_keys, grad_values = attend_back(plan, *attention, grad_mixed, logs)
+    own_sum, first, second, give = span_grads(
+        place, grad_scaled, grad_keys, grad_values, weights_t, grad_one
+    )
+    first, up_got, down_got, out_pieces[2] = tie(first, up_got, down_got, out_pieces[2])
     up_parts = [low_sum(up_keep[i], up_got[i]) for i in (0, 1)]
     down_parts = [low_sum(down_keep[i], down_got[i]) for i in (0, 1)]
     up_got, down_got = shard_swap(up_parts[1]), across_swap(down_parts[1])
-    own_sum, first, second, give = span_grads(
-        place, grad_scaled, grad_keys, grad_values, weights_t, grad_one
-    )
     got = core_swap(give)
     shared = reach - count
     to_own = lax.dynamic_slice_in_dim(got, (1 - core) * shared, count, 0)

time: 336 us -> 332 us (0.988)
  starting transfers between devices: 73.2 us -> 68.9 us
    unnamed x119 -> x121, local copies, waits for them, and re-layouts: 9.87 us -> 12.2 us
  transfers between devices with their start and end apart: 57 -> 57, of which waited for: 25 -> 24; matrix products, arithmetic and copies ran while one was open for 15% -> 14% of each run, Pallas kernels for 26% -> 28%
where the time goes in v2:
time: 332 us; the launch traced here: 328 us
  waiting for transfers between devices  95.7 us (29%)
  Pallas kernels  94.8 us (29%)
  starting transfers between devices  68.9 us (21%)
  other arithmetic  35.2 us (11%)
  local copies, waits for them, and re-layouts  30.9 us (9%)
    ppermute x13, waiting for transfers between devices, tp_shifts(): lax.ppermute(array[cut], 'tp', [(i, (i + shift) % 4) for i in range(4)])  45.4 us
    ppermute x6, waiting for transfers between devices, scatter_tp_start(): lax.ppermute(sent, 'tp', [(i, (i + shift) % 4) for i in range(4)])  22.4 us
    pallas_call x1, Pallas kernels, attend_back(): pl.pallas_call(partial(attend_back_kernel, span, short_span(reach)), grid...  21 us
    ppermute x23, starting transfers between devices, ctx_swap(): return lax.ppermute(array, 'ctx', [(i, i ^ bit) for i in range(4)])  20.7 us
    ppermute x13, starting transfers between devices, tp_shifts(): lax.ppermute(array[cut], 'tp', [(i, (i + shift) % 4) for i in range(4)])  16.6 us
    ppermute x23, waiting for transfers between devices, ctx_swap(): return lax.ppermute(array, 'ctx', [(i, i ^ bit) for i in range(4)])  15.6 us
    pallas_call x1, Pallas kernels, ffn_back(): pl.pallas_call(ffn_back_kernel, grid_spec=pltpu.PrefetchScalarGridSpec(nu...  13.2 us
    pallas_call x2, Pallas kernels, attend(): pl.pallas_call(partial(attend_kernel, span), grid=(1, count // QBLOCK), i...  13.1 us
  transfers between devices with their start and end apart: 57, of which 24 were waited for; matrix products, arithmetic and copies ran while one was open for 14% of the time, Pallas kernels for 28%

profile of v2, /device:TPU:1, one launch (start us, length us, event | category | flops | bytes accessed | tf_op | source)
XLA Modules:
  0.0 327.7 jit_solution(9885650613359088912)
XLA Ops:
  9.7 2.7 dynamic-slice_bitcast_fusion
  24.9 4.7 %collective-permute-done.4 = bf16[864,384]{1,0:T(8,128)(2,1)} collective-permute-done((bf16[864,384]{1,0:T(8,128)(2,1)}, bf16[864,384]{1,0:T(8,128)(2,1)}, u32[]{:S(2)}, u32[]{:S(2)}) %collective-permute-start.4) | collective-permute-done | bytes 663584 | tf_op jit(solution)/shard_map/ppermute | solution.py:1257
  35.1 2.9 collective-permute-start.9
  38.7 3.1 collective-permute-start.7
  46.9 3.8 %collective-permute-done.6 = bf16[864,384]{1,0:T(8,128)(2,1)} collective-permute-done((bf16[864,384]{1,0:T(8,128)(2,1)}, bf16[864,384]{1,0:T(8,128)(2,1)}, u32[]{:S(2)}, u32[]{:S(2)}) %collective-permute-start.6) | collective-permute-done | bytes 663584 | tf_op jit(solution)/shard_map/ppermute | solution.py:1244
  50.7 2.9 collective-permute-done.5
  55.1 3.7 %collective-permute-start.8 = (bf16[2,4,304,384]{3,2,1,0:T(8,128)(2,1)S(1)}, bf16[2,4,304,384]{3,2,1,0:T(8,128)(2,1)}, u32[]{:S(2)}, u32[]{:S(2)}) collective-permute-start(bf16[2,4,304,384]{3,2,1,0:T(8,128)(2,1)S(1)} %pad_maximum_fusion.1.w_mine), channel_id=1, source_target_pairs={{0,4},{4,0},{8,12},{12,8},{1,5},{5,1},{9,13},{13,9},{2,6},{6,2},{1... | collective-permute-start | bytes 5603336 | tf_op jit(solution)/shard_map/ppermute | solution.py:1210
  73.2 7.0 %project.1 = (bf16[384,768]{1,0:T(8,128)(2,1)S(1)}, bf16[1408,768]{1,0:T(8,128)(2,1)S(1)}, bf16[1408,768]{1,0:T(8,128)(2,1)S(1)}, bf16[1408,768]{1,0:T(8,128)(2,1)S(1)}, bf16[3,768,768]{2,1,0:T(8,128)(2,1)S(1)}) custom-call(s32[5]{0:T(128)S(1)} %stack.258.place_ref, bf16[2,4,304,384]{3,2,1,0:T(8,128)(2,1)S(1)} %pad_maximum_fusion.1.w_mine, ...), custom_call_target="tpu_custom_call" | custom-call | flops 3321888768 | bytes 16777216 | tf_op jit(solution)/shard_map/project/pallas_call | solution.py:743
  82.0 6.5 %attend.2 = (bf16[384,768]{1,0:T(8,128)(2,1)S(1)}, f32[2,384,6]{2,1,0:T(8,128)S(1)}) custom-call(bf16[384,768]{1,0:T(8,128)(2,1)S(1)} %get-tuple-element.154.q_ref, bf16[1408,768]{1,0:T(8,128)(2,1)S(1)} %get-tuple-element.155.k_ref, bf16[1408,768]{1,0:T(8,128)(2,1)S(1)} %get-tuple-element.156.v_ref, s32[1,1408]{1,0:T(1,128)S(1)} %broadcast_in_dim.34.kd_ref, ...), custom_call_target="tpu_custom_call" | custom-call | flops 2717908992 | bytes 4194304 | tf_op jit(solution)/shard_map/attend/pallas_call | solution.py:420
  88.6 7.6 %collective-permute-done.13 = bf16[480,384]{1,0:T(8,128)(2,1)S(1)} collective-permute-done((bf16[480,384]{1,0:T(8,128)(2,1)S(1)}, bf16[480,384]{1,0:T(8,128)(2,1)S(1)}, u32[]{:S(2)}, u32[]{:S(2)}) %collective-permute-start.13) | collective-permute-done | bytes 368672 | tf_op jit(solution)/shard_map/ppermute | solution.py:1244
  97.3 6.5 %attend.3 = (bf16[384,768]{1,0:T(8,128)(2,1)S(1)}, f32[2,384,6]{2,1,0:T(8,128)S(1)}) custom-call(bf16[384,768]{1,0:T(8,128)(2,1)S(1)} %get-tuple-element.154.q_ref, bf16[1408,768]{1,0:T(8,128)(2,1)S(1)} %get-tuple-element.155.k_ref, bf16[1408,768]{1,0:T(8,128)(2,1)S(1)} %get-tuple-element.156.v_ref, ...), custom_call_target="tpu_custom_call", output_to_operand_aliasing={{0}: (5, {}), {1}: (6, {})} | custom-call | flops 2717908992 | bytes 4194304 | tf_op jit(solution)/shard_map/attend/pallas_call | solution.py:420
  114.6 7.0 %ffn.2 = (bf16[768,1536]{1,0:T(8,128)(2,1)S(1)}, bf16[768,1536]{1,0:T(8,128)(2,1)S(1)}, f32[768,768]{1,0:T(8,128)S(1)}) custom-call(s32[5]{0:T(128)S(1)} %stack.258.place_ref, bf16[384,768]{1,0:T(8,128)(2,1)S(1)} %get-tuple-element.170.h_ref, bf16[384,768]{1,0:T(8,128)(2,1)S(1)} %collective-permute-done.17.other_h_ref, ...), custom_call_target="tpu_custom_call" | custom-call | flops 8153726976 | bytes 9437184 | tf_op jit(solution)/shard_map/ffn/pallas_call | solution.py:639
  122.1 2.5 ffn.3
  131.5 13.2 %ffn_back.1 = (bf16[384,768]{1,0:T(8,128)(2,1)S(1)}, bf16[384,768]{1,0:T(8,128)(2,1)S(1)}, bf16[2,4,192,384]{3,2,1,0:T(8,128)(2,1)S(1)}, bf16[2,4,192,384]{3,2,1...) custom-call(s32[5]{0:T(128)S(1)} %stack.258.place_ref, ...), custom_call_target="tpu_custom_call" | custom-call | flops 10871635968 | bytes 20971520 | tf_op jit(solution)/shard_map/ffn_back/pallas_call | solution.py:661
  151.5 21.0 %attend_back.1 = (bf16[384,768]{1,0:T(8,128)(2,1)S(1)}, bf16[1408,768]{1,0:T(8,128)(2,1)S(1)}, bf16[1408,768]{1,0:T(8,128)(2,1)S(1)}) custom-call(s32[2,3]{1,0:T(2,128)S(1)} %pad_add_fusion.plan_ref, bf16[384,768]{1,0:T(8,128)(2,1)S(1)} %get-tuple-element.154.q_ref, bf16[1408,768]{1,0:T(8,128)(2,1)S(1)} %get-tuple-element.155.k_ref, ...), custom_call_target="tpu_custom_call" | custom-call | flops 13589544960 | bytes 12582912 | tf_op jit(solution)/shard_map/attend_back/pallas_call | solution.py:444
  172.6 6.3 %span_grads.1 = (f32[384,768]{1,0:T(8,128)S(1)}, bf16[384,768]{1,0:T(8,128)(2,1)S(1)}, bf16[128,768]{1,0:T(8,128)(2,1)S(1)}, bf16[512,768]{1,0:T(8,128)(2,1)}) custom-call(s32[5]{0:T(128)S(1)} %stack.258.place_ref, bf16[384,768]{1,0:T(8,128)(2,1)S(1)} %get-tuple-element.196.dq_ref, bf16[1408,768]{1,0:T(8,128)(2,1)S(1)} %get-tuple-element.213.dk_ref, ...), custom_call_target="tpu_custom_call" | custom-call | flops 3321888768 | bytes 12582912 | tf_op jit(solution)/shard_map/span_grads/pallas_call | solution.py:1057
  182.0 3.8 %collective-permute-start.32 = (bf16[128,768]{1,0:T(8,128)(2,1)}, bf16[128,768]{1,0:T(8,128)(2,1)S(1)}, u32[]{:S(2)}, u32[]{:S(2)}) collective-permute-start(bf16[128,768]{1,0:T(8,128)(2,1)} %copy-done.17), channel_id=1, source_target_pairs={{4,5},{1,0},{5,13},{9,1},{13,12},{8,9},{6,7},{3,2},{7,15},{11,3},{... | collective-permute-start | bytes 589832 | tf_op jit(solution)/shard_map/ppermute | solution.py:1518
  188.0 2.9 collective-permute-start.31
  190.8 3.3 %collective-permute-done.30.four = bf16[384,768]{1,0:T(8,128)(2,1)S(1)} collective-permute-done((bf16[384,768]{1,0:T(8,128)(2,1)S(1)}, bf16[384,768]{1,0:T(8,128)(2,1)S(1)}, u32[]{:S(2)}, u32[]{:S(2)}) %collective-permute-start.30) | collective-permute-done | bytes 589856 | tf_op jit(solution)/shard_map/ppermute | solution.py:1244
  205.8 8.3 %attn_grads.1 = (bf16[2,2,4,200,384]{4,3,2,1,0:T(8,128)(2,1)S(1)}, bf16[2,2,4,200,384]{4,3,2,1,0:T(8,128)(2,1)}) custom-call(s32[5]{0:T(128)S(1)} %stack.258.place_ref, bf16[384,768]{1,0:T(8,128)(2,1)S(1)} %copy-done.25, bf16[1408,768]{1,0:T(8,128)(2,1)S(1)} %copy-done.21, bf16[1408,768]{1,0:T(8,128)(2,1)S(1)} %copy-done.23, ...), custom_call_target="tpu_custom_call" | custom-call | flops 4227858432 | bytes 16777216 | tf_op jit(solution)/shard_map/attn_grads/pallas_call | solution.py:982
  222.5 3.4 %collective-permute-start.36 = (bf16[128,768]{1,0:T(8,128)(2,1)S(1)}, bf16[128,768]{1,0:T(8,128)(2,1)S(1)}, u32[]{:S(2)}, u32[]{:S(2)}) collective-permute-start(bf16[128,768]{1,0:T(8,128)(2,1)S(1)} %get-tuple-element.285), channel_id=1, source_target_pairs={{4,8},{8,0},{1,9},{13,1},{6,10},{10,2},{3,11},{15,3},{20,24},{24,1... | collective-permute-start | bytes 589832 | tf_op jit(solution)/shard_map/ppermute | solution.py:1455
  227.9 8.4 %collective-permute-done.39 = bf16[384,384]{1,0:T(8,128)(2,1)S(1)} collective-permute-done((bf16[384,384]{1,0:T(8,128)(2,1)S(1)}, bf16[384,384]{1,0:T(8,128)(2,1)S(1)}, u32[]{:S(2)}, u32[]{:S(2)}) %collective-permute-start.39) | collective-permute-done | bytes 294944 | tf_op jit(solution)/shard_map/ppermute | solution.py:1269
  240.8 3.3 collective-permute-start.42
  248.2 8.6 %collective-permute-done.41.two = bf16[384,768]{1,0:T(8,128)(2,1)S(1)} collective-permute-done((bf16[384,768]{1,0:T(8,128)(2,1)S(1)}, bf16[384,768]{1,0:T(8,128)(2,1)S(1)}, u32[]{:S(2)}, u32[]{:S(2)}) %collective-permute-start.41) | collective-permute-done | bytes 589856 | tf_op jit(solution)/shard_map/ppermute | solution.py:1244
  256.9 10.8 %collective-permute-done.42.four = bf16[384,768]{1,0:T(8,128)(2,1)S(1)} collective-permute-done((bf16[384,768]{1,0:T(8,128)(2,1)S(1)}, bf16[384,768]{1,0:T(8,128)(2,1)S(1)}, u32[]{:S(2)}, u32[]{:S(2)}) %collective-permute-start.42) | collective-permute-done | bytes 589856 | tf_op jit(solution)/shard_map/ppermute | solution.py:1244
  274.8 9.0 %collective-permute-done.43 = bf16[4,200,384]{2,1,0:T(8,128)(2,1)} collective-permute-done((bf16[4,200,384]{2,1,0:T(8,128)(2,1)}, bf16[4,200,384]{2,1,0:T(8,128)(2,1)}, u32[]{:S(2)}, u32[]{:S(2)}) %collective-permute-start.43) | collective-permute-done | bytes 614432 | tf_op jit(solution)/shard_map/ppermute | solution.py:1210
  287.5 3.1 assemble.2
  290.6 9.2 %collective-permute-done.46.three = bf16[384,768]{1,0:T(8,128)(2,1)S(1)} collective-permute-done((bf16[384,768]{1,0:T(8,128)(2,1)S(1)}, bf16[384,768]{1,0:T(8,128)(2,1)S(1)}, u32[]{:S(2)}, u32[]{:S(2)}) %collective-permute-start.46) | collective-permute-done | bytes 589856 | tf_op jit(solution)/shard_map/ppermute | solution.py:1244
  299.7 3.2 collective-permute-done.47
  306.2 4.9 %collective-permute-done.49 = bf16[200,384]{1,0:T(8,128)(2,1)S(1)} collective-permute-done((bf16[200,384]{1,0:T(8,128)(2,1)S(1)}, bf16[200,384]{1,0:T(8,128)(2,1)S(1)}, u32[]{:S(2)}, u32[]{:S(2)}) %collective-permute-start.49) | collective-permute-done | bytes 153632 | tf_op jit(solution)/shard_map/ppermute | solution.py:1269
  311.1 5.8 %collective-permute-done.50 = bf16[200,384]{1,0:T(8,128)(2,1)S(1)} collective-permute-done((bf16[200,384]{1,0:T(8,128)(2,1)S(1)}, bf16[200,384]{1,0:T(8,128)(2,1)S(1)}, u32[]{:S(2)}, u32[]{:S(2)}) %collective-permute-start.50) | collective-permute-done | bytes 153632 | tf_op jit(solution)/shard_map/ppermute | solution.py:1269
  319.1 3.1 assemble.3
  (334 shorter events, 132.7 us)
Async XLA Ops:
  4.2 20.0 %collective-permute-start = (bf16[304,384]{1,0:T(8,128)(2,1)}, bf16[304,384]{1,0:T(8,128)(2,1)}, u32[]{:S(2)}, u32[]{:S(2)}) collective-permute-start(bf16[304,384]{1,0:T(8,128)(2,1)} %maximum_maximum_fusion), channel_id=1, source_target_pairs={{0,1},{1,2},{2,3},{3,0},{4,5},{5,6},{6,7},{7,4},{8,9},{9,10},{10,1... | collective-permute-start | bytes 700424 | tf_op jit(solution)/shard_map/ppermute | solution.py:1244
  6.3 18.5 %collective-permute-start.1 = (bf16[304,384]{1,0:T(8,128)(2,1)}, bf16[304,384]{1,0:T(8,128)(2,1)}, u32[]{:S(2)}, u32[]{:S(2)}) collective-permute-start(bf16[304,384]{1,0:T(8,128)(2,1)} %maximum_maximum_fusion), channel_id=1, source_target_pairs={{0,2},{1,3},{2,0},{3,1},{4,6},{5,7},{6,4},{7,5},{8,10},{9,11},{10,... | collective-permute-start | bytes 700424 | tf_op jit(solution)/shard_map/ppermute | solution.py:1244
  8.7 16.2 %collective-permute-start.2 = (bf16[304,384]{1,0:T(8,128)(2,1)}, bf16[304,384]{1,0:T(8,128)(2,1)}, u32[]{:S(2)}, u32[]{:S(2)}) collective-permute-start(bf16[304,384]{1,0:T(8,128)(2,1)} %maximum_maximum_fusion), channel_id=1, source_target_pairs={{0,3},{1,0},{2,1},{3,2},{4,7},{5,4},{6,5},{7,6},{8,11},{9,8},{10,9... | collective-permute-start | bytes 700424 | tf_op jit(solution)/shard_map/ppermute | solution.py:1244
  12.4 17.8 %collective-permute-start.3 = (bf16[2,256,768]{2,1,0:T(8,128)(2,1)}, bf16[2,256,768]{2,1,0:T(8,128)(2,1)S(1)}, u32[]{:S(2)}, u32[]{:S(2)}) collective-permute-start(bf16[2,256,768]{2,1,0:T(8,128)(2,1)} %get-tuple-element.268), channel_id=1, source_target_pairs={{0,8},{4,12},{8,0},{12,4},{1,9},{5,13},{9,1},{13,5},{2,10},{6,14},... | collective-permute-start | bytes 2359304 | tf_op jit(solution)/shard_map/ppermute | solution.py:1210
  14.7 14.9 %collective-permute-start.4 = (bf16[864,384]{1,0:T(8,128)(2,1)}, bf16[864,384]{1,0:T(8,128)(2,1)}, u32[]{:S(2)}, u32[]{:S(2)}) collective-permute-start(bf16[864,384]{1,0:T(8,128)(2,1)} %pad_maximum_fusion.9), channel_id=1, source_target_pairs={{0,16},{16,0},{1,17},{17,1},{2,18},{18,2},{3,19},{19,3},{4,20},{20... | collective-permute-start | bytes 1990664 | tf_op jit(solution)/shard_map/ppermute | solution.py:1257
  33.4 20.2 %collective-permute-start.5 = (bf16[4,304,384]{2,1,0:T(8,128)(2,1)}, bf16[4,304,384]{2,1,0:T(8,128)(2,1)}, u32[]{:S(2)}, u32[]{:S(2)}) collective-permute-start(bf16[4,304,384]{2,1,0:T(8,128)(2,1)} %get-tuple-element.277), channel_id=1, source_target_pairs={{0,16},{16,0},{1,17},{17,1},{2,18},{18,2},{3,19},{19,3},{4,20},{20... | collective-permute-start | bytes 2801672 | tf_op jit(solution)/shard_map/ppermute | solution.py:1257
  34.7 16.0 %collective-permute-start.6 = (bf16[864,384]{1,0:T(8,128)(2,1)}, bf16[864,384]{1,0:T(8,128)(2,1)}, u32[]{:S(2)}, u32[]{:S(2)}) collective-permute-start(bf16[864,384]{1,0:T(8,128)(2,1)} %pad_maximum_fusion.9), channel_id=1, source_target_pairs={{0,1},{1,2},{2,3},{3,0},{4,5},{5,6},{6,7},{7,4},{8,9},{9,10},{10,1... | collective-permute-start | bytes 1990664 | tf_op jit(solution)/shard_map/ppermute | solution.py:1244
  35.1 30.9 %collective-permute-start.9 = (bf16[864,384]{1,0:T(8,128)(2,1)}, bf16[864,384]{1,0:T(8,128)(2,1)}, u32[]{:S(2)}, u32[]{:S(2)}) collective-permute-start(bf16[864,384]{1,0:T(8,128)(2,1)} %pad_maximum_fusion.9), channel_id=1, source_target_pairs={{0,3},{1,0},{2,1},{3,2},{4,7},{5,4},{6,5},{7,6},{8,11},{9,8},{10,9... | collective-permute-start | bytes 1990664 | tf_op jit(solution)/shard_map/ppermute | solution.py:1244
  61.8 26.7 %collective-permute-start.11 = (bf16[864,384]{1,0:T(8,128)(2,1)}, bf16[864,384]{1,0:T(8,128)(2,1)S(1)}, u32[]{:S(2)}, u32[]{:S(2)}) collective-permute-start(bf16[864,384]{1,0:T(8,128)(2,1)} %collective-permute-done.6), channel_id=1, source_target_pairs={{0,16},{16,0},{1,17},{17,1},{2,18},{18,2},{3,19},{19,3},{4,20},{20... | collective-permute-start | bytes 1990664 | tf_op jit(solution)/shard_map/ppermute | solution.py:1257
  66.0 30.2 %collective-permute-start.12 = (bf16[864,384]{1,0:T(8,128)(2,1)}, bf16[864,384]{1,0:T(8,128)(2,1)S(1)}, u32[]{:S(2)}, u32[]{:S(2)}) collective-permute-start(bf16[864,384]{1,0:T(8,128)(2,1)} %collective-permute-done.9), channel_id=1, source_target_pairs={{0,16},{16,0},{1,17},{17,1},{2,18},{18,2},{3,19},{19,3},{4,20},{20... | collective-permute-start | bytes 1990664 | tf_op jit(solution)/shard_map/ppermute | solution.py:1257
  70.8 25.4 %collective-permute-start.13 = (bf16[480,384]{1,0:T(8,128)(2,1)S(1)}, bf16[480,384]{1,0:T(8,128)(2,1)S(1)}, u32[]{:S(2)}, u32[]{:S(2)}) collective-permute-start(bf16[480,384]{1,0:T(8,128)(2,1)S(1)} %slice.294), channel_id=1, source_target_pairs={{0,2},{1,3},{2,0},{3,1},{4,6},{5,7},{6,4},{7,5},{8,10},{9,11},{10,... | collective-permute-start | bytes 1105928 | tf_op jit(solution)/shard_map/ppermute | solution.py:1244
  70.8 33.0 %collective-permute-start.15 = (bf16[384,384]{1,0:T(8,128)(2,1)S(1)}, bf16[384,384]{1,0:T(8,128)(2,1)S(1)}, u32[]{:S(2)}, u32[]{:S(2)}) collective-permute-start(bf16[384,384]{1,0:T(8,128)(2,1)S(1)} %slice.295), channel_id=1, source_target_pairs={{0,2},{1,3},{2,0},{3,1},{4,6},{5,7},{6,4},{7,5},{8,10},{9,11},{10,... | collective-permute-start | bytes 884744 | tf_op jit(solution)/shard_map/ppermute | solution.py:1244
  80.2 45.7 %collective-permute-start.20 = (bf16[2,256,768]{2,1,0:T(8,128)(2,1)S(1)}, bf16[2,256,768]{2,1,0:T(8,128)(2,1)S(1)}, u32[]{:S(2)}, u32[]{:S(2)}) collective-permute-start(bf16[2,256,768]{2,1,0:T(8,128)(2,1)S(1)} %pad_maximum_fusion.5.g_ref), channel_id=1, source_target_pairs={{0,4},{4,0},{8,12},{12,8},{1,5},{5,1},{9,13},{13,9},{2,6},{6,2},{1... | collective-permute-start | bytes 2359304 | tf_op jit(solution)/shard_map/ppermute | solution.py:1210
  129.9 16.6 %collective-permute-start.22 = (bf16[384,768]{1,0:T(8,128)(2,1)S(1)}, bf16[384,768]{1,0:T(8,128)(2,1)S(1)}, u32[]{:S(2)}, u32[]{:S(2)}) collective-permute-start(bf16[384,768]{1,0:T(8,128)(2,1)S(1)} %get-tuple-element.182.one), channel_id=1, source_target_pairs={{0,1},{1,2},{2,3},{3,0},{4,5},{5,6},{6,7},{7,4},{8,9},{9,10},{10,1... | collective-permute-start | bytes 1769480 | tf_op jit(solution)/shard_map/ppermute | solution.py:1244
  145.2 34.5 %collective-permute-start.26 = (bf16[384,768]{1,0:T(8,128)(2,1)S(1)}, bf16[384,768]{1,0:T(8,128)(2,1)S(1)}, u32[]{:S(2)}, u32[]{:S(2)}) collective-permute-start(bf16[384,768]{1,0:T(8,128)(2,1)S(1)} %get-tuple-element.182.one), channel_id=1, source_target_pairs={{0,2},{1,3},{2,0},{3,1},{4,6},{5,7},{6,4},{7,5},{8,10},{9,11},{10,... | collective-permute-start | bytes 1769480 | tf_op jit(solution)/shard_map/ppermute | solution.py:1244
  146.5 33.2 %collective-permute-start.24 = (bf16[2,4,192,384]{3,2,1,0:T(8,128)(2,1)S(1)}, bf16[2,4,192,384]{3,2,1,0:T(8,128)(2,1)S(1)}, u32[]{:S(2)}, u32[]{:S(2)}) collective-permute-start(bf16[2,4,192,384]{3,2,1,0:T(8,128)(2,1)S(1)} %get-tuple-element.202), channel_id=1, source_target_pairs={{0,8},{4,12},{8,0},{12,4},{1,9},{5,13},{9,1},{13,5},{2,10},{6,14},... | collective-permute-start | bytes 3538952 | tf_op jit(solution)/shard_map/ppermute | solution.py:1210
  147.7 32.0 %collective-permute-start.25 = (bf16[2,4,192,384]{3,2,1,0:T(8,128)(2,1)S(1)}, bf16[2,4,192,384]{3,2,1,0:T(8,128)(2,1)S(1)}, u32[]{:S(2)}, u32[]{:S(2)}) collective-permute-start(bf16[2,4,192,384]{3,2,1,0:T(8,128)(2,1)S(1)} %get-tuple-element.203), channel_id=1, source_target_pairs={{0,16},{16,0},{1,17},{17,1},{2,18},{18,2},{3,19},{19,3},{4,20},{20... | collective-permute-start | bytes 3538952 | tf_op jit(solution)/shard_map/ppermute | solution.py:1257
  182.0 33.6 %collective-permute-start.32 = (bf16[128,768]{1,0:T(8,128)(2,1)}, bf16[128,768]{1,0:T(8,128)(2,1)S(1)}, u32[]{:S(2)}, u32[]{:S(2)}) collective-permute-start(bf16[128,768]{1,0:T(8,128)(2,1)} %copy-done.17), channel_id=1, source_target_pairs={{4,5},{1,0},{5,13},{9,1},{13,12},{8,9},{6,7},{3,2},{7,15},{11,3},{... | collective-permute-start | bytes 589832 | tf_op jit(solution)/shard_map/ppermute | solution.py:1518
  188.0 27.7 %collective-permute-start.31 = (bf16[384,768]{1,0:T(8,128)(2,1)S(1)}, bf16[384,768]{1,0:T(8,128)(2,1)S(1)}, u32[]{:S(2)}, u32[]{:S(2)}) collective-permute-start(bf16[384,768]{1,0:T(8,128)(2,1)S(1)} %add_convert_fusion.7), channel_id=1, source_target_pairs={{4,1},{1,4},{5,9},{9,5},{13,8},{8,13},{6,3},{3,6},{7,11},{11,7},{1... | collective-permute-start | bytes 1769480 | tf_op jit(solution)/shard_map/ppermute | solution.py:1517
  200.9 15.6 %collective-permute-start.33 = (bf16[384,384]{1,0:T(8,128)(2,1)S(1)}, bf16[384,384]{1,0:T(8,128)(2,1)S(1)}, u32[]{:S(2)}, u32[]{:S(2)}) collective-permute-start(bf16[384,384]{1,0:T(8,128)(2,1)S(1)} %get-tuple-element.270), channel_id=1, source_target_pairs={{0,1},{1,2},{2,3},{3,0},{4,5},{5,6},{6,7},{7,4},{8,9},{9,10},{10,1... | collective-permute-start | bytes 884744 | tf_op jit(solution)/shard_map/ppermute | solution.py:1269
  202.0 15.2 %collective-permute-start.34 = (bf16[384,384]{1,0:T(8,128)(2,1)S(1)}, bf16[384,384]{1,0:T(8,128)(2,1)S(1)}, u32[]{:S(2)}, u32[]{:S(2)}) collective-permute-start(bf16[384,384]{1,0:T(8,128)(2,1)S(1)} %get-tuple-element.271), channel_id=1, source_target_pairs={{0,3},{1,0},{2,1},{3,2},{4,7},{5,4},{6,5},{7,6},{8,11},{9,8},{10,9... | collective-permute-start | bytes 884744 | tf_op jit(solution)/shard_map/ppermute | solution.py:1269
  217.9 19.2 %collective-permute-start.38 = (bf16[2,2,4,200,384]{4,3,2,1,0:T(8,128)(2,1)}, bf16[2,2,4,200,384]{4,3,2,1,0:T(8,128)(2,1)}, u32[]{:S(2)}, u32[]{:S(2)}) collective-permute-start(bf16[2,2,4,200,384]{4,3,2,1,0:T(8,128)(2,1)} %get-tuple-element.226), channel_id=1, source_target_pairs={{0,4},{4,0},{8,12},{12,8},{1,5},{5,1},{9,13},{13,9},{2,6},{6,2},{1... | collective-permute-start | bytes 7372808 | tf_op jit(solution)/shard_map/ppermute | solution.py:1210
  220.8 15.6 %collective-permute-start.39 = (bf16[384,384]{1,0:T(8,128)(2,1)S(1)}, bf16[384,384]{1,0:T(8,128)(2,1)S(1)}, u32[]{:S(2)}, u32[]{:S(2)}) collective-permute-start(bf16[384,384]{1,0:T(8,128)(2,1)S(1)} %copy-done.49), channel_id=1, source_target_pairs={{0,2},{1,3},{2,0},{3,1},{4,6},{5,7},{6,4},{7,5},{8,10},{9,11},{10,... | collective-permute-start | bytes 884744 | tf_op jit(solution)/shard_map/ppermute | solution.py:1269
  239.3 29.2 %collective-permute-start.40 = (bf16[2,4,200,384]{3,2,1,0:T(8,128)(2,1)S(1)}, bf16[2,4,200,384]{3,2,1,0:T(8,128)(2,1)S(1)}, u32[]{:S(2)}, u32[]{:S(2)}) collective-permute-start(bf16[2,4,200,384]{3,2,1,0:T(8,128)(2,1)S(1)} %get-tuple-element.265), channel_id=1, source_target_pairs={{0,16},{16,0},{1,17},{17,1},{2,18},{18,2},{3,19},{19,3},{4,20},{20... | collective-permute-start | bytes 3686408 | tf_op jit(solution)/shard_map/ppermute | solution.py:1257
  240.8 16.1 %collective-permute-start.41 = (bf16[384,768]{1,0:T(8,128)(2,1)S(1)}, bf16[384,768]{1,0:T(8,128)(2,1)S(1)}, u32[]{:S(2)}, u32[]{:S(2)}) collective-permute-start(bf16[384,768]{1,0:T(8,128)(2,1)S(1)} %pad_maximum_fusion.11.one), channel_id=1, source_target_pairs={{0,1},{1,2},{2,3},{3,0},{4,5},{5,6},{6,7},{7,4},{8,9},{9,10},{10,1... | collective-permute-start | bytes 1769480 | tf_op jit(solution)/shard_map/ppermute | solution.py:1244
  240.8 26.8 %collective-permute-start.42 = (bf16[384,768]{1,0:T(8,128)(2,1)S(1)}, bf16[384,768]{1,0:T(8,128)(2,1)S(1)}, u32[]{:S(2)}, u32[]{:S(2)}) collective-permute-start(bf16[384,768]{1,0:T(8,128)(2,1)S(1)} %pad_maximum_fusion.11.one), channel_id=1, source_target_pairs={{0,3},{1,0},{2,1},{3,2},{4,7},{5,4},{6,5},{7,6},{8,11},{9,8},{10,9... | collective-permute-start | bytes 1769480 | tf_op jit(solution)/shard_map/ppermute | solution.py:1244
  245.1 29.7 %collective-permute-start.45 = (bf16[4,128,768]{2,1,0:T(8,128)(2,1)}, bf16[4,128,768]{2,1,0:T(8,128)(2,1)}, u32[]{:S(2)}, u32[]{:S(2)}) collective-permute-start(bf16[4,128,768]{2,1,0:T(8,128)(2,1)} %pad_maximum_fusion.7), channel_id=1, source_target_pairs={{0,4},{4,0},{8,12},{12,8},{1,5},{5,1},{9,13},{13,9},{2,6},{6,2},{1... | collective-permute-start | bytes 2359304 | tf_op jit(solution)/shard_map/ppermute | solution.py:1210
  247.4 27.4 %collective-permute-start.44 = (bf16[2,256,768]{2,1,0:T(8,128)(2,1)}, bf16[2,256,768]{2,1,0:T(8,128)(2,1)}, u32[]{:S(2)}, u32[]{:S(2)}) collective-permute-start(bf16[2,256,768]{2,1,0:T(8,128)(2,1)} %pad_maximum_fusion.6), channel_id=1, source_target_pairs={{0,12},{4,8},{8,4},{12,0},{1,13},{5,9},{9,5},{13,1},{2,14},{6,10},... | collective-permute-start | bytes 2359304 | tf_op jit(solution)/shard_map/ppermute | solution.py:1558
  271.1 28.7 %collective-permute-start.46 = (bf16[384,768]{1,0:T(8,128)(2,1)S(1)}, bf16[384,768]{1,0:T(8,128)(2,1)S(1)}, u32[]{:S(2)}, u32[]{:S(2)}) collective-permute-start(bf16[384,768]{1,0:T(8,128)(2,1)S(1)} %pad_maximum_fusion.11.one), channel_id=1, source_target_pairs={{0,2},{1,3},{2,0},{3,1},{4,6},{5,7},{6,4},{7,5},{8,10},{9,11},{10,... | collective-permute-start | bytes 1769480 | tf_op jit(solution)/shard_map/ppermute | solution.py:1244
  274.5 16.1 %collective-permute-start.48 = (bf16[384,384]{1,0:T(8,128)(2,1)S(1)}, bf16[384,384]{1,0:T(8,128)(2,1)S(1)}, u32[]{:S(2)}, u32[]{:S(2)}) collective-permute-start(bf16[384,384]{1,0:T(8,128)(2,1)S(1)} %fusion.15.mine), channel_id=1, source_target_pairs={{0,8},{4,12},{8,0},{12,4},{1,9},{5,13},{9,1},{13,5},{2,10},{6,14},... | collective-permute-start | bytes 884744 | tf_op jit(solution)/shard_map/ppermute | solution.py:1210
  285.4 17.6 %collective-permute-start.47 = (bf16[200,384]{1,0:T(8,128)(2,1)S(1)}, bf16[200,384]{1,0:T(8,128)(2,1)S(1)}, u32[]{:S(2)}, u32[]{:S(2)}) collective-permute-start(bf16[200,384]{1,0:T(8,128)(2,1)S(1)} %get-tuple-element.280), channel_id=1, source_target_pairs={{0,3},{1,0},{2,1},{3,2},{4,7},{5,4},{6,5},{7,6},{8,11},{9,8},{10,9... | collective-permute-start | bytes 460808 | tf_op jit(solution)/shard_map/ppermute | solution.py:1269
  303.1 16.0 %collective-permute-start.52 = (bf16[4,128,768]{2,1,0:T(8,128)(2,1)S(1)}, bf16[4,128,768]{2,1,0:T(8,128)(2,1)S(1)}, u32[]{:S(2)}, u32[]{:S(2)}) collective-permute-start(bf16[4,128,768]{2,1,0:T(8,128)(2,1)S(1)} %pad_maximum_fusion.8), channel_id=1, source_target_pairs={{0,4},{4,0},{8,12},{12,8},{1,5},{5,1},{9,13},{13,9},{2,6},{6,2},{1... | collective-permute-start | bytes 2359304 | tf_op jit(solution)/shard_map/ppermute | solution.py:1210
  (86 other events, 661.0 us)

commit v3 on v2

--- a/solution.py
+++ b/solution.py
@@ -330,9 +330,8 @@
     o_ref, l_ref = refs[-2:]
     here = pl.ds(pl.multiple_of(pl.program_id(1) * QBLOCK, QBLOCK), span)
     same = qd_ref[:, :1] == kd_ref[:, here]
-    logs = []
-    for pair in range(q_ref.shape[1] // PAIR):
-        cols = slice(pair * PAIR, (pair + 1) * PAIR)
+
+    def one_pair(cols):
         scores = masked_scores(stack_heads(q_ref[:, cols]), k_ref[here, cols], same)
         top = jnp.max(scores, axis=1, keepdims=True)
         expo = jnp.exp(scores - top)
@@ -340,8 +339,20 @@
         mixed = dot32(expo.astype(jnp.bfloat16), v_ref[here, cols]) * (1.0 / total)
         o_ref[:, cols] = unstack_heads(mixed).astype(jnp.bfloat16)
         log = top + jnp.log(total)
-        logs += [log[:QBLOCK], log[QBLOCK:]]
-    l_ref[0] = jnp.concatenate(logs, axis=1)
+        return log[:QBLOCK], log[QBLOCK:]
+
+    pairs = q_ref.shape[1] // PAIR
+    if len(refs) > 2:
+        logs = [log for p in range(pairs) for log in one_pair(slice(p * PAIR, (p + 1) * PAIR))]
+        l_ref[0] = jnp.concatenate(logs, axis=1)
+    else:
+        lane = lax.broadcasted_iota(jnp.int32, l_ref.shape[1:], 1)
+
+        @pl.loop(0, pairs)
+        def _(pair):
+            first, second = one_pair(pl.ds(pl.multiple_of(pair * PAIR, PAIR), PAIR))
+            logs = jnp.where(lane == 2 * pair, first, l_ref[0])
+            l_ref[0] = jnp.where(lane == 2 * pair + 1, second, logs)
 
 
 def attend_back_kernel(

time: 332 us -> 333 us (level)
    ppermute x13, waiting for transfers between devices: 45.4 us -> 40.8 us  [tp_shifts(): lax.ppermute(array[cut], 'tp', [(i, (i + shift) % 4) for i in range(4)])]
    ppermute x23, starting transfers between devices: 20.7 us -> 24.7 us  [ctx_swap(): return lax.ppermute(array, 'ctx', [(i, i ^ bit) for i in range(4)])]
where the time goes in v3:
time: 333 us; the launch traced here: 328 us
  waiting for transfers between devices  95.5 us (29%)
  Pallas kernels  94 us (28%)
  starting transfers between devices  70.1 us (21%)
  other arithmetic  35.2 us (11%)
  local copies, waits for them, and re-layouts  31.1 us (9%)
    ppermute x13, waiting for transfers between devices, tp_shifts(): lax.ppermute(array[cut], 'tp', [(i, (i + shift) % 4) for i in range(4)])  40.8 us
    ppermute x23, starting transfers between devices, ctx_swap(): return lax.ppermute(array, 'ctx', [(i, i ^ bit) for i in range(4)])  24.7 us
    ppermute x6, waiting for transfers between devices, scatter_tp_start(): lax.ppermute(sent, 'tp', [(i, (i + shift) % 4) for i in range(4)])  24 us
    pallas_call x1, Pallas kernels, attend_back(): pl.pallas_call(partial(attend_back_kernel, span, short_span(reach)), grid...  18.3 us
    ppermute x23, waiting for transfers between devices, ctx_swap(): return lax.ppermute(array, 'ctx', [(i, i ^ bit) for i in range(4)])  17.5 us
    ppermute x13, starting transfers between devices, tp_shifts(): lax.ppermute(array[cut], 'tp', [(i, (i + shift) % 4) for i in range(4)])  16.6 us
    pallas_call x2, Pallas kernels, attend(): pl.pallas_call(partial(attend_kernel, span), grid=(1, count // QBLOCK), i...  14.9 us
    pallas_call x1, Pallas kernels, ffn_back(): pl.pallas_call(ffn_back_kernel, grid_spec=pltpu.PrefetchScalarGridSpec(nu...  13.2 us
  transfers between devices with their start and end apart: 57, of which 24 were waited for; matrix products, arithmetic and copies ran while one was open for 14% of the time, Pallas kernels for 28%

profile of v3, /device:TPU:1, one launch (start us, length us, event | category | flops | bytes accessed | tf_op | source)
XLA Modules:
  0.0 328.1 jit_solution(2574591205952662786)
XLA Ops:
  9.7 2.7 dynamic-slice_bitcast_fusion
  24.9 4.7 %collective-permute-done.4 = bf16[864,384]{1,0:T(8,128)(2,1)} collective-permute-done((bf16[864,384]{1,0:T(8,128)(2,1)}, bf16[864,384]{1,0:T(8,128)(2,1)}, u32[]{:S(2)}, u32[]{:S(2)}) %collective-permute-start.4) | collective-permute-done | bytes 663584 | tf_op jit(solution)/shard_map/ppermute | solution.py:1268
  35.1 2.9 collective-permute-start.9
  38.7 3.1 collective-permute-start.7
  46.9 3.8 %collective-permute-done.6 = bf16[864,384]{1,0:T(8,128)(2,1)} collective-permute-done((bf16[864,384]{1,0:T(8,128)(2,1)}, bf16[864,384]{1,0:T(8,128)(2,1)}, u32[]{:S(2)}, u32[]{:S(2)}) %collective-permute-start.6) | collective-permute-done | bytes 663584 | tf_op jit(solution)/shard_map/ppermute | solution.py:1255
  50.7 2.9 collective-permute-done.5
  55.1 3.7 %collective-permute-start.8 = (bf16[2,4,304,384]{3,2,1,0:T(8,128)(2,1)S(1)}, bf16[2,4,304,384]{3,2,1,0:T(8,128)(2,1)}, u32[]{:S(2)}, u32[]{:S(2)}) collective-permute-start(bf16[2,4,304,384]{3,2,1,0:T(8,128)(2,1)S(1)} %pad_maximum_fusion.1.w_mine), channel_id=1, source_target_pairs={{0,4},{4,0},{8,12},{12,8},{1,5},{5,1},{9,13},{13,9},{2,6},{6,2},{1... | collective-permute-start | bytes 5603336 | tf_op jit(solution)/shard_map/ppermute | solution.py:1221
  73.2 7.0 %project.1 = (bf16[384,768]{1,0:T(8,128)(2,1)S(1)}, bf16[1408,768]{1,0:T(8,128)(2,1)S(1)}, bf16[1408,768]{1,0:T(8,128)(2,1)S(1)}, bf16[1408,768]{1,0:T(8,128)(2,1)S(1)}, bf16[3,768,768]{2,1,0:T(8,128)(2,1)S(1)}) custom-call(s32[5]{0:T(128)S(1)} %stack.258.place_ref, bf16[2,4,304,384]{3,2,1,0:T(8,128)(2,1)S(1)} %pad_maximum_fusion.1.w_mine, ...), custom_call_target="tpu_custom_call" | custom-call | flops 3321888768 | bytes 16777216 | tf_op jit(solution)/shard_map/project/pallas_call | solution.py:754
  82.0 8.4 %attend.2 = (bf16[384,768]{1,0:T(8,128)(2,1)S(1)}, f32[2,384,6]{2,1,0:T(8,128)S(1)}) custom-call(bf16[384,768]{1,0:T(8,128)(2,1)S(1)} %get-tuple-element.154.q_ref, bf16[1408,768]{1,0:T(8,128)(2,1)S(1)} %get-tuple-element.155.k_ref, bf16[1408,768]{1,0:T(8,128)(2,1)S(1)} %get-tuple-element.156.v_ref, s32[1,1408]{1,0:T(1,128)S(1)} %broadcast_in_dim.34.kd_ref, ...), custom_call_target="tpu_custom_call" | custom-call | flops 2717908992 | bytes 4194304 | tf_op jit(solution)/shard_map/attend/pallas_call | solution.py:431
  90.4 5.7 %collective-permute-done.13 = bf16[480,384]{1,0:T(8,128)(2,1)S(1)} collective-permute-done((bf16[480,384]{1,0:T(8,128)(2,1)S(1)}, bf16[480,384]{1,0:T(8,128)(2,1)S(1)}, u32[]{:S(2)}, u32[]{:S(2)}) %collective-permute-start.13) | collective-permute-done | bytes 368672 | tf_op jit(solution)/shard_map/ppermute | solution.py:1255
  97.3 6.5 %attend.3 = (bf16[384,768]{1,0:T(8,128)(2,1)S(1)}, f32[2,384,6]{2,1,0:T(8,128)S(1)}) custom-call(bf16[384,768]{1,0:T(8,128)(2,1)S(1)} %get-tuple-element.154.q_ref, bf16[1408,768]{1,0:T(8,128)(2,1)S(1)} %get-tuple-element.155.k_ref, bf16[1408,768]{1,0:T(8,128)(2,1)S(1)} %get-tuple-element.156.v_ref, ...), custom_call_target="tpu_custom_call", output_to_operand_aliasing={{0}: (5, {}), {1}: (6, {})} | custom-call | flops 2717908992 | bytes 4194304 | tf_op jit(solution)/shard_map/attend/pallas_call | solution.py:431
  114.6 7.0 %ffn.2 = (bf16[768,1536]{1,0:T(8,128)(2,1)S(1)}, bf16[768,1536]{1,0:T(8,128)(2,1)S(1)}, f32[768,768]{1,0:T(8,128)S(1)}) custom-call(s32[5]{0:T(128)S(1)} %stack.258.place_ref, bf16[384,768]{1,0:T(8,128)(2,1)S(1)} %get-tuple-element.170.h_ref, bf16[384,768]{1,0:T(8,128)(2,1)S(1)} %collective-permute-done.17.other_h_ref, ...), custom_call_target="tpu_custom_call" | custom-call | flops 8153726976 | bytes 9437184 | tf_op jit(solution)/shard_map/ffn/pallas_call | solution.py:650
  122.1 2.5 ffn.3
  131.5 13.2 %ffn_back.1 = (bf16[384,768]{1,0:T(8,128)(2,1)S(1)}, bf16[384,768]{1,0:T(8,128)(2,1)S(1)}, bf16[2,4,192,384]{3,2,1,0:T(8,128)(2,1)S(1)}, bf16[2,4,192,384]{3,2,1...) custom-call(s32[5]{0:T(128)S(1)} %stack.258.place_ref, ...), custom_call_target="tpu_custom_call" | custom-call | flops 10871635968 | bytes 20971520 | tf_op jit(solution)/shard_map/ffn_back/pallas_call | solution.py:672
  151.5 18.3 %attend_back.1 = (bf16[384,768]{1,0:T(8,128)(2,1)S(1)}, bf16[1408,768]{1,0:T(8,128)(2,1)S(1)}, bf16[1408,768]{1,0:T(8,128)(2,1)S(1)}) custom-call(s32[2,3]{1,0:T(2,128)S(1)} %pad_add_fusion.plan_ref, bf16[384,768]{1,0:T(8,128)(2,1)S(1)} %get-tuple-element.154.q_ref, bf16[1408,768]{1,0:T(8,128)(2,1)S(1)} %get-tuple-element.155.k_ref, ...), custom_call_target="tpu_custom_call" | custom-call | flops 13589544960 | bytes 12582912 | tf_op jit(solution)/shard_map/attend_back/pallas_call | solution.py:455
  169.9 6.3 %span_grads.1 = (f32[384,768]{1,0:T(8,128)S(1)}, bf16[384,768]{1,0:T(8,128)(2,1)S(1)}, bf16[128,768]{1,0:T(8,128)(2,1)S(1)}, bf16[512,768]{1,0:T(8,128)(2,1)}) custom-call(s32[5]{0:T(128)S(1)} %stack.258.place_ref, bf16[384,768]{1,0:T(8,128)(2,1)S(1)} %get-tuple-element.196.dq_ref, bf16[1408,768]{1,0:T(8,128)(2,1)S(1)} %get-tuple-element.213.dk_ref, ...), custom_call_target="tpu_custom_call" | custom-call | flops 3321888768 | bytes 12582912 | tf_op jit(solution)/shard_map/span_grads/pallas_call | solution.py:1068
  179.7 2.9 collective-permute-start.29
  183.7 3.8 %collective-permute-start.32 = (bf16[128,768]{1,0:T(8,128)(2,1)}, bf16[128,768]{1,0:T(8,128)(2,1)S(1)}, u32[]{:S(2)}, u32[]{:S(2)}) collective-permute-start(bf16[128,768]{1,0:T(8,128)(2,1)} %copy-done.17), channel_id=1, source_target_pairs={{4,5},{1,0},{5,13},{9,1},{13,12},{8,9},{6,7},{3,2},{7,15},{11,3},{... | collective-permute-start | bytes 589832 | tf_op jit(solution)/shard_map/ppermute | solution.py:1529
  189.7 2.5 collective-permute-start.31
  193.6 3.0 collective-permute-done.29
  207.8 8.3 %attn_grads.1 = (bf16[2,2,4,200,384]{4,3,2,1,0:T(8,128)(2,1)S(1)}, bf16[2,2,4,200,384]{4,3,2,1,0:T(8,128)(2,1)}) custom-call(s32[5]{0:T(128)S(1)} %stack.258.place_ref, bf16[384,768]{1,0:T(8,128)(2,1)S(1)} %copy-done.25, bf16[1408,768]{1,0:T(8,128)(2,1)S(1)} %copy-done.21, bf16[1408,768]{1,0:T(8,128)(2,1)S(1)} %copy-done.23, ...), custom_call_target="tpu_custom_call" | custom-call | flops 4227858432 | bytes 16777216 | tf_op jit(solution)/shard_map/attn_grads/pallas_call | solution.py:993
  228.5 9.6 %collective-permute-done.39 = bf16[384,384]{1,0:T(8,128)(2,1)S(1)} collective-permute-done((bf16[384,384]{1,0:T(8,128)(2,1)S(1)}, bf16[384,384]{1,0:T(8,128)(2,1)S(1)}, u32[]{:S(2)}, u32[]{:S(2)}) %collective-permute-start.39) | collective-permute-done | bytes 294944 | tf_op jit(solution)/shard_map/ppermute | solution.py:1280
  242.2 3.3 collective-permute-start.42
  248.6 9.8 %collective-permute-done.41.two = bf16[384,768]{1,0:T(8,128)(2,1)S(1)} collective-permute-done((bf16[384,768]{1,0:T(8,128)(2,1)S(1)}, bf16[384,768]{1,0:T(8,128)(2,1)S(1)}, u32[]{:S(2)}, u32[]{:S(2)}) %collective-permute-start.41) | collective-permute-done | bytes 589856 | tf_op jit(solution)/shard_map/ppermute | solution.py:1255
  258.5 10.8 %collective-permute-done.42.four = bf16[384,768]{1,0:T(8,128)(2,1)S(1)} collective-permute-done((bf16[384,768]{1,0:T(8,128)(2,1)S(1)}, bf16[384,768]{1,0:T(8,128)(2,1)S(1)}, u32[]{:S(2)}, u32[]{:S(2)}) %collective-permute-start.42) | collective-permute-done | bytes 589856 | tf_op jit(solution)/shard_map/ppermute | solution.py:1255
  276.4 9.2 %collective-permute-done.43 = bf16[4,200,384]{2,1,0:T(8,128)(2,1)} collective-permute-done((bf16[4,200,384]{2,1,0:T(8,128)(2,1)}, bf16[4,200,384]{2,1,0:T(8,128)(2,1)}, u32[]{:S(2)}, u32[]{:S(2)}) %collective-permute-start.43) | collective-permute-done | bytes 614432 | tf_op jit(solution)/shard_map/ppermute | solution.py:1221
  289.7 3.1 assemble.2
  292.8 7.2 %collective-permute-done.46.three = bf16[384,768]{1,0:T(8,128)(2,1)S(1)} collective-permute-done((bf16[384,768]{1,0:T(8,128)(2,1)S(1)}, bf16[384,768]{1,0:T(8,128)(2,1)S(1)}, u32[]{:S(2)}, u32[]{:S(2)}) %collective-permute-start.46) | collective-permute-done | bytes 589856 | tf_op jit(solution)/shard_map/ppermute | solution.py:1255
  300.0 3.5 %collective-permute-done.47 = bf16[200,384]{1,0:T(8,128)(2,1)S(1)} collective-permute-done((bf16[200,384]{1,0:T(8,128)(2,1)S(1)}, bf16[200,384]{1,0:T(8,128)(2,1)S(1)}, u32[]{:S(2)}, u32[]{:S(2)}) %collective-permute-start.47) | collective-permute-done | bytes 153632 | tf_op jit(solution)/shard_map/ppermute | solution.py:1280
  306.5 5.0 %collective-permute-done.49 = bf16[200,384]{1,0:T(8,128)(2,1)S(1)} collective-permute-done((bf16[200,384]{1,0:T(8,128)(2,1)S(1)}, bf16[200,384]{1,0:T(8,128)(2,1)S(1)}, u32[]{:S(2)}, u32[]{:S(2)}) %collective-permute-start.49) | collective-permute-done | bytes 153632 | tf_op jit(solution)/shard_map/ppermute | solution.py:1280
  311.6 5.8 %collective-permute-done.50 = bf16[200,384]{1,0:T(8,128)(2,1)S(1)} collective-permute-done((bf16[200,384]{1,0:T(8,128)(2,1)S(1)}, bf16[200,384]{1,0:T(8,128)(2,1)S(1)}, u32[]{:S(2)}, u32[]{:S(2)}) %collective-permute-start.50) | collective-permute-done | bytes 153632 | tf_op jit(solution)/shard_map/ppermute | solution.py:1280
  320.5 3.1 assemble.3
  (334 shorter events, 135.9 us)
Async XLA Ops:
  4.2 20.0 %collective-permute-start = (bf16[304,384]{1,0:T(8,128)(2,1)}, bf16[304,384]{1,0:T(8,128)(2,1)}, u32[]{:S(2)}, u32[]{:S(2)}) collective-permute-start(bf16[304,384]{1,0:T(8,128)(2,1)} %maximum_maximum_fusion), channel_id=1, source_target_pairs={{0,1},{1,2},{2,3},{3,0},{4,5},{5,6},{6,7},{7,4},{8,9},{9,10},{10,1... | collective-permute-start | bytes 700424 | tf_op jit(solution)/shard_map/ppermute | solution.py:1255
  6.3 18.5 %collective-permute-start.1 = (bf16[304,384]{1,0:T(8,128)(2,1)}, bf16[304,384]{1,0:T(8,128)(2,1)}, u32[]{:S(2)}, u32[]{:S(2)}) collective-permute-start(bf16[304,384]{1,0:T(8,128)(2,1)} %maximum_maximum_fusion), channel_id=1, source_target_pairs={{0,2},{1,3},{2,0},{3,1},{4,6},{5,7},{6,4},{7,5},{8,10},{9,11},{10,... | collective-permute-start | bytes 700424 | tf_op jit(solution)/shard_map/ppermute | solution.py:1255
  8.7 16.2 %collective-permute-start.2 = (bf16[304,384]{1,0:T(8,128)(2,1)}, bf16[304,384]{1,0:T(8,128)(2,1)}, u32[]{:S(2)}, u32[]{:S(2)}) collective-permute-start(bf16[304,384]{1,0:T(8,128)(2,1)} %maximum_maximum_fusion), channel_id=1, source_target_pairs={{0,3},{1,0},{2,1},{3,2},{4,7},{5,4},{6,5},{7,6},{8,11},{9,8},{10,9... | collective-permute-start | bytes 700424 | tf_op jit(solution)/shard_map/ppermute | solution.py:1255
  12.4 17.8 %collective-permute-start.3 = (bf16[2,256,768]{2,1,0:T(8,128)(2,1)}, bf16[2,256,768]{2,1,0:T(8,128)(2,1)S(1)}, u32[]{:S(2)}, u32[]{:S(2)}) collective-permute-start(bf16[2,256,768]{2,1,0:T(8,128)(2,1)} %get-tuple-element.268), channel_id=1, source_target_pairs={{0,8},{4,12},{8,0},{12,4},{1,9},{5,13},{9,1},{13,5},{2,10},{6,14},... | collective-permute-start | bytes 2359304 | tf_op jit(solution)/shard_map/ppermute | solution.py:1221
  33.4 20.2 %collective-permute-start.5 = (bf16[4,304,384]{2,1,0:T(8,128)(2,1)}, bf16[4,304,384]{2,1,0:T(8,128)(2,1)}, u32[]{:S(2)}, u32[]{:S(2)}) collective-permute-start(bf16[4,304,384]{2,1,0:T(8,128)(2,1)} %get-tuple-element.277), channel_id=1, source_target_pairs={{0,16},{16,0},{1,17},{17,1},{2,18},{18,2},{3,19},{19,3},{4,20},{20... | collective-permute-start | bytes 2801672 | tf_op jit(solution)/shard_map/ppermute | solution.py:1268
  34.7 16.0 %collective-permute-start.6 = (bf16[864,384]{1,0:T(8,128)(2,1)}, bf16[864,384]{1,0:T(8,128)(2,1)}, u32[]{:S(2)}, u32[]{:S(2)}) collective-permute-start(bf16[864,384]{1,0:T(8,128)(2,1)} %pad_maximum_fusion.9), channel_id=1, source_target_pairs={{0,1},{1,2},{2,3},{3,0},{4,5},{5,6},{6,7},{7,4},{8,9},{9,10},{10,1... | collective-permute-start | bytes 1990664 | tf_op jit(solution)/shard_map/ppermute | solution.py:1255
  35.1 30.9 %collective-permute-start.9 = (bf16[864,384]{1,0:T(8,128)(2,1)}, bf16[864,384]{1,0:T(8,128)(2,1)}, u32[]{:S(2)}, u32[]{:S(2)}) collective-permute-start(bf16[864,384]{1,0:T(8,128)(2,1)} %pad_maximum_fusion.9), channel_id=1, source_target_pairs={{0,3},{1,0},{2,1},{3,2},{4,7},{5,4},{6,5},{7,6},{8,11},{9,8},{10,9... | collective-permute-start | bytes 1990664 | tf_op jit(solution)/shard_map/ppermute | solution.py:1255
  61.8 28.6 %collective-permute-start.11 = (bf16[864,384]{1,0:T(8,128)(2,1)}, bf16[864,384]{1,0:T(8,128)(2,1)S(1)}, u32[]{:S(2)}, u32[]{:S(2)}) collective-permute-start(bf16[864,384]{1,0:T(8,128)(2,1)} %collective-permute-done.6), channel_id=1, source_target_pairs={{0,16},{16,0},{1,17},{17,1},{2,18},{18,2},{3,19},{19,3},{4,20},{20... | collective-permute-start | bytes 1990664 | tf_op jit(solution)/shard_map/ppermute | solution.py:1268
  66.0 30.2 %collective-permute-start.12 = (bf16[864,384]{1,0:T(8,128)(2,1)}, bf16[864,384]{1,0:T(8,128)(2,1)S(1)}, u32[]{:S(2)}, u32[]{:S(2)}) collective-permute-start(bf16[864,384]{1,0:T(8,128)(2,1)} %collective-permute-done.9), channel_id=1, source_target_pairs={{0,16},{16,0},{1,17},{17,1},{2,18},{18,2},{3,19},{19,3},{4,20},{20... | collective-permute-start | bytes 1990664 | tf_op jit(solution)/shard_map/ppermute | solution.py:1268
  70.8 25.4 %collective-permute-start.13 = (bf16[480,384]{1,0:T(8,128)(2,1)S(1)}, bf16[480,384]{1,0:T(8,128)(2,1)S(1)}, u32[]{:S(2)}, u32[]{:S(2)}) collective-permute-start(bf16[480,384]{1,0:T(8,128)(2,1)S(1)} %slice.294), channel_id=1, source_target_pairs={{0,2},{1,3},{2,0},{3,1},{4,6},{5,7},{6,4},{7,5},{8,10},{9,11},{10,... | collective-permute-start | bytes 1105928 | tf_op jit(solution)/shard_map/ppermute | solution.py:1255
  70.8 33.0 %collective-permute-start.15 = (bf16[384,384]{1,0:T(8,128)(2,1)S(1)}, bf16[384,384]{1,0:T(8,128)(2,1)S(1)}, u32[]{:S(2)}, u32[]{:S(2)}) collective-permute-start(bf16[384,384]{1,0:T(8,128)(2,1)S(1)} %slice.295), channel_id=1, source_target_pairs={{0,2},{1,3},{2,0},{3,1},{4,6},{5,7},{6,4},{7,5},{8,10},{9,11},{10,... | collective-permute-start | bytes 884744 | tf_op jit(solution)/shard_map/ppermute | solution.py:1255
  80.2 45.7 %collective-permute-start.20 = (bf16[2,256,768]{2,1,0:T(8,128)(2,1)S(1)}, bf16[2,256,768]{2,1,0:T(8,128)(2,1)S(1)}, u32[]{:S(2)}, u32[]{:S(2)}) collective-permute-start(bf16[2,256,768]{2,1,0:T(8,128)(2,1)S(1)} %pad_maximum_fusion.5.g_ref), channel_id=1, source_target_pairs={{0,4},{4,0},{8,12},{12,8},{1,5},{5,1},{9,13},{13,9},{2,6},{6,2},{1... | collective-permute-start | bytes 2359304 | tf_op jit(solution)/shard_map/ppermute | solution.py:1221
  129.9 16.6 %collective-permute-start.22 = (bf16[384,768]{1,0:T(8,128)(2,1)S(1)}, bf16[384,768]{1,0:T(8,128)(2,1)S(1)}, u32[]{:S(2)}, u32[]{:S(2)}) collective-permute-start(bf16[384,768]{1,0:T(8,128)(2,1)S(1)} %get-tuple-element.182.one), channel_id=1, source_target_pairs={{0,1},{1,2},{2,3},{3,0},{4,5},{5,6},{6,7},{7,4},{8,9},{9,10},{10,1... | collective-permute-start | bytes 1769480 | tf_op jit(solution)/shard_map/ppermute | solution.py:1255
  145.2 33.4 %collective-permute-start.26 = (bf16[384,768]{1,0:T(8,128)(2,1)S(1)}, bf16[384,768]{1,0:T(8,128)(2,1)S(1)}, u32[]{:S(2)}, u32[]{:S(2)}) collective-permute-start(bf16[384,768]{1,0:T(8,128)(2,1)S(1)} %get-tuple-element.182.one), channel_id=1, source_target_pairs={{0,2},{1,3},{2,0},{3,1},{4,6},{5,7},{6,4},{7,5},{8,10},{9,11},{10,... | collective-permute-start | bytes 1769480 | tf_op jit(solution)/shard_map/ppermute | solution.py:1255
  146.5 32.1 %collective-permute-start.24 = (bf16[2,4,192,384]{3,2,1,0:T(8,128)(2,1)S(1)}, bf16[2,4,192,384]{3,2,1,0:T(8,128)(2,1)S(1)}, u32[]{:S(2)}, u32[]{:S(2)}) collective-permute-start(bf16[2,4,192,384]{3,2,1,0:T(8,128)(2,1)S(1)} %get-tuple-element.202), channel_id=1, source_target_pairs={{0,8},{4,12},{8,0},{12,4},{1,9},{5,13},{9,1},{13,5},{2,10},{6,14},... | collective-permute-start | bytes 3538952 | tf_op jit(solution)/shard_map/ppermute | solution.py:1221
  147.7 30.9 %collective-permute-start.25 = (bf16[2,4,192,384]{3,2,1,0:T(8,128)(2,1)S(1)}, bf16[2,4,192,384]{3,2,1,0:T(8,128)(2,1)S(1)}, u32[]{:S(2)}, u32[]{:S(2)}) collective-permute-start(bf16[2,4,192,384]{3,2,1,0:T(8,128)(2,1)S(1)} %get-tuple-element.203), channel_id=1, source_target_pairs={{0,16},{16,0},{1,17},{17,1},{2,18},{18,2},{3,19},{19,3},{4,20},{20... | collective-permute-start | bytes 3538952 | tf_op jit(solution)/shard_map/ppermute | solution.py:1268
  179.7 16.9 %collective-permute-start.29 = (bf16[4,192,384]{2,1,0:T(8,128)(2,1)}, bf16[4,192,384]{2,1,0:T(8,128)(2,1)}, u32[]{:S(2)}, u32[]{:S(2)}) collective-permute-start(bf16[4,192,384]{2,1,0:T(8,128)(2,1)} %fusion.10), channel_id=1, source_target_pairs={{0,8},{4,12},{8,0},{12,4},{1,9},{5,13},{9,1},{13,5},{2,10},{6,14},... | collective-permute-start | bytes 1769480 | tf_op jit(solution)/shard_map/ppermute | solution.py:1221
  183.7 33.9 %collective-permute-start.32 = (bf16[128,768]{1,0:T(8,128)(2,1)}, bf16[128,768]{1,0:T(8,128)(2,1)S(1)}, u32[]{:S(2)}, u32[]{:S(2)}) collective-permute-start(bf16[128,768]{1,0:T(8,128)(2,1)} %copy-done.17), channel_id=1, source_target_pairs={{4,5},{1,0},{5,13},{9,1},{13,12},{8,9},{6,7},{3,2},{7,15},{11,3},{... | collective-permute-start | bytes 589832 | tf_op jit(solution)/shard_map/ppermute | solution.py:1529
  189.7 27.9 %collective-permute-start.31 = (bf16[384,768]{1,0:T(8,128)(2,1)S(1)}, bf16[384,768]{1,0:T(8,128)(2,1)S(1)}, u32[]{:S(2)}, u32[]{:S(2)}) collective-permute-start(bf16[384,768]{1,0:T(8,128)(2,1)S(1)} %add_convert_fusion.7), channel_id=1, source_target_pairs={{4,1},{1,4},{5,9},{9,5},{13,8},{8,13},{6,3},{3,6},{7,11},{11,7},{1... | collective-permute-start | bytes 1769480 | tf_op jit(solution)/shard_map/ppermute | solution.py:1528
  202.9 15.6 %collective-permute-start.33 = (bf16[384,384]{1,0:T(8,128)(2,1)S(1)}, bf16[384,384]{1,0:T(8,128)(2,1)S(1)}, u32[]{:S(2)}, u32[]{:S(2)}) collective-permute-start(bf16[384,384]{1,0:T(8,128)(2,1)S(1)} %get-tuple-element.270), channel_id=1, source_target_pairs={{0,1},{1,2},{2,3},{3,0},{4,5},{5,6},{6,7},{7,4},{8,9},{9,10},{10,1... | collective-permute-start | bytes 884744 | tf_op jit(solution)/shard_map/ppermute | solution.py:1280
  204.0 15.2 %collective-permute-start.34 = (bf16[384,384]{1,0:T(8,128)(2,1)S(1)}, bf16[384,384]{1,0:T(8,128)(2,1)S(1)}, u32[]{:S(2)}, u32[]{:S(2)}) collective-permute-start(bf16[384,384]{1,0:T(8,128)(2,1)S(1)} %get-tuple-element.271), channel_id=1, source_target_pairs={{0,3},{1,0},{2,1},{3,2},{4,7},{5,4},{6,5},{7,6},{8,11},{9,8},{10,9... | collective-permute-start | bytes 884744 | tf_op jit(solution)/shard_map/ppermute | solution.py:1280
  219.9 18.9 %collective-permute-start.38 = (bf16[2,2,4,200,384]{4,3,2,1,0:T(8,128)(2,1)}, bf16[2,2,4,200,384]{4,3,2,1,0:T(8,128)(2,1)}, u32[]{:S(2)}, u32[]{:S(2)}) collective-permute-start(bf16[2,2,4,200,384]{4,3,2,1,0:T(8,128)(2,1)} %get-tuple-element.226), channel_id=1, source_target_pairs={{0,4},{4,0},{8,12},{12,8},{1,5},{5,1},{9,13},{13,9},{2,6},{6,2},{1... | collective-permute-start | bytes 7372808 | tf_op jit(solution)/shard_map/ppermute | solution.py:1221
  222.5 15.6 %collective-permute-start.39 = (bf16[384,384]{1,0:T(8,128)(2,1)S(1)}, bf16[384,384]{1,0:T(8,128)(2,1)S(1)}, u32[]{:S(2)}, u32[]{:S(2)}) collective-permute-start(bf16[384,384]{1,0:T(8,128)(2,1)S(1)} %copy-done.49), channel_id=1, source_target_pairs={{0,2},{1,3},{2,0},{3,1},{4,6},{5,7},{6,4},{7,5},{8,10},{9,11},{10,... | collective-permute-start | bytes 884744 | tf_op jit(solution)/shard_map/ppermute | solution.py:1280
  241.1 29.0 %collective-permute-start.40 = (bf16[2,4,200,384]{3,2,1,0:T(8,128)(2,1)S(1)}, bf16[2,4,200,384]{3,2,1,0:T(8,128)(2,1)S(1)}, u32[]{:S(2)}, u32[]{:S(2)}) collective-permute-start(bf16[2,4,200,384]{3,2,1,0:T(8,128)(2,1)S(1)} %get-tuple-element.265), channel_id=1, source_target_pairs={{0,16},{16,0},{1,17},{17,1},{2,18},{18,2},{3,19},{19,3},{4,20},{20... | collective-permute-start | bytes 3686408 | tf_op jit(solution)/shard_map/ppermute | solution.py:1268
  242.2 16.3 %collective-permute-start.41 = (bf16[384,768]{1,0:T(8,128)(2,1)S(1)}, bf16[384,768]{1,0:T(8,128)(2,1)S(1)}, u32[]{:S(2)}, u32[]{:S(2)}) collective-permute-start(bf16[384,768]{1,0:T(8,128)(2,1)S(1)} %pad_maximum_fusion.11.one), channel_id=1, source_target_pairs={{0,1},{1,2},{2,3},{3,0},{4,5},{5,6},{6,7},{7,4},{8,9},{9,10},{10,1... | collective-permute-start | bytes 1769480 | tf_op jit(solution)/shard_map/ppermute | solution.py:1255
  242.2 27.1 %collective-permute-start.42 = (bf16[384,768]{1,0:T(8,128)(2,1)S(1)}, bf16[384,768]{1,0:T(8,128)(2,1)S(1)}, u32[]{:S(2)}, u32[]{:S(2)}) collective-permute-start(bf16[384,768]{1,0:T(8,128)(2,1)S(1)} %pad_maximum_fusion.11.one), channel_id=1, source_target_pairs={{0,3},{1,0},{2,1},{3,2},{4,7},{5,4},{6,5},{7,6},{8,11},{9,8},{10,9... | collective-permute-start | bytes 1769480 | tf_op jit(solution)/shard_map/ppermute | solution.py:1255
  246.5 29.9 %collective-permute-start.45 = (bf16[4,128,768]{2,1,0:T(8,128)(2,1)}, bf16[4,128,768]{2,1,0:T(8,128)(2,1)}, u32[]{:S(2)}, u32[]{:S(2)}) collective-permute-start(bf16[4,128,768]{2,1,0:T(8,128)(2,1)} %pad_maximum_fusion.7), channel_id=1, source_target_pairs={{0,4},{4,0},{8,12},{12,8},{1,5},{5,1},{9,13},{13,9},{2,6},{6,2},{1... | collective-permute-start | bytes 2359304 | tf_op jit(solution)/shard_map/ppermute | solution.py:1221
  248.6 27.8 %collective-permute-start.44 = (bf16[2,256,768]{2,1,0:T(8,128)(2,1)}, bf16[2,256,768]{2,1,0:T(8,128)(2,1)}, u32[]{:S(2)}, u32[]{:S(2)}) collective-permute-start(bf16[2,256,768]{2,1,0:T(8,128)(2,1)} %pad_maximum_fusion.6), channel_id=1, source_target_pairs={{0,12},{4,8},{8,4},{12,0},{1,13},{5,9},{9,5},{13,1},{2,14},{6,10},... | collective-permute-start | bytes 2359304 | tf_op jit(solution)/shard_map/ppermute | solution.py:1569
  271.4 28.6 %collective-permute-start.46 = (bf16[384,768]{1,0:T(8,128)(2,1)S(1)}, bf16[384,768]{1,0:T(8,128)(2,1)S(1)}, u32[]{:S(2)}, u32[]{:S(2)}) collective-permute-start(bf16[384,768]{1,0:T(8,128)(2,1)S(1)} %pad_maximum_fusion.11.one), channel_id=1, source_target_pairs={{0,2},{1,3},{2,0},{3,1},{4,6},{5,7},{6,4},{7,5},{8,10},{9,11},{10,... | collective-permute-start | bytes 1769480 | tf_op jit(solution)/shard_map/ppermute | solution.py:1255
  274.9 17.9 %collective-permute-start.48 = (bf16[384,384]{1,0:T(8,128)(2,1)S(1)}, bf16[384,384]{1,0:T(8,128)(2,1)S(1)}, u32[]{:S(2)}, u32[]{:S(2)}) collective-permute-start(bf16[384,384]{1,0:T(8,128)(2,1)S(1)} %fusion.15.mine), channel_id=1, source_target_pairs={{0,8},{4,12},{8,0},{12,4},{1,9},{5,13},{9,1},{13,5},{2,10},{6,14},... | collective-permute-start | bytes 884744 | tf_op jit(solution)/shard_map/ppermute | solution.py:1221
  287.2 16.3 %collective-permute-start.47 = (bf16[200,384]{1,0:T(8,128)(2,1)S(1)}, bf16[200,384]{1,0:T(8,128)(2,1)S(1)}, u32[]{:S(2)}, u32[]{:S(2)}) collective-permute-start(bf16[200,384]{1,0:T(8,128)(2,1)S(1)} %get-tuple-element.280), channel_id=1, source_target_pairs={{0,3},{1,0},{2,1},{3,2},{4,7},{5,4},{6,5},{7,6},{8,11},{9,8},{10,9... | collective-permute-start | bytes 460808 | tf_op jit(solution)/shard_map/ppermute | solution.py:1280
  303.6 16.8 %collective-permute-start.52 = (bf16[4,128,768]{2,1,0:T(8,128)(2,1)S(1)}, bf16[4,128,768]{2,1,0:T(8,128)(2,1)S(1)}, u32[]{:S(2)}, u32[]{:S(2)}) collective-permute-start(bf16[4,128,768]{2,1,0:T(8,128)(2,1)S(1)} %pad_maximum_fusion.8), channel_id=1, source_target_pairs={{0,4},{4,0},{8,12},{12,8},{1,5},{5,1},{9,13},{13,9},{2,6},{6,2},{1... | collective-permute-start | bytes 2359304 | tf_op jit(solution)/shard_map/ppermute | solution.py:1221
  (86 other events, 675.8 us)

commit v4 on v3

--- a/solution.py
+++ b/solution.py
@@ -326,12 +326,12 @@
     return jnp.where(jnp.concatenate([same, same], axis=0), scores, jnp.float32(far_below))
 
 
-def attend_kernel(span, q_ref, k_ref, v_ref, kd_ref, qd_ref, *refs):
+def attend_kernel(span, short, q_ref, k_ref, v_ref, kd_ref, qd_ref, *refs):
     o_ref, l_ref = refs[-2:]
-    here = pl.ds(pl.multiple_of(pl.program_id(1) * QBLOCK, QBLOCK), span)
-    same = qd_ref[:, :1] == kd_ref[:, here]
-
-    def one_pair(cols):
+    step = pl.program_id(1)
+    pairs = q_ref.shape[1] // PAIR
+
+    def one_pair(here, same, cols):
         scores = masked_scores(stack_heads(q_ref[:, cols]), k_ref[here, cols], same)
         top = jnp.max(scores, axis=1, keepdims=True)
         expo = jnp.exp(scores - top)
@@ -341,18 +341,33 @@
         log = top + jnp.log(total)
         return log[:QBLOCK], log[QBLOCK:]
 
-    pairs = q_ref.shape[1] // PAIR
-    if len(refs) > 2:
-        logs = [log for p in range(pairs) for log in one_pair(slice(p * PAIR, (p + 1) * PAIR))]
-        l_ref[0] = jnp.concatenate(logs, axis=1)
-    else:
+    def looped():
+        here = pl.ds(pl.multiple_of(step * QBLOCK, QBLOCK), span)
+        same = qd_ref[:, :1] == kd_ref[:, here]
         lane = lax.broadcasted_iota(jnp.int32, l_ref.shape[1:], 1)
 
         @pl.loop(0, pairs)
         def _(pair):
-            first, second = one_pair(pl.ds(pl.multiple_of(pair * PAIR, PAIR), PAIR))
+            cols = pl.ds(pl.multiple_of(pair * PAIR, PAIR), PAIR)
+            first, second = one_pair(here, same, cols)
             logs = jnp.where(lane == 2 * pair, first, l_ref[0])
             l_ref[0] = jnp.where(lane == 2 * pair + 1, second, logs)
+
+    if len(refs) == 2:
+        looped()
+    else:
+        plan_ref = refs[0]
+        fits = plan_ref[1, step] == 1
+        pl.when(jnp.logical_not(fits))(looped)
+
+        @pl.when(fits)
+        def _():
+            here = pl.ds(pl.multiple_of(plan_ref[0, step], QBLOCK), short)
+            same = qd_ref[:, :1] == kd_ref[:, here]
+            logs = []
+            for pair in range(pairs):
+                logs += one_pair(here, same, slice(pair * PAIR, (pair + 1) * PAIR))
+            l_ref[0] = jnp.concatenate(logs, axis=1)
 
 
 def attend_back_kernel(
@@ -429,16 +444,17 @@
     span = QBLOCK + 2 * reach
     rows, key_spec, kd_spec, qd_spec, logs = attention_specs(window, cols, half)
     return pl.pallas_call(
-        partial(attend_kernel, span),
+        partial(attend_kernel, span, short_span(reach)),
         grid=(1, count // QBLOCK),
         in_specs=[rows, key_spec, key_spec, kd_spec, qd_spec]
-        + [pl.BlockSpec(memory_space=pl.ANY)] * len(prior),
+        + ([pl.BlockSpec(memory_space=pltpu.SMEM)] if prior else [])
+        + [pl.BlockSpec(memory_space=pl.ANY)] * (len(prior) - 1),
         out_specs=[rows, logs],
         out_shape=[
             jax.ShapeDtypeStruct((count, width), jnp.bfloat16),
             jax.ShapeDtypeStruct((2, count, cols // HEAD_DIM), jnp.float32),
         ],
-        input_output_aliases={5 + i: i for i in range(len(prior))},
+        input_output_aliases={6: 0, 7: 1} if prior else {},
         compiler_params=pltpu.CompilerParams(vmem_limit_bytes=16 << 20),
         cost_estimate=pl.CostEstimate(
             flops=16 * count * span * cols, bytes_accessed=4 << 20, transcendentals=0
@@ -1409,13 +1425,12 @@
         place, in_mine, in_other, pair, pair_other, in_biases, count, window
     )
     attention = queries, keys, values, key_docs, query_docs, reach
+    plan = key_plan(window_docs, reach, count)
     mixed, logs = attend(*attention, 0)
     mixed, far_one, far_three, some_two = tie(mixed, far_one, far_three, some_two)
     far_some_two = shard_swap(some_two)
-    mixed, logs = attend(*attention, 1, (mixed, logs))
-    mixed, far_some_two, up_two, plan = tie(
-        mixed, far_some_two, up_two, key_plan(window_docs, reach, count)
-    )
+    mixed, logs = attend(*attention, 1, (plan, mixed, logs))
+    mixed, far_some_two, up_two = tie(mixed, far_some_two, up_two)
     far_up_two = shard_swap(up_two)
     out_mine = jnp.stack(
         [

time: 333 us -> 332 us (level)
  transfers between devices with their start and end apart: 57 -> 57, of which waited for: 24 -> 24; matrix products, arithmetic and copies ran while one was open for 14% -> 14% of each run, Pallas kernels for 28% -> 27%
where the time goes in v4:
time: 332 us; the launch traced here: 326 us
  waiting for transfers between devices  93.6 us (28%)
  Pallas kernels  92.6 us (28%)
  starting transfers between devices  71.8 us (22%)
  other arithmetic  35.2 us (11%)
  local copies, waits for them, and re-layouts  30.9 us (9%)
    ppermute x13, waiting for transfers between devices, tp_shifts(): lax.ppermute(array[cut], 'tp', [(i, (i + shift) % 4) for i in range(4)])  42 us
    ppermute x6, waiting for transfers between devices, scatter_tp_start(): lax.ppermute(sent, 'tp', [(i, (i + shift) % 4) for i in range(4)])  22.5 us
    ppermute x23, starting transfers between devices, ctx_swap(): return lax.ppermute(array, 'ctx', [(i, i ^ bit) for i in range(4)])  22.3 us
    pallas_call x1, Pallas kernels, attend_back(): pl.pallas_call(partial(attend_back_kernel, span, short_span(reach)), grid...  18.3 us
    ppermute x13, starting transfers between devices, tp_shifts(): lax.ppermute(array[cut], 'tp', [(i, (i + shift) % 4) for i in range(4)])  16.6 us
    ppermute x23, waiting for transfers between devices, ctx_swap(): return lax.ppermute(array, 'ctx', [(i, i ^ bit) for i in range(4)])  15.6 us
    pallas_call x2, Pallas kernels, attend(): pl.pallas_call(partial(attend_kernel, span, short_span(reach)), grid=(1,...  13.6 us
    pallas_call x1, Pallas kernels, ffn_back(): pl.pallas_call(ffn_back_kernel, grid_spec=pltpu.PrefetchScalarGridSpec(nu...  13.2 us
  transfers between devices with their start and end apart: 57, of which 24 were waited for; matrix products, arithmetic and copies ran while one was open for 14% of the time, Pallas kernels for 27%

profile of v4, /device:TPU:1, one launch (start us, length us, event | category | flops | bytes accessed | tf_op | source)
XLA Modules:
  0.0 326.4 jit_solution(7611138741432162848)
XLA Ops:
  9.7 2.7 dynamic-slice_bitcast_fusion
  24.9 4.7 %collective-permute-done.4 = bf16[864,384]{1,0:T(8,128)(2,1)} collective-permute-done((bf16[864,384]{1,0:T(8,128)(2,1)}, bf16[864,384]{1,0:T(8,128)(2,1)}, u32[]{:S(2)}, u32[]{:S(2)}) %collective-permute-start.4) | collective-permute-done | bytes 663584 | tf_op jit(solution)/shard_map/ppermute | solution.py:1284
  35.1 2.9 collective-permute-start.9
  38.7 3.1 collective-permute-start.7
  46.9 3.8 %collective-permute-done.6 = bf16[864,384]{1,0:T(8,128)(2,1)} collective-permute-done((bf16[864,384]{1,0:T(8,128)(2,1)}, bf16[864,384]{1,0:T(8,128)(2,1)}, u32[]{:S(2)}, u32[]{:S(2)}) %collective-permute-start.6) | collective-permute-done | bytes 663584 | tf_op jit(solution)/shard_map/ppermute | solution.py:1271
  50.7 2.9 collective-permute-done.5
  55.1 3.7 %collective-permute-start.8 = (bf16[2,4,304,384]{3,2,1,0:T(8,128)(2,1)S(1)}, bf16[2,4,304,384]{3,2,1,0:T(8,128)(2,1)}, u32[]{:S(2)}, u32[]{:S(2)}) collective-permute-start(bf16[2,4,304,384]{3,2,1,0:T(8,128)(2,1)S(1)} %pad_maximum_fusion.1.w_mine), channel_id=1, source_target_pairs={{0,4},{4,0},{8,12},{12,8},{1,5},{5,1},{9,13},{13,9},{2,6},{6,2},{1... | collective-permute-start | bytes 5603336 | tf_op jit(solution)/shard_map/ppermute | solution.py:1237
  73.2 7.0 %project.1 = (bf16[384,768]{1,0:T(8,128)(2,1)S(1)}, bf16[1408,768]{1,0:T(8,128)(2,1)S(1)}, bf16[1408,768]{1,0:T(8,128)(2,1)S(1)}, bf16[1408,768]{1,0:T(8,128)(2,1)S(1)}, bf16[3,768,768]{2,1,0:T(8,128)(2,1)S(1)}) custom-call(s32[5]{0:T(128)S(1)} %stack.258.place_ref, bf16[2,4,304,384]{3,2,1,0:T(8,128)(2,1)S(1)} %pad_maximum_fusion.1.w_mine, ...), custom_call_target="tpu_custom_call" | custom-call | flops 3321888768 | bytes 16777216 | tf_op jit(solution)/shard_map/project/pallas_call | solution.py:770
  82.0 8.4 %attend.2 = (bf16[384,768]{1,0:T(8,128)(2,1)S(1)}, f32[2,384,6]{2,1,0:T(8,128)S(1)}) custom-call(bf16[384,768]{1,0:T(8,128)(2,1)S(1)} %get-tuple-element.153.q_ref, bf16[1408,768]{1,0:T(8,128)(2,1)S(1)} %get-tuple-element.154.k_ref, bf16[1408,768]{1,0:T(8,128)(2,1)S(1)} %get-tuple-element.155.v_ref, s32[1,1408]{1,0:T(1,128)S(1)} %broadcast_in_dim.34.kd_ref, ...), custom_call_target="tpu_custom_call" | custom-call | flops 2717908992 | bytes 4194304 | tf_op jit(solution)/shard_map/attend/pallas_call | solution.py:446
  90.4 5.7 %collective-permute-done.13 = bf16[480,384]{1,0:T(8,128)(2,1)S(1)} collective-permute-done((bf16[480,384]{1,0:T(8,128)(2,1)S(1)}, bf16[480,384]{1,0:T(8,128)(2,1)S(1)}, u32[]{:S(2)}, u32[]{:S(2)}) %collective-permute-start.13) | collective-permute-done | bytes 368672 | tf_op jit(solution)/shard_map/ppermute | solution.py:1271
  97.3 5.2 %attend.3 = (bf16[384,768]{1,0:T(8,128)(2,1)S(1)}, f32[2,384,6]{2,1,0:T(8,128)S(1)}) custom-call(bf16[384,768]{1,0:T(8,128)(2,1)S(1)} %get-tuple-element.153.q_ref, bf16[1408,768]{1,0:T(8,128)(2,1)S(1)} %get-tuple-element.154.k_ref, bf16[1408,768]{1,0:T(8,128)(2,1)S(1)} %get-tuple-element.155.v_ref, ...), custom_call_target="tpu_custom_call", output_to_operand_aliasing={{0}: (6, {}), {1}: (7, {})} | custom-call | flops 2717908992 | bytes 4194304 | tf_op jit(solution)/shard_map/attend/pallas_call | solution.py:446
  102.5 3.2 collective-permute-done.14
  114.6 7.0 %ffn.2 = (bf16[768,1536]{1,0:T(8,128)(2,1)S(1)}, bf16[768,1536]{1,0:T(8,128)(2,1)S(1)}, f32[768,768]{1,0:T(8,128)S(1)}) custom-call(s32[5]{0:T(128)S(1)} %stack.258.place_ref, bf16[384,768]{1,0:T(8,128)(2,1)S(1)} %get-tuple-element.169.h_ref, bf16[384,768]{1,0:T(8,128)(2,1)S(1)} %collective-permute-done.17.other_h_ref, ...), custom_call_target="tpu_custom_call" | custom-call | flops 8153726976 | bytes 9437184 | tf_op jit(solution)/shard_map/ffn/pallas_call | solution.py:666
  131.5 13.2 %ffn_back.1 = (bf16[384,768]{1,0:T(8,128)(2,1)S(1)}, bf16[384,768]{1,0:T(8,128)(2,1)S(1)}, bf16[2,4,192,384]{3,2,1,0:T(8,128)(2,1)S(1)}, bf16[2,4,192,384]{3,2,1...) custom-call(s32[5]{0:T(128)S(1)} %stack.258.place_ref, ...), custom_call_target="tpu_custom_call" | custom-call | flops 10871635968 | bytes 20971520 | tf_op jit(solution)/shard_map/ffn_back/pallas_call | solution.py:688
  151.5 18.3 %attend_back.1 = (bf16[384,768]{1,0:T(8,128)(2,1)S(1)}, bf16[1408,768]{1,0:T(8,128)(2,1)S(1)}, bf16[1408,768]{1,0:T(8,128)(2,1)S(1)}) custom-call(s32[2,3]{1,0:T(2,128)S(1)} %pad_add_fusion.refs_0_.plan_ref, bf16[384,768]{1,0:T(8,128)(2,1)S(1)} %get-tuple-element.153.q_ref, bf16[1408,768]{1,0:T(8,128)(2,1)S(1)} %get-tuple-element.154.k_ref, ...), custom_call_target="tpu_custom_call" | custom-call | flops 13589544960 | bytes 12582912 | tf_op jit(solution)/shard_map/attend_back/pallas_call | solution.py:471
  169.9 6.3 %span_grads.1 = (f32[384,768]{1,0:T(8,128)S(1)}, bf16[384,768]{1,0:T(8,128)(2,1)S(1)}, bf16[128,768]{1,0:T(8,128)(2,1)S(1)}, bf16[512,768]{1,0:T(8,128)(2,1)}) custom-call(s32[5]{0:T(128)S(1)} %stack.258.place_ref, bf16[384,768]{1,0:T(8,128)(2,1)S(1)} %get-tuple-element.194.dq_ref, bf16[1408,768]{1,0:T(8,128)(2,1)S(1)} %get-tuple-element.211.dk_ref, ...), custom_call_target="tpu_custom_call" | custom-call | flops 3321888768 | bytes 12582912 | tf_op jit(solution)/shard_map/span_grads/pallas_call | solution.py:1084
  181.6 3.6 %collective-permute-start.32 = (bf16[128,768]{1,0:T(8,128)(2,1)}, bf16[128,768]{1,0:T(8,128)(2,1)S(1)}, u32[]{:S(2)}, u32[]{:S(2)}) collective-permute-start(bf16[128,768]{1,0:T(8,128)(2,1)} %copy-done.17), channel_id=1, source_target_pairs={{4,5},{1,0},{5,13},{9,1},{13,12},{8,9},{6,7},{3,2},{7,15},{11,3},{... | collective-permute-start | bytes 589832 | tf_op jit(solution)/shard_map/ppermute | solution.py:1544
  187.5 3.4 %collective-permute-start.31 = (bf16[384,768]{1,0:T(8,128)(2,1)S(1)}, bf16[384,768]{1,0:T(8,128)(2,1)S(1)}, u32[]{:S(2)}, u32[]{:S(2)}) collective-permute-start(bf16[384,768]{1,0:T(8,128)(2,1)S(1)} %add_convert_fusion.7), channel_id=1, source_target_pairs={{4,1},{1,4},{5,9},{9,5},{13,8},{8,13},{6,3},{3,6},{7,11},{11,7},{1... | collective-permute-start | bytes 1769480 | tf_op jit(solution)/shard_map/ppermute | solution.py:1543
  190.8 2.8 collective-permute-done.30.four
  205.1 8.3 %attn_grads.1 = (bf16[2,2,4,200,384]{4,3,2,1,0:T(8,128)(2,1)S(1)}, bf16[2,2,4,200,384]{4,3,2,1,0:T(8,128)(2,1)}) custom-call(s32[5]{0:T(128)S(1)} %stack.258.place_ref, bf16[384,768]{1,0:T(8,128)(2,1)S(1)} %copy-done.25, bf16[1408,768]{1,0:T(8,128)(2,1)S(1)} %copy-done.21, bf16[1408,768]{1,0:T(8,128)(2,1)S(1)} %copy-done.23, ...), custom_call_target="tpu_custom_call" | custom-call | flops 4227858432 | bytes 16777216 | tf_op jit(solution)/shard_map/attn_grads/pallas_call | solution.py:1009
  221.6 3.1 collective-permute-start.36
  226.7 8.7 %collective-permute-done.39 = bf16[384,384]{1,0:T(8,128)(2,1)S(1)} collective-permute-done((bf16[384,384]{1,0:T(8,128)(2,1)S(1)}, bf16[384,384]{1,0:T(8,128)(2,1)S(1)}, u32[]{:S(2)}, u32[]{:S(2)}) %collective-permute-start.39) | collective-permute-done | bytes 294944 | tf_op jit(solution)/shard_map/ppermute | solution.py:1296
  239.8 3.3 collective-permute-start.42
  247.5 8.3 %collective-permute-done.41.two = bf16[384,768]{1,0:T(8,128)(2,1)S(1)} collective-permute-done((bf16[384,768]{1,0:T(8,128)(2,1)S(1)}, bf16[384,768]{1,0:T(8,128)(2,1)S(1)}, u32[]{:S(2)}, u32[]{:S(2)}) %collective-permute-start.41) | collective-permute-done | bytes 589856 | tf_op jit(solution)/shard_map/ppermute | solution.py:1271
  255.8 10.8 %collective-permute-done.42.four = bf16[384,768]{1,0:T(8,128)(2,1)S(1)} collective-permute-done((bf16[384,768]{1,0:T(8,128)(2,1)S(1)}, bf16[384,768]{1,0:T(8,128)(2,1)S(1)}, u32[]{:S(2)}, u32[]{:S(2)}) %collective-permute-start.42) | collective-permute-done | bytes 589856 | tf_op jit(solution)/shard_map/ppermute | solution.py:1271
  273.8 9.0 %collective-permute-done.43 = bf16[4,200,384]{2,1,0:T(8,128)(2,1)} collective-permute-done((bf16[4,200,384]{2,1,0:T(8,128)(2,1)}, bf16[4,200,384]{2,1,0:T(8,128)(2,1)}, u32[]{:S(2)}, u32[]{:S(2)}) %collective-permute-start.43) | collective-permute-done | bytes 614432 | tf_op jit(solution)/shard_map/ppermute | solution.py:1237
  286.8 3.1 assemble.2
  289.9 8.6 %collective-permute-done.46.three = bf16[384,768]{1,0:T(8,128)(2,1)S(1)} collective-permute-done((bf16[384,768]{1,0:T(8,128)(2,1)S(1)}, bf16[384,768]{1,0:T(8,128)(2,1)S(1)}, u32[]{:S(2)}, u32[]{:S(2)}) %collective-permute-start.46) | collective-permute-done | bytes 589856 | tf_op jit(solution)/shard_map/ppermute | solution.py:1271
  298.5 3.2 collective-permute-done.47
  305.1 4.7 %collective-permute-done.49 = bf16[200,384]{1,0:T(8,128)(2,1)S(1)} collective-permute-done((bf16[200,384]{1,0:T(8,128)(2,1)S(1)}, bf16[200,384]{1,0:T(8,128)(2,1)S(1)}, u32[]{:S(2)}, u32[]{:S(2)}) %collective-permute-start.49) | collective-permute-done | bytes 153632 | tf_op jit(solution)/shard_map/ppermute | solution.py:1296
  309.8 5.8 %collective-permute-done.50 = bf16[200,384]{1,0:T(8,128)(2,1)S(1)} collective-permute-done((bf16[200,384]{1,0:T(8,128)(2,1)S(1)}, bf16[200,384]{1,0:T(8,128)(2,1)S(1)}, u32[]{:S(2)}, u32[]{:S(2)}) %collective-permute-start.50) | collective-permute-done | bytes 153632 | tf_op jit(solution)/shard_map/ppermute | solution.py:1296
  317.8 3.1 assemble.3
  (334 shorter events, 136.1 us)
Async XLA Ops:
  4.2 20.0 %collective-permute-start = (bf16[304,384]{1,0:T(8,128)(2,1)}, bf16[304,384]{1,0:T(8,128)(2,1)}, u32[]{:S(2)}, u32[]{:S(2)}) collective-permute-start(bf16[304,384]{1,0:T(8,128)(2,1)} %maximum_maximum_fusion), channel_id=1, source_target_pairs={{0,1},{1,2},{2,3},{3,0},{4,5},{5,6},{6,7},{7,4},{8,9},{9,10},{10,1... | collective-permute-start | bytes 700424 | tf_op jit(solution)/shard_map/ppermute | solution.py:1271
  6.3 18.5 %collective-permute-start.1 = (bf16[304,384]{1,0:T(8,128)(2,1)}, bf16[304,384]{1,0:T(8,128)(2,1)}, u32[]{:S(2)}, u32[]{:S(2)}) collective-permute-start(bf16[304,384]{1,0:T(8,128)(2,1)} %maximum_maximum_fusion), channel_id=1, source_target_pairs={{0,2},{1,3},{2,0},{3,1},{4,6},{5,7},{6,4},{7,5},{8,10},{9,11},{10,... | collective-permute-start | bytes 700424 | tf_op jit(solution)/shard_map/ppermute | solution.py:1271
  8.7 16.2 %collective-permute-start.2 = (bf16[304,384]{1,0:T(8,128)(2,1)}, bf16[304,384]{1,0:T(8,128)(2,1)}, u32[]{:S(2)}, u32[]{:S(2)}) collective-permute-start(bf16[304,384]{1,0:T(8,128)(2,1)} %maximum_maximum_fusion), channel_id=1, source_target_pairs={{0,3},{1,0},{2,1},{3,2},{4,7},{5,4},{6,5},{7,6},{8,11},{9,8},{10,9... | collective-permute-start | bytes 700424 | tf_op jit(solution)/shard_map/ppermute | solution.py:1271
  12.4 17.8 %collective-permute-start.3 = (bf16[2,256,768]{2,1,0:T(8,128)(2,1)}, bf16[2,256,768]{2,1,0:T(8,128)(2,1)S(1)}, u32[]{:S(2)}, u32[]{:S(2)}) collective-permute-start(bf16[2,256,768]{2,1,0:T(8,128)(2,1)} %get-tuple-element.266), channel_id=1, source_target_pairs={{0,8},{4,12},{8,0},{12,4},{1,9},{5,13},{9,1},{13,5},{2,10},{6,14},... | collective-permute-start | bytes 2359304 | tf_op jit(solution)/shard_map/ppermute | solution.py:1237
  33.4 20.2 %collective-permute-start.5 = (bf16[4,304,384]{2,1,0:T(8,128)(2,1)}, bf16[4,304,384]{2,1,0:T(8,128)(2,1)}, u32[]{:S(2)}, u32[]{:S(2)}) collective-permute-start(bf16[4,304,384]{2,1,0:T(8,128)(2,1)} %get-tuple-element.275), channel_id=1, source_target_pairs={{0,16},{16,0},{1,17},{17,1},{2,18},{18,2},{3,19},{19,3},{4,20},{20... | collective-permute-start | bytes 2801672 | tf_op jit(solution)/shard_map/ppermute | solution.py:1284
  34.7 16.0 %collective-permute-start.6 = (bf16[864,384]{1,0:T(8,128)(2,1)}, bf16[864,384]{1,0:T(8,128)(2,1)}, u32[]{:S(2)}, u32[]{:S(2)}) collective-permute-start(bf16[864,384]{1,0:T(8,128)(2,1)} %pad_maximum_fusion.9), channel_id=1, source_target_pairs={{0,1},{1,2},{2,3},{3,0},{4,5},{5,6},{6,7},{7,4},{8,9},{9,10},{10,1... | collective-permute-start | bytes 1990664 | tf_op jit(solution)/shard_map/ppermute | solution.py:1271
  35.1 30.9 %collective-permute-start.9 = (bf16[864,384]{1,0:T(8,128)(2,1)}, bf16[864,384]{1,0:T(8,128)(2,1)}, u32[]{:S(2)}, u32[]{:S(2)}) collective-permute-start(bf16[864,384]{1,0:T(8,128)(2,1)} %pad_maximum_fusion.9), channel_id=1, source_target_pairs={{0,3},{1,0},{2,1},{3,2},{4,7},{5,4},{6,5},{7,6},{8,11},{9,8},{10,9... | collective-permute-start | bytes 1990664 | tf_op jit(solution)/shard_map/ppermute | solution.py:1271
  61.8 28.6 %collective-permute-start.11 = (bf16[864,384]{1,0:T(8,128)(2,1)}, bf16[864,384]{1,0:T(8,128)(2,1)S(1)}, u32[]{:S(2)}, u32[]{:S(2)}) collective-permute-start(bf16[864,384]{1,0:T(8,128)(2,1)} %collective-permute-done.6), channel_id=1, source_target_pairs={{0,16},{16,0},{1,17},{17,1},{2,18},{18,2},{3,19},{19,3},{4,20},{20... | collective-permute-start | bytes 1990664 | tf_op jit(solution)/shard_map/ppermute | solution.py:1284
  66.0 30.2 %collective-permute-start.12 = (bf16[864,384]{1,0:T(8,128)(2,1)}, bf16[864,384]{1,0:T(8,128)(2,1)S(1)}, u32[]{:S(2)}, u32[]{:S(2)}) collective-permute-start(bf16[864,384]{1,0:T(8,128)(2,1)} %collective-permute-done.9), channel_id=1, source_target_pairs={{0,16},{16,0},{1,17},{17,1},{2,18},{18,2},{3,19},{19,3},{4,20},{20... | collective-permute-start | bytes 1990664 | tf_op jit(solution)/shard_map/ppermute | solution.py:1284
  70.8 25.4 %collective-permute-start.13 = (bf16[480,384]{1,0:T(8,128)(2,1)S(1)}, bf16[480,384]{1,0:T(8,128)(2,1)S(1)}, u32[]{:S(2)}, u32[]{:S(2)}) collective-permute-start(bf16[480,384]{1,0:T(8,128)(2,1)S(1)} %slice.297), channel_id=1, source_target_pairs={{0,2},{1,3},{2,0},{3,1},{4,6},{5,7},{6,4},{7,5},{8,10},{9,11},{10,... | collective-permute-start | bytes 1105928 | tf_op jit(solution)/shard_map/ppermute | solution.py:1271
  70.8 31.7 %collective-permute-start.15 = (bf16[384,384]{1,0:T(8,128)(2,1)S(1)}, bf16[384,384]{1,0:T(8,128)(2,1)S(1)}, u32[]{:S(2)}, u32[]{:S(2)}) collective-permute-start(bf16[384,384]{1,0:T(8,128)(2,1)S(1)} %slice.298), channel_id=1, source_target_pairs={{0,2},{1,3},{2,0},{3,1},{4,6},{5,7},{6,4},{7,5},{8,10},{9,11},{10,... | collective-permute-start | bytes 884744 | tf_op jit(solution)/shard_map/ppermute | solution.py:1271
  80.2 45.7 %collective-permute-start.20 = (bf16[2,256,768]{2,1,0:T(8,128)(2,1)S(1)}, bf16[2,256,768]{2,1,0:T(8,128)(2,1)S(1)}, u32[]{:S(2)}, u32[]{:S(2)}) collective-permute-start(bf16[2,256,768]{2,1,0:T(8,128)(2,1)S(1)} %pad_maximum_fusion.5.g_ref), channel_id=1, source_target_pairs={{0,4},{4,0},{8,12},{12,8},{1,5},{5,1},{9,13},{13,9},{2,6},{6,2},{1... | collective-permute-start | bytes 2359304 | tf_op jit(solution)/shard_map/ppermute | solution.py:1237
  129.9 16.6 %collective-permute-start.22 = (bf16[384,768]{1,0:T(8,128)(2,1)S(1)}, bf16[384,768]{1,0:T(8,128)(2,1)S(1)}, u32[]{:S(2)}, u32[]{:S(2)}) collective-permute-start(bf16[384,768]{1,0:T(8,128)(2,1)S(1)} %get-tuple-element.181.one), channel_id=1, source_target_pairs={{0,1},{1,2},{2,3},{3,0},{4,5},{5,6},{6,7},{7,4},{8,9},{9,10},{10,1... | collective-permute-start | bytes 1769480 | tf_op jit(solution)/shard_map/ppermute | solution.py:1271
  145.2 33.4 %collective-permute-start.26 = (bf16[384,768]{1,0:T(8,128)(2,1)S(1)}, bf16[384,768]{1,0:T(8,128)(2,1)S(1)}, u32[]{:S(2)}, u32[]{:S(2)}) collective-permute-start(bf16[384,768]{1,0:T(8,128)(2,1)S(1)} %get-tuple-element.181.one), channel_id=1, source_target_pairs={{0,2},{1,3},{2,0},{3,1},{4,6},{5,7},{6,4},{7,5},{8,10},{9,11},{10,... | collective-permute-start | bytes 1769480 | tf_op jit(solution)/shard_map/ppermute | solution.py:1271
  146.5 32.1 %collective-permute-start.24 = (bf16[2,4,192,384]{3,2,1,0:T(8,128)(2,1)S(1)}, bf16[2,4,192,384]{3,2,1,0:T(8,128)(2,1)S(1)}, u32[]{:S(2)}, u32[]{:S(2)}) collective-permute-start(bf16[2,4,192,384]{3,2,1,0:T(8,128)(2,1)S(1)} %get-tuple-element.200), channel_id=1, source_target_pairs={{0,8},{4,12},{8,0},{12,4},{1,9},{5,13},{9,1},{13,5},{2,10},{6,14},... | collective-permute-start | bytes 3538952 | tf_op jit(solution)/shard_map/ppermute | solution.py:1237
  147.7 30.9 %collective-permute-start.25 = (bf16[2,4,192,384]{3,2,1,0:T(8,128)(2,1)S(1)}, bf16[2,4,192,384]{3,2,1,0:T(8,128)(2,1)S(1)}, u32[]{:S(2)}, u32[]{:S(2)}) collective-permute-start(bf16[2,4,192,384]{3,2,1,0:T(8,128)(2,1)S(1)} %get-tuple-element.201), channel_id=1, source_target_pairs={{0,16},{16,0},{1,17},{17,1},{2,18},{18,2},{3,19},{19,3},{4,20},{20... | collective-permute-start | bytes 3538952 | tf_op jit(solution)/shard_map/ppermute | solution.py:1284
  179.7 15.3 %collective-permute-start.29 = (bf16[4,192,384]{2,1,0:T(8,128)(2,1)}, bf16[4,192,384]{2,1,0:T(8,128)(2,1)}, u32[]{:S(2)}, u32[]{:S(2)}) collective-permute-start(bf16[4,192,384]{2,1,0:T(8,128)(2,1)} %fusion.10), channel_id=1, source_target_pairs={{0,8},{4,12},{8,0},{12,4},{1,9},{5,13},{9,1},{13,5},{2,10},{6,14},... | collective-permute-start | bytes 1769480 | tf_op jit(solution)/shard_map/ppermute | solution.py:1237
  181.6 33.3 %collective-permute-start.32 = (bf16[128,768]{1,0:T(8,128)(2,1)}, bf16[128,768]{1,0:T(8,128)(2,1)S(1)}, u32[]{:S(2)}, u32[]{:S(2)}) collective-permute-start(bf16[128,768]{1,0:T(8,128)(2,1)} %copy-done.17), channel_id=1, source_target_pairs={{4,5},{1,0},{5,13},{9,1},{13,12},{8,9},{6,7},{3,2},{7,15},{11,3},{... | collective-permute-start | bytes 589832 | tf_op jit(solution)/shard_map/ppermute | solution.py:1544
  187.5 27.5 %collective-permute-start.31 = (bf16[384,768]{1,0:T(8,128)(2,1)S(1)}, bf16[384,768]{1,0:T(8,128)(2,1)S(1)}, u32[]{:S(2)}, u32[]{:S(2)}) collective-permute-start(bf16[384,768]{1,0:T(8,128)(2,1)S(1)} %add_convert_fusion.7), channel_id=1, source_target_pairs={{4,1},{1,4},{5,9},{9,5},{13,8},{8,13},{6,3},{3,6},{7,11},{11,7},{1... | collective-permute-start | bytes 1769480 | tf_op jit(solution)/shard_map/ppermute | solution.py:1543
  200.2 15.6 %collective-permute-start.33 = (bf16[384,384]{1,0:T(8,128)(2,1)S(1)}, bf16[384,384]{1,0:T(8,128)(2,1)S(1)}, u32[]{:S(2)}, u32[]{:S(2)}) collective-permute-start(bf16[384,384]{1,0:T(8,128)(2,1)S(1)} %get-tuple-element.268), channel_id=1, source_target_pairs={{0,1},{1,2},{2,3},{3,0},{4,5},{5,6},{6,7},{7,4},{8,9},{9,10},{10,1... | collective-permute-start | bytes 884744 | tf_op jit(solution)/shard_map/ppermute | solution.py:1296
  201.4 15.1 %collective-permute-start.34 = (bf16[384,384]{1,0:T(8,128)(2,1)S(1)}, bf16[384,384]{1,0:T(8,128)(2,1)S(1)}, u32[]{:S(2)}, u32[]{:S(2)}) collective-permute-start(bf16[384,384]{1,0:T(8,128)(2,1)S(1)} %get-tuple-element.269), channel_id=1, source_target_pairs={{0,3},{1,0},{2,1},{3,2},{4,7},{5,4},{6,5},{7,6},{8,11},{9,8},{10,9... | collective-permute-start | bytes 884744 | tf_op jit(solution)/shard_map/ppermute | solution.py:1296
  217.2 19.0 %collective-permute-start.38 = (bf16[2,2,4,200,384]{4,3,2,1,0:T(8,128)(2,1)}, bf16[2,2,4,200,384]{4,3,2,1,0:T(8,128)(2,1)}, u32[]{:S(2)}, u32[]{:S(2)}) collective-permute-start(bf16[2,2,4,200,384]{4,3,2,1,0:T(8,128)(2,1)} %get-tuple-element.224), channel_id=1, source_target_pairs={{0,4},{4,0},{8,12},{12,8},{1,5},{5,1},{9,13},{13,9},{2,6},{6,2},{1... | collective-permute-start | bytes 7372808 | tf_op jit(solution)/shard_map/ppermute | solution.py:1237
  219.9 15.6 %collective-permute-start.39 = (bf16[384,384]{1,0:T(8,128)(2,1)S(1)}, bf16[384,384]{1,0:T(8,128)(2,1)S(1)}, u32[]{:S(2)}, u32[]{:S(2)}) collective-permute-start(bf16[384,384]{1,0:T(8,128)(2,1)S(1)} %copy-done.49), channel_id=1, source_target_pairs={{0,2},{1,3},{2,0},{3,1},{4,6},{5,7},{6,4},{7,5},{8,10},{9,11},{10,... | collective-permute-start | bytes 884744 | tf_op jit(solution)/shard_map/ppermute | solution.py:1296
  238.4 29.0 %collective-permute-start.40 = (bf16[2,4,200,384]{3,2,1,0:T(8,128)(2,1)S(1)}, bf16[2,4,200,384]{3,2,1,0:T(8,128)(2,1)S(1)}, u32[]{:S(2)}, u32[]{:S(2)}) collective-permute-start(bf16[2,4,200,384]{3,2,1,0:T(8,128)(2,1)S(1)} %get-tuple-element.263), channel_id=1, source_target_pairs={{0,16},{16,0},{1,17},{17,1},{2,18},{18,2},{3,19},{19,3},{4,20},{20... | collective-permute-start | bytes 3686408 | tf_op jit(solution)/shard_map/ppermute | solution.py:1284
  239.8 16.1 %collective-permute-start.41 = (bf16[384,768]{1,0:T(8,128)(2,1)S(1)}, bf16[384,768]{1,0:T(8,128)(2,1)S(1)}, u32[]{:S(2)}, u32[]{:S(2)}) collective-permute-start(bf16[384,768]{1,0:T(8,128)(2,1)S(1)} %pad_maximum_fusion.11.one), channel_id=1, source_target_pairs={{0,1},{1,2},{2,3},{3,0},{4,5},{5,6},{6,7},{7,4},{8,9},{9,10},{10,1... | collective-permute-start | bytes 1769480 | tf_op jit(solution)/shard_map/ppermute | solution.py:1271
  239.8 26.8 %collective-permute-start.42 = (bf16[384,768]{1,0:T(8,128)(2,1)S(1)}, bf16[384,768]{1,0:T(8,128)(2,1)S(1)}, u32[]{:S(2)}, u32[]{:S(2)}) collective-permute-start(bf16[384,768]{1,0:T(8,128)(2,1)S(1)} %pad_maximum_fusion.11.one), channel_id=1, source_target_pairs={{0,3},{1,0},{2,1},{3,2},{4,7},{5,4},{6,5},{7,6},{8,11},{9,8},{10,9... | collective-permute-start | bytes 1769480 | tf_op jit(solution)/shard_map/ppermute | solution.py:1271
  244.1 29.7 %collective-permute-start.45 = (bf16[4,128,768]{2,1,0:T(8,128)(2,1)}, bf16[4,128,768]{2,1,0:T(8,128)(2,1)}, u32[]{:S(2)}, u32[]{:S(2)}) collective-permute-start(bf16[4,128,768]{2,1,0:T(8,128)(2,1)} %pad_maximum_fusion.7), channel_id=1, source_target_pairs={{0,4},{4,0},{8,12},{12,8},{1,5},{5,1},{9,13},{13,9},{2,6},{6,2},{1... | collective-permute-start | bytes 2359304 | tf_op jit(solution)/shard_map/ppermute | solution.py:1237
  246.4 27.4 %collective-permute-start.44 = (bf16[2,256,768]{2,1,0:T(8,128)(2,1)}, bf16[2,256,768]{2,1,0:T(8,128)(2,1)}, u32[]{:S(2)}, u32[]{:S(2)}) collective-permute-start(bf16[2,256,768]{2,1,0:T(8,128)(2,1)} %pad_maximum_fusion.6), channel_id=1, source_target_pairs={{0,12},{4,8},{8,4},{12,0},{1,13},{5,9},{9,5},{13,1},{2,14},{6,10},... | collective-permute-start | bytes 2359304 | tf_op jit(solution)/shard_map/ppermute | solution.py:1584
  270.0 28.5 %collective-permute-start.46 = (bf16[384,768]{1,0:T(8,128)(2,1)S(1)}, bf16[384,768]{1,0:T(8,128)(2,1)S(1)}, u32[]{:S(2)}, u32[]{:S(2)}) collective-permute-start(bf16[384,768]{1,0:T(8,128)(2,1)S(1)} %pad_maximum_fusion.11.one), channel_id=1, source_target_pairs={{0,2},{1,3},{2,0},{3,1},{4,6},{5,7},{6,4},{7,5},{8,10},{9,11},{10,... | collective-permute-start | bytes 1769480 | tf_op jit(solution)/shard_map/ppermute | solution.py:1271
  273.4 16.5 %collective-permute-start.48 = (bf16[384,384]{1,0:T(8,128)(2,1)S(1)}, bf16[384,384]{1,0:T(8,128)(2,1)S(1)}, u32[]{:S(2)}, u32[]{:S(2)}) collective-permute-start(bf16[384,384]{1,0:T(8,128)(2,1)S(1)} %fusion.15.mine), channel_id=1, source_target_pairs={{0,8},{4,12},{8,0},{12,4},{1,9},{5,13},{9,1},{13,5},{2,10},{6,14},... | collective-permute-start | bytes 884744 | tf_op jit(solution)/shard_map/ppermute | solution.py:1237
  284.3 17.4 %collective-permute-start.47 = (bf16[200,384]{1,0:T(8,128)(2,1)S(1)}, bf16[200,384]{1,0:T(8,128)(2,1)S(1)}, u32[]{:S(2)}, u32[]{:S(2)}) collective-permute-start(bf16[200,384]{1,0:T(8,128)(2,1)S(1)} %get-tuple-element.278), channel_id=1, source_target_pairs={{0,3},{1,0},{2,1},{3,2},{4,7},{5,4},{6,5},{7,6},{8,11},{9,8},{10,9... | collective-permute-start | bytes 460808 | tf_op jit(solution)/shard_map/ppermute | solution.py:1296
  301.9 15.9 %collective-permute-start.52 = (bf16[4,128,768]{2,1,0:T(8,128)(2,1)S(1)}, bf16[4,128,768]{2,1,0:T(8,128)(2,1)S(1)}, u32[]{:S(2)}, u32[]{:S(2)}) collective-permute-start(bf16[4,128,768]{2,1,0:T(8,128)(2,1)S(1)} %pad_maximum_fusion.8), channel_id=1, source_target_pairs={{0,4},{4,0},{8,12},{12,8},{1,5},{5,1},{9,13},{13,9},{2,6},{6,2},{1... | collective-permute-start | bytes 2359304 | tf_op jit(solution)/shard_map/ppermute | solution.py:1237
  (86 other events, 662.5 us)
